TPU v7x, 128 devices: a whole 4x4x4 slice. The times are simulated.
128 devices in a mesh: ctx: 32 (over x, z, y_lo), tp: 4 (over y_hi, core).
Axes of the slice: x: 4, y: 4 (y_hi: 2, y_lo: 2; y = y_hi * 2 + y_lo), z: 4, core: 2. Of those that a mesh axis runs over, the one named last changes fastest.
Arguments:
- queries: bfloat16 [1024, 8192], P('ctx', 'tp'), may hold values from -15 to 15
- new_keys: bfloat16 [1024, 1024], P('ctx', 'tp'), may hold values from -6 to 6
- new_values: bfloat16 [1024, 1024], P('ctx', 'tp'), may hold values from -6 to 6
- cache_keys: bfloat16 [131072, 1024], P('ctx', 'tp'), may hold values from -6 to 6
- cache_values: bfloat16 [131072, 1024], P('ctx', 'tp'), may hold values from -6 to 6
- keep_tiles: int32 [32, 8, 24], P('ctx', 'tp'), may hold values from 0 to 31, as said below
- tile_count: int32 [32, 8], P('ctx', 'tp'), may hold values from 1 to 24
- owner_slot: int32 [32], replicated, may hold values from 0 to 31, each once
- out_weight: bfloat16 [8192, 8192], P('tp', 'ctx'), may hold values from -0.0625 to 0.0625
Outputs:
- projected_out: float32 [1024, 8192], P('tp', 'ctx')
Inputs may be any that keep to these rules, and one draw needn't show every extreme that they name: `keep_tiles`: the 24 entries of each keep list are distinct tile numbers; entries at or past tile_count are ignored.
All inputs are finite; a program needn't handle non-finite values.
Results may differ from a plain program's by a relative error of at most 0.0055.
Values may be sent and summed in bfloat16 or wider, within the bound.
A program may use at most 128 MiB of HBM per device.

v0:
```python
import jax
import jax.numpy as jnp
from jax import lax
from jax.sharding import PartitionSpec as P

DH = 128
TILE = 128
TB = 4


NEG_INF = -jnp.inf


def fold_scores(state_now, scores, value_rows):
    run_max, run_total, run_sum = state_now
    new_max = jnp.maximum(run_max, jnp.max(scores, axis=-1))
    shrink = jnp.exp(run_max - new_max)
    weights = jnp.exp(scores - new_max[..., None])
    run_total = run_total * shrink + jnp.sum(weights, axis=-1)
    mixture = jnp.einsum(
        "rhk,kd->rhd", weights.astype(jnp.bfloat16), value_rows, preferred_element_type=jnp.float32
    )
    run_sum = run_sum * shrink[..., None] + mixture
    return (new_max, run_total, run_sum)


def body(
    queries,
    new_keys,
    new_values,
    cache_keys,
    cache_values,
    keep_tiles,
    tile_count,
    owner_slot,
    out_weight,
):
    q_dev = queries.shape[0]
    kv_local = new_keys.shape[1] // DH
    q_local = queries.shape[1] // DH
    group_size = q_local // kv_local
    ctx_count = lax.axis_size("ctx")
    total_rows = q_dev * ctx_count
    my_index = lax.axis_index("ctx")
    score_scale = DH ** (-0.5)
    slot_count = keep_tiles.shape[2]
    key_place = owner_slot[my_index] * q_dev + jnp.arange(q_dev, dtype=jnp.int32)
    tiled_keys = cache_keys.reshape(-1, TILE, kv_local, DH)
    tiled_values = cache_values.reshape(-1, TILE, kv_local, DH)
    kept_keys = [
        jnp.take(tiled_keys[:, :, kv_head, :], keep_tiles[0, kv_head], axis=0)
        for kv_head in range(kv_local)
    ]
    kept_values = [
        jnp.take(tiled_values[:, :, kv_head, :], keep_tiles[0, kv_head], axis=0)
        for kv_head in range(kv_local)
    ]
    query_rows = lax.all_gather(queries, "ctx", axis=0, tiled=True)
    row_count = query_rows.shape[0]
    row_ids = jnp.arange(row_count, dtype=jnp.int32)
    query_place = owner_slot[row_ids // q_dev] * q_dev + row_ids % q_dev
    causal = query_place[:, None] >= key_place[None, :]
    pieces_max = []
    pieces_total = []
    pieces_sum = []
    for kv_head in range(kv_local):
        query_head = query_rows[
            :, kv_head * group_size * DH : (kv_head + 1) * group_size * DH
        ].reshape(row_count, group_size, DH)
        start_state = (
            jnp.full((row_count, group_size), NEG_INF, jnp.float32),
            jnp.zeros((row_count, group_size), jnp.float32),
            jnp.zeros((row_count, group_size, DH), jnp.float32),
        )
        live_count = tile_count[0, kv_head]

        def tile_block(
            block_id, state_inner, kv_head=kv_head, query_head=query_head, live_count=live_count
        ):
            key_block = lax.dynamic_slice_in_dim(kept_keys[kv_head], block_id * TB, TB, 0).reshape(
                TB * TILE, DH
            )
            value_block = lax.dynamic_slice_in_dim(
                kept_values[kv_head], block_id * TB, TB, 0
            ).reshape(TB * TILE, DH)
            tile_ids = block_id * TB + jnp.arange(TB, dtype=jnp.int32)
            live_keys = jnp.repeat(tile_ids < live_count, TILE)
            scores = (
                jnp.einsum("rhd,kd->rhk", query_head, key_block, preferred_element_type=jnp.float32)
                * score_scale
            )
            scores = jnp.where(live_keys[None, None, :], scores, NEG_INF)
            return fold_scores(state_inner, scores, value_block)

        block_limit = slot_count // TB
        state_head = lax.fori_loop(0, block_limit, tile_block, start_state)
        fresh_keys = new_keys[:, kv_head * DH : (kv_head + 1) * DH]
        fresh_values = new_values[:, kv_head * DH : (kv_head + 1) * DH]
        scores = (
            jnp.einsum("rhd,kd->rhk", query_head, fresh_keys, preferred_element_type=jnp.float32)
            * score_scale
        )
        scores = jnp.where(causal[:, None, :], scores, NEG_INF)
        head_max, head_total, head_sum = fold_scores(state_head, scores, fresh_values)
        pieces_max.append(head_max)
        pieces_total.append(head_total)
        pieces_sum.append(head_sum.reshape(row_count, group_size * DH))
    maxima_all = jnp.concatenate(pieces_max, axis=1)
    totals_all = jnp.concatenate(pieces_total, axis=1)
    sums_all = jnp.concatenate(pieces_sum, axis=1)
    top_max = lax.pmax(maxima_all, "ctx")
    factor = jnp.exp(maxima_all - top_max)
    scaled = (sums_all.reshape(total_rows, q_local, DH) * factor[..., None]).reshape(
        total_rows, q_local * DH
    )
    numerator, denominator = (
        lax.psum_scatter(scaled, "ctx", scatter_dimension=0, tiled=True),
        lax.psum_scatter(totals_all * factor, "ctx", scatter_dimension=0, tiled=True),
    )
    attn_rows = (
        (numerator.reshape(q_dev, q_local, DH) / denominator[..., None])
        .reshape(q_dev, q_local * DH)
        .astype(jnp.bfloat16)
    )
    projected = jnp.dot(
        lax.all_gather(attn_rows, "ctx", axis=0, tiled=True),
        out_weight,
        preferred_element_type=jnp.float32,
    )
    return lax.psum_scatter(projected, "tp", scatter_dimension=0, tiled=True)


def solution(mesh):
    return jax.shard_map(
        body,
        mesh=mesh,
        in_specs=(
            P("ctx", "tp"),
            P("ctx", "tp"),
            P("ctx", "tp"),
            P("ctx", "tp"),
            P("ctx", "tp"),
            P("ctx", "tp", None),
            P("ctx", "tp"),
            P(),
            P("tp", "ctx"),
        ),
        out_specs=P("tp", "ctx"),
        check_vma=False,
    )
```

profile of v0, /device:TPU:125, one launch (start us, length us, event | category | flops | bytes accessed | tf_op | source)
XLA Modules:
  0.0 1220.4 jit_solution(18363022142407999071)
XLA Ops:
  7.4 2.6 reshape.338
  9.9 4.0 reshape.339
  14.0 6.1 fusion.48
  21.9 2.8 gather_fusion.3
  24.7 3.8 fusion.49
  29.9 2.8 gather_fusion.2
  38.8 4.2 compare_select_fusion.1
  43.7 15.2 %fusion.43 = s32[1024]{0:T(1024)S(1)} fusion(pred[1024]{0:T(1024)(128)(4,1)S(1)} %compare_reduce_fusion, pred[1024]{0:T(1024)(128)(4,1)S(1)} %compare_reduce_fusion.1, pred[1024]{0:T(1024)(128)(4,1)S(1)} %compare_reduce_fusion.2, pred[1024]{0:T(1024)(128)(4,1)S(1)} %compare_reduce_fusion.3, pred[1024]{0:T(1024)(128)(4,1)S(1)} %compare_reduce_fusion.4, ...), kind=kLoop, calls=%fused_computation.122 | loop fusion | flops 33792 | bytes 33892 | tf_op jit(solution)/shard_map/add | solution.py:61
  59.0 2.8 broadcast_select_fusion
  61.7 2.5 broadcast_select_fusion.2
  64.2 72.7 %all-gather.3.cloned.1.call-done = bf16[1024,2048]{1,0:T(8,128)(2,1)} async-done(((bf16[32,2048]{1,0:T(8,128)(2,1)}), bf16[1024,2048]{1,0:T(8,128)(2,1)}) %all-gather.3.cloned.1.call-update) | async-done | bytes 4194320 | tf_op jit(solution)/shard_map/all_gather | solution.py:58
  136.9 4.0 fusion.47
  140.9 2.6 copy.66
  143.5 3.0 copy.45
  146.6 4.0 copy.69
  150.5 3.8 fusion.54
  156.4 3.9 copy.51
  160.3 103.2 %while.37 = (s32[]{:T(128)}, f32[1024,8]{0,1:T(8,128)S(1)}, f32[1024,8]{0,1:T(8,128)S(1)}, f32[1024,8,128]{2,0,1:T(8,128)}, s32[]{:T(128)}, /*index=5*/bf16[24,1...) while((s32[]{:T(128)}, f32[1024,8]{0,1:T(8,128)S(1)}, ...), condition=%wide.region_8.10_spmd.clone, body=%wide.region_5.9_spmd.clone.sunk | while | flops 2196807680 | bytes 62130376 | solution.py:96
  162.1 4.0 bitcast_reduce_fusion.5
  166.1 3.8 fusion.91
  169.9 6.3 fusion.93
  178.0 4.0 bitcast_reduce_fusion.5
  182.0 3.8 fusion.91
  185.8 7.9 fusion.93
  195.5 4.0 bitcast_reduce_fusion.5
  199.5 3.8 fusion.91
  203.3 7.9 fusion.93
  212.9 4.0 bitcast_reduce_fusion.5
  216.9 3.8 fusion.91
  220.8 7.9 fusion.93
  230.4 4.0 bitcast_reduce_fusion.5
  234.4 3.8 fusion.91
  238.2 7.9 fusion.93
  247.9 4.0 bitcast_reduce_fusion.5
  251.9 3.8 fusion.91
  255.7 7.9 fusion.93
  263.6 5.4 copy.53
  268.9 93.2 %while.36 = (s32[]{:T(128)}, f32[1024,8]{0,1:T(8,128)S(1)}, f32[1024,8]{0,1:T(8,128)S(1)}, f32[1024,8,128]{2,0,1:T(8,128)}, s32[]{:T(128)}, /*index=5*/bf16[24,1...) while((s32[]{:T(128)}, f32[1024,8]{0,1:T(8,128)S(1)}, ...), condition=%wide.region_3.5_spmd.clone, body=%wide.region_0.4_spmd.clone.sunk | while | flops 2196807680 | bytes 62130376 | solution.py:96
  270.6 2.4 bitcast_reduce_fusion.4
  273.0 3.8 fusion.84
  276.8 6.3 fusion.86
  284.8 2.4 bitcast_reduce_fusion.4
  287.2 3.8 fusion.84
  291.1 7.9 fusion.86
  303.0 3.8 fusion.84
  306.9 7.9 fusion.86
  318.8 3.8 fusion.84
  322.6 7.9 fusion.86
  332.2 2.4 bitcast_reduce_fusion.4
  334.6 3.8 fusion.84
  338.4 7.9 fusion.86
  350.4 3.8 fusion.84
  354.2 7.9 fusion.86
  362.1 5.5 copy.47
  368.9 5.5 multiply_add_fusion
  374.3 2.8 multiply_add_fusion.1
  377.1 267.1 %all-reduce.2.cloned.1.call-done = f32[1024,16]{0,1:T(8,128)} async-done(((f32[1024,16]{0,1:T(8,128)}), f32[1024,16]{0,1:T(8,128)}) %all-reduce.2.cloned.1.call-update) | async-done | bytes 65552 | tf_op jit(solution)/shard_map/pmax | solution.py:111
  646.2 8.7 maximum_multiply_fusion
  654.8 9.1 copy.61
  664.0 124.6 %reduce-scatter.12.cloned.1.call-done = f32[32,16]{1,0:T(8,128)} async-done(((f32[1024,16]{1,0:T(8,128)}), f32[32,16]{1,0:T(8,128)}) %reduce-scatter.12.cloned.1.call-update) | async-done | bytes 2064
  789.5 225.9 %reduce-scatter.10.cloned.1.call-done = f32[32,2048]{1,0:T(8,128)} async-done(((f32[1024,2048]{1,0:T(8,128)}), f32[32,2048]{1,0:T(8,128)}) %reduce-scatter.10.cloned.1.call-update) | async-done | bytes 262160
  1017.6 129.4 %all-gather.5.cloned.1.call-done = bf16[1024,2048]{1,0:T(8,128)(2,1)} async-done(((bf16[32,2048]{1,0:T(8,128)(2,1)}), bf16[1024,2048]{1,0:T(8,128)(2,1)}) %all-gather.5.cloned.1.call-update) | async-done | bytes 4194320 | tf_op jit(solution)/shard_map/all_gather | solution.py:126
  1147.0 4.4 fusion.55
  1151.4 62.1 %reduce-scatter.8.cloned.1.call-done = f32[256,256]{1,0:T(8,128)} async-done(((f32[1024,256]{1,0:T(8,128)}), f32[256,256]{1,0:T(8,128)}) %reduce-scatter.8.cloned.1.call-update) | async-done | bytes 262160 | tf_op jit(solution)/shard_map/reduce_scatter | solution.py:130
  (171 shorter events, 46.5 us)
Async XLA Ops:
  6.5 1140.4 %copy-start = (bf16[2048,256]{1,0:T(8,128)(2,1)S(1)}, bf16[2048,256]{1,0:T(8,128)(2,1)}, u32[]{:S(2)}) copy-start(bf16[2048,256]{1,0:T(8,128)(2,1)} %param.23) | copy-start | bytes 3145732
  6.5 130.4 %all-gather.3.cloned.1.call-start = ((), (), s32[]{:S(2)}) async-start(), calls=%async_computation.3 | async-start | bytes 4325376 | tf_op jit(solution)/shard_map/all_gather | solution.py:58
  7.3 637.0 %all-reduce.2.cloned.1.call-start = ((), (), s32[]{:S(2)}) async-start(), calls=%async_computation.4 | async-start | bytes 131072 | tf_op jit(solution)/shard_map/pmax | solution.py:111
  7.4 6.6 copy-start.13
  28.5 4.2 copy-start.5
  28.5 7.3 copy-start.7
  28.5 14.5 %copy-start.12 = (s32[1,2]{1,0:T(1,128)S(1)}, s32[1,2]{1,0:T(1,128)}, u32[]{:S(2)}) copy-start(s32[1,2]{1,0:T(1,128)} %param.21) | copy-start | bytes 28
  34.3 27.5 %copy-start.6 = (bf16[24,128,128]{2,1,0:T(8,128)(2,1)S(1)}, bf16[24,128,128]{2,1,0:T(8,128)(2,1)}, u32[]{:S(2)}) copy-start(bf16[24,128,128]{2,1,0:T(8,128)(2,1)} %gather_fusion.1) | copy-start | bytes 2359300
  143.5 7.0 copy-start.10
  150.5 3.9 copy-start.1
  362.1 5.5 copy-start.9
  362.1 5.5 copy-start.4
  362.1 5.8 copy-start.8
  362.1 6.4 copy-start.3
  362.1 6.7 copy-start.11
  368.8 419.9 %reduce-scatter.12.cloned.1.call-start = ((), (), s32[]{:S(2)}) async-start(), calls=%async_computation.8 | async-start | bytes 540672
  368.9 5.5 copy-start.2
  646.1 369.2 %reduce-scatter.10.cloned.1.call-start = ((), (), s32[]{:S(2)}) async-start(), calls=%async_computation.7 | async-start | bytes 8650752
  664.0 483.0 %all-gather.5.cloned.1.call-start = ((), (), s32[]{:S(2)}) async-start(), calls=%async_computation.5 | async-start | bytes 4325376 | tf_op jit(solution)/shard_map/all_gather | solution.py:126
  1017.6 196.0 %reduce-scatter.8.cloned.1.call-start = ((), (), s32[]{:S(2)}) async-start(), calls=%async_computation.6 | async-start | bytes 1310720 | tf_op jit(solution)/shard_map/reduce_scatter | solution.py:130
Sparse Core Ops, SparseCore 0:
  9.0 127.8 all-gather.2
  368.9 275.2 all-reduce.1
  646.7 141.9 reduce-scatter.11
  790.9 224.3 reduce-scatter.9
  1017.7 129.2 all-gather.4
  1151.5 61.9 reduce-scatter.7
where the time goes:
time: 1230 us; the launch traced here: 1220 us
  waiting for transfers between devices  883 us (72%)
  matrix products  148 us (12%)
  other arithmetic  90.1 us (7%)
  local copies, waits for them, and re-layouts  84.6 us (7%)
  between operations  14.4 us (1%)
    unnamed x8, waiting for transfers between devices  351 us
    pmax x1, waiting for transfers between devices, body(): top_max = lax.pmax(maxima_all, 'ctx')  267 us
    all_gather x1, waiting for transfers between devices, body(): lax.all_gather(attn_rows, 'ctx', axis=0, tiled=True)  129 us
    dot_general x14, matrix products, fold_scores(): jnp.einsum('rhk,kd->rhd', weights.astype(jnp.bfloat16), value_rows, prefe...  99.5 us
    all_gather x1, waiting for transfers between devices, body(): query_rows = lax.all_gather(queries, 'ctx', axis=0, tiled=True)  72.7 us
    reduce_scatter x1, waiting for transfers between devices, body(): return lax.psum_scatter(projected, 'tp', scatter_dimension=0, tiled=True)  62.1 us
    reduce_sum x14, other arithmetic, fold_scores(): run_total = run_total * shrink + jnp.sum(weights, axis=-1)  45.9 us
    dot_general x12, matrix products, tile_block(): jnp.einsum('rhd,kd->rhk', query_head, key_block, preferred_element_type=j...  38.1 us
  transfers between devices with their start and end apart: 6, of which 6 were waited for; matrix products, arithmetic and copies ran while one was open for 7% of the time, Pallas kernels for 0%

commit v1 on v0

--- a/solution.py
+++ b/solution.py
@@ -1,14 +1,76 @@
+import functools
+
 import jax
 import jax.numpy as jnp
 from jax import lax
+from jax.experimental import pallas as pl
+from jax.experimental.pallas import tpu as pltpu
 from jax.sharding import PartitionSpec as P
 
 DH = 128
 TILE = 128
 TB = 4
-
+MESH = pl.DeviceIdType.MESH
 
 NEG_INF = -jnp.inf
+
+
+def push_kernel(axis, n, per_dest, count, *refs):
+    x_refs = refs[:count]
+    y_refs = refs[count : 2 * count]
+    send_sem, recv_sem, local_sem = refs[2 * count :]
+    me = lax.axis_index(axis)
+    barrier = pltpu.get_barrier_semaphore()
+    for k in range(1, n):
+        peer = lax.rem(me + k, n)
+        pl.semaphore_signal(barrier, inc=1, device_id={axis: peer}, device_id_type=MESH)
+    pl.semaphore_wait(barrier, n - 1)
+    copies = []
+    for a in range(count):
+        for k in range(1, n):
+            peer = lax.rem(me + k, n)
+            src = x_refs[a].at[peer] if per_dest else x_refs[a]
+            copy = pltpu.make_async_remote_copy(
+                src_ref=src,
+                dst_ref=y_refs[a].at[me],
+                send_sem=send_sem.at[a, k],
+                recv_sem=recv_sem.at[a, k],
+                device_id={axis: peer},
+                device_id_type=MESH,
+            )
+            copy.start()
+            copies.append(copy)
+    locals_ = []
+    for a in range(count):
+        src = x_refs[a].at[me] if per_dest else x_refs[a]
+        local = pltpu.make_async_copy(src, y_refs[a].at[me], local_sem.at[a])
+        local.start()
+        locals_.append(local)
+    for local in locals_:
+        local.wait()
+    for copy in copies:
+        copy.wait()
+
+
+def push(xs, axis, n, per_dest, collective_id):
+    count = len(xs)
+    out_shape = []
+    for x in xs:
+        block = x.shape[1:] if per_dest else x.shape
+        out_shape.append(jax.ShapeDtypeStruct((n,) + tuple(block), x.dtype))
+    any_spec = pl.BlockSpec(memory_space=pl.ANY)
+    return pl.pallas_call(
+        functools.partial(push_kernel, axis, n, per_dest, count),
+        out_shape=tuple(out_shape),
+        in_specs=[any_spec] * count,
+        out_specs=tuple([any_spec] * count),
+        scratch_shapes=[
+            pltpu.SemaphoreType.DMA((count, n)),
+            pltpu.SemaphoreType.DMA((count, n)),
+            pltpu.SemaphoreType.DMA((count,)),
+        ],
+        compiler_params=pltpu.CompilerParams(collective_id=collective_id, has_side_effects=True),
+    )(*xs)
 
 
 def fold_scores(state_now, scores, value_rows):
@@ -40,6 +102,7 @@
     q_local = queries.shape[1] // DH
     group_size = q_local // kv_local
     ctx_count = lax.axis_size("ctx")
+    tp_count = lax.axis_size("tp")
     total_rows = q_dev * ctx_count
     my_index = lax.axis_index("ctx")
     score_scale = DH ** (-0.5)
@@ -55,7 +118,8 @@
         jnp.take(tiled_values[:, :, kv_head, :], keep_tiles[0, kv_head], axis=0)
         for kv_head in range(kv_local)
     ]
-    query_rows = lax.all_gather(queries, "ctx", axis=0, tiled=True)
+    (query_blocks,) = push((queries,), "ctx", ctx_count, False, 0)
+    query_rows = query_blocks.reshape(total_rows, queries.shape[1])
     row_count = query_rows.shape[0]
     row_ids = jnp.arange(row_count, dtype=jnp.int32)
     query_place = owner_slot[row_ids // q_dev] * q_dev + row_ids % q_dev
@@ -105,29 +169,30 @@
         pieces_max.append(head_max)
         pieces_total.append(head_total)
         pieces_sum.append(head_sum.reshape(row_count, group_size * DH))
-    maxima_all = jnp.concatenate(pieces_max, axis=1)
-    totals_all = jnp.concatenate(pieces_total, axis=1)
-    sums_all = jnp.concatenate(pieces_sum, axis=1)
-    top_max = lax.pmax(maxima_all, "ctx")
-    factor = jnp.exp(maxima_all - top_max)
-    scaled = (sums_all.reshape(total_rows, q_local, DH) * factor[..., None]).reshape(
-        total_rows, q_local * DH
-    )
-    numerator, denominator = (
-        lax.psum_scatter(scaled, "ctx", scatter_dimension=0, tiled=True),
-        lax.psum_scatter(totals_all * factor, "ctx", scatter_dimension=0, tiled=True),
+    maxima_all = jnp.concatenate(pieces_max, axis=1).reshape(ctx_count, q_dev, q_local)
+    totals_all = jnp.concatenate(pieces_total, axis=1).reshape(ctx_count, q_dev, q_local)
+    sums_all = jnp.concatenate(pieces_sum, axis=1).reshape(ctx_count, q_dev, q_local * DH)
+    part_max, part_total, part_sum = push((maxima_all, totals_all, sums_all), "ctx", ctx_count, True, 1)
+    top_max = jnp.max(part_max, axis=0)
+    factor = jnp.exp(part_max - top_max[None])
+    denominator = jnp.sum(part_total * factor, axis=0)
+    numerator = jnp.sum(
+        part_sum.reshape(ctx_count, q_dev, q_local, DH) * factor[..., None], axis=0
     )
     attn_rows = (
-        (numerator.reshape(q_dev, q_local, DH) / denominator[..., None])
-        .reshape(q_dev, q_local * DH)
-        .astype(jnp.bfloat16)
-    )
+        (numerator / denominator[..., None]).reshape(q_dev, q_local * DH).astype(jnp.bfloat16)
+    )
+    (attn_blocks,) = push((attn_rows,), "ctx", ctx_count, False, 2)
     projected = jnp.dot(
-        lax.all_gather(attn_rows, "ctx", axis=0, tiled=True),
+        attn_blocks.reshape(total_rows, q_local * DH),
         out_weight,
         preferred_element_type=jnp.float32,
     )
-    return lax.psum_scatter(projected, "tp", scatter_dimension=0, tiled=True)
+    out_rows = total_rows // tp_count
+    (proj_parts,) = push(
+        (projected.reshape(tp_count, out_rows, projected.shape[1]),), "tp", tp_count, True, 3
+    )
+    return jnp.sum(proj_parts, axis=0)
 
 
 def solution(mesh):

time: 1230 us -> 872 us (0.71)
  waiting for transfers between devices: 883 us -> 0 us
  Pallas kernels: 0 us -> 398 us
  other arithmetic: 90.1 us -> 153 us
  matrix products: 148 us -> 191 us
  local copies, waits for them, and re-layouts: 84.6 us -> 127 us
  between operations: 14.4 us -> 1 us
    pallas_call x0 -> x4, Pallas kernels: none -> 398 us  [push(): pl.pallas_call(functools.partial(push_kernel, axis, n, per_dest, count),...]
    unnamed x8 -> x0, waiting for transfers between devices: 351 us -> none
    pmax x1 -> x0, waiting for transfers between devices: 267 us -> none  [body(): top_max = lax.pmax(maxima_all, 'ctx')]
    all_gather x2 -> x0, waiting for transfers between devices: 202 us -> none  [the longest x1 129 us: body(): lax.all_gather(attn_rows, 'ctx', axis=0, tiled=True)]
    reduce_scatter x1 -> x0, waiting for transfers between devices: 62.1 us -> none  [body(): return lax.psum_scatter(projected, 'tp', scatter_dimension=0, tiled=True)]
    reduce_sum x14, other arithmetic: 45.9 us -> 98.9 us  [fold_scores(): run_total = run_total * shrink + jnp.sum(weights, axis=-1)]
    dot_general x12, matrix products: 38.1 us -> 83.9 us  [tile_block(): jnp.einsum('rhd,kd->rhk', query_head, key_block, preferred_element_type=j...]
    while x14 -> x36, local copies, waits for them, and re-layouts: 10.9 us -> 30.9 us  [the longest x2 10.9 us: body(): state_head = lax.fori_loop(0, block_limit, tile_block, start_state)]
  transfers between devices with their start and end apart: 6 -> 0, of which waited for: 6 -> 0; matrix products, arithmetic and copies ran while one was open for 7% -> 0% of each run, Pallas kernels for 0% -> 0%
where the time goes in v1:
time: 872 us; the launch traced here: 870 us
  Pallas kernels  398 us (46%)
  matrix products  191 us (22%)
  other arithmetic  153 us (18%)
  local copies, waits for them, and re-layouts  127 us (15%)
    pallas_call x4, Pallas kernels, push(): pl.pallas_call(functools.partial(push_kernel, axis, n, per_dest, count),...  398 us
    reduce_sum x14, other arithmetic, fold_scores(): run_total = run_total * shrink + jnp.sum(weights, axis=-1)  98.9 us
    dot_general x14, matrix products, fold_scores(): jnp.einsum('rhk,kd->rhd', weights.astype(jnp.bfloat16), value_rows, prefe...  98.7 us
    dot_general x12, matrix products, tile_block(): jnp.einsum('rhd,kd->rhk', query_head, key_block, preferred_element_type=j...  83.9 us
    while x36, local copies, waits for them, and re-layouts  30.9 us

profile of v1, /device:TPU:125, one launch (start us, length us, event | category | flops | bytes accessed | tf_op | source)
XLA Modules:
  0.0 870.3 jit_solution(17850011083169862223)
XLA Ops:
  1.9 4.4 compare_select_fusion.1
  9.3 15.5 %fusion.45 = s32[1024]{0:T(1024)S(1)} fusion(pred[1024]{0:T(1024)(128)(4,1)S(1)} %compare_reduce_fusion, pred[1024]{0:T(1024)(128)(4,1)S(1)} %compare_reduce_fusion.1, pred[1024]{0:T(1024)(128)(4,1)S(1)} %compare_reduce_fusion.2, pred[1024]{0:T(1024)(128)(4,1)S(1)} %compare_reduce_fusion.3, pred[1024]{0:T(1024)(128)(4,1)S(1)} %compare_reduce_fusion.4, ...), kind=kLoop, calls=%fused_computation.126 | loop fusion | flops 33792 | bytes 33892 | tf_op jit(solution)/shard_map/add | solution.py:125
  25.6 90.4 %shard_map.91 = bf16[32,32,2048]{2,1,0:T(8,128)(2,1)} custom-call(bf16[32,2048]{1,0:T(8,128)(2,1)} %refs_0_.1), custom_call_target="tpu_custom_call" | custom-call | tf_op jit(solution)/shard_map/pallas_call | solution.py:62
  116.0 4.7 fusion.49
  120.8 2.9 copy.53
  125.4 4.0 reshape.356
  129.4 5.9 fusion.51
  140.8 3.8 fusion.50
  150.1 3.0 copy.35
  153.8 161.6 %while.36 = (s32[]{:T(128)}, f32[1024,8]{0,1:T(8,128)S(1)}, f32[1024,8]{0,1:T(8,128)S(1)}, f32[1024,8,128]{2,0,1:T(8,128)}, s32[]{:T(128)}, /*index=5*/bf16[24,1...) while((s32[]{:T(128)}, f32[1024,8]{0,1:T(8,128)S(1)}, ...), condition=%wide.region_3.5_spmd.clone, body=%wide.region_0.4_spmd.clone.sunk | while | flops 2196807680 | bytes 129239264 | solution.py:160
  155.5 7.0 bitcast_reduce_fusion.4
  162.5 8.0 fusion.84
  173.1 6.3 fusion.86
  181.1 7.0 bitcast_reduce_fusion.4
  188.1 8.0 fusion.84
  198.7 7.9 fusion.86
  208.3 7.0 bitcast_reduce_fusion.4
  215.3 8.0 fusion.84
  225.9 7.9 fusion.86
  235.5 7.0 bitcast_reduce_fusion.4
  242.5 8.0 fusion.84
  253.1 7.9 fusion.86
  262.7 7.0 bitcast_reduce_fusion.4
  269.7 8.0 fusion.84
  280.3 7.9 fusion.86
  289.9 7.0 bitcast_reduce_fusion.4
  296.9 8.0 fusion.84
  307.5 7.9 fusion.86
  316.9 3.8 multiply_add_fusion.1
  320.7 4.4 copy.44
  325.0 4.9 concatenate.16
  329.9 2.9 copy.56
  337.3 2.8 gather_fusion.3
  342.8 3.0 copy.40
  345.9 161.5 %while.37 = (s32[]{:T(128)}, f32[1024,8]{0,1:T(8,128)S(1)}, f32[1024,8]{0,1:T(8,128)S(1)}, f32[1024,8,128]{2,0,1:T(8,128)}, s32[]{:T(128)}, /*index=5*/bf16[24,1...) while((s32[]{:T(128)}, f32[1024,8]{0,1:T(8,128)S(1)}, ...), condition=%wide.region_8.10_spmd.clone, body=%wide.region_5.9_spmd.clone.sunk | while | flops 2196807680 | bytes 129239264 | solution.py:160
  347.6 7.0 bitcast_reduce_fusion.5
  354.6 8.0 fusion.91
  365.2 6.3 fusion.93
  373.2 7.0 bitcast_reduce_fusion.5
  380.2 8.0 fusion.91
  390.8 7.9 fusion.93
  400.4 7.0 bitcast_reduce_fusion.5
  407.4 8.0 fusion.91
  418.0 7.9 fusion.93
  427.6 7.0 bitcast_reduce_fusion.5
  434.6 8.0 fusion.91
  445.2 7.9 fusion.93
  454.7 7.0 bitcast_reduce_fusion.5
  461.7 8.0 fusion.91
  472.3 7.9 fusion.93
  481.9 7.0 bitcast_reduce_fusion.5
  488.9 8.0 fusion.91
  499.5 7.9 fusion.93
  508.8 3.9 multiply_add_fusion
  512.7 4.4 copy.45
  517.1 4.9 concatenate.17
  522.0 7.8 pad_maximum_fusion.refs_2_
  531.8 197.1 %shard_map.92 = (f32[32,32,16]{2,1,0:T(8,128)}, f32[32,32,16]{2,1,0:T(8,128)}, f32[32,32,2048]{2,1,0:T(8,128)}) custom-call(f32[32,32,16]{2,1,0:T(8,128)} %bitcast.178, f32[32,32,16]{2,1,0:T(8,128)} %bitcast.177, f32[32,32,2048]{2,1,0:T(8,128)} %pad_maximum_fusion.refs_2_), custom_call_target="tpu_custom_call" | custom-call | tf_op jit(solution)/shard_map/pallas_call | solution.py:62
  731.4 4.5 mul.154
  735.9 9.3 %mul.155 = f32[32,32,2048]{2,1,0:T(8,128)} reshape(f32[32,32,16,128]{3,2,1,0:T(8,128)} %mul.154) | data formatting | bytes 16777216 | tf_op jit(solution)/shard_map/mul | solution.py:180
  745.2 7.0 multiply_reduce_fusion
  753.1 92.2 %shard_map.93 = bf16[32,32,2048]{2,1,0:T(8,128)(2,1)} custom-call(bf16[32,2048]{1,0:T(8,128)(2,1)} %fusion.36.refs_0_), custom_call_target="tpu_custom_call" | custom-call | tf_op jit(solution)/shard_map/pallas_call | solution.py:62
  845.3 4.4 fusion.26.refs_0_
  849.7 18.6 %shard_map.94 = f32[4,256,256]{2,1,0:T(8,128)} custom-call(f32[4,256,256]{2,1,0:T(8,128)} %fusion.26.refs_0_), custom_call_target="tpu_custom_call" | custom-call | tf_op jit(solution)/shard_map/pallas_call | solution.py:62
  (175 shorter events, 87.4 us)
Async XLA Ops:
  0.0 845.2 %copy-start = (bf16[2048,256]{1,0:T(8,128)(2,1)S(1)}, bf16[2048,256]{1,0:T(8,128)(2,1)}, u32[]{:S(2)}) copy-start(bf16[2048,256]{1,0:T(8,128)(2,1)} %param.23) | copy-start | bytes 3145732
  120.7 2.9 copy-start.6
  120.7 4.6 copy-start.9
  123.6 11.7 %copy-start.3 = (bf16[1024,1024]{0,1:T(8,128)(2,1)}, bf16[1024,1024]{0,1:T(8,128)(2,1)S(1)}, u32[]{:S(2)}) copy-start(bf16[1024,1024]{0,1:T(8,128)(2,1)S(1)} %copy.53) | copy-start | bytes 6291460
  144.6 3.0 copy-start.5
  146.0 7.1 copy-start.8
  153.8 163.1 %copy-start.7 = (bf16[32,256]{1,0:T(8,128)(2,1)S(1)}, bf16[32,256]{1,0:T(8,128)(2,1)}, u32[]{:S(2)}) copy-start(bf16[32,256]{1,0:T(8,128)(2,1)} %param.17) | copy-start | bytes 49156
  162.5 10.6 %copy-start.1 = (f32[512,1024,8]{1,0,2:T(8,128)S(1)}, f32[512,1024,8]{1,0,2:T(8,128)}, u32[]{:S(2)}) copy-start(f32[512,1024,8]{1,0,2:T(8,128)} %get-tuple-element.601) | copy-start | bytes 50331652 | tf_op jit(solution)/shard_map/while
  188.1 10.6 %copy-start.1 = (f32[512,1024,8]{1,0,2:T(8,128)S(1)}, f32[512,1024,8]{1,0,2:T(8,128)}, u32[]{:S(2)}) copy-start(f32[512,1024,8]{1,0,2:T(8,128)} %get-tuple-element.601) | copy-start | bytes 50331652 | tf_op jit(solution)/shard_map/while
  215.3 10.6 %copy-start.1 = (f32[512,1024,8]{1,0,2:T(8,128)S(1)}, f32[512,1024,8]{1,0,2:T(8,128)}, u32[]{:S(2)}) copy-start(f32[512,1024,8]{1,0,2:T(8,128)} %get-tuple-element.601) | copy-start | bytes 50331652 | tf_op jit(solution)/shard_map/while
  242.5 10.6 %copy-start.1 = (f32[512,1024,8]{1,0,2:T(8,128)S(1)}, f32[512,1024,8]{1,0,2:T(8,128)}, u32[]{:S(2)}) copy-start(f32[512,1024,8]{1,0,2:T(8,128)} %get-tuple-element.601) | copy-start | bytes 50331652 | tf_op jit(solution)/shard_map/while
  269.7 10.6 %copy-start.1 = (f32[512,1024,8]{1,0,2:T(8,128)S(1)}, f32[512,1024,8]{1,0,2:T(8,128)}, u32[]{:S(2)}) copy-start(f32[512,1024,8]{1,0,2:T(8,128)} %get-tuple-element.601) | copy-start | bytes 50331652 | tf_op jit(solution)/shard_map/while
  296.9 10.6 %copy-start.1 = (f32[512,1024,8]{1,0,2:T(8,128)S(1)}, f32[512,1024,8]{1,0,2:T(8,128)}, u32[]{:S(2)}) copy-start(f32[512,1024,8]{1,0,2:T(8,128)} %get-tuple-element.601) | copy-start | bytes 50331652 | tf_op jit(solution)/shard_map/while
  332.8 10.0 %copy-start.4 = (bf16[1024,1024]{0,1:T(8,128)(2,1)}, bf16[1024,1024]{0,1:T(8,128)(2,1)S(1)}, u32[]{:S(2)}) copy-start(bf16[1024,1024]{0,1:T(8,128)(2,1)S(1)} %copy.56) | copy-start | bytes 6291460
  354.6 10.6 %copy-start.2 = (f32[512,1024,8]{1,0,2:T(8,128)S(1)}, f32[512,1024,8]{1,0,2:T(8,128)}, u32[]{:S(2)}) copy-start(f32[512,1024,8]{1,0,2:T(8,128)} %get-tuple-element.615) | copy-start | bytes 50331652 | tf_op jit(solution)/shard_map/while
  380.2 10.6 %copy-start.2 = (f32[512,1024,8]{1,0,2:T(8,128)S(1)}, f32[512,1024,8]{1,0,2:T(8,128)}, u32[]{:S(2)}) copy-start(f32[512,1024,8]{1,0,2:T(8,128)} %get-tuple-element.615) | copy-start | bytes 50331652 | tf_op jit(solution)/shard_map/while
  407.4 10.6 %copy-start.2 = (f32[512,1024,8]{1,0,2:T(8,128)S(1)}, f32[512,1024,8]{1,0,2:T(8,128)}, u32[]{:S(2)}) copy-start(f32[512,1024,8]{1,0,2:T(8,128)} %get-tuple-element.615) | copy-start | bytes 50331652 | tf_op jit(solution)/shard_map/while
  434.6 10.6 %copy-start.2 = (f32[512,1024,8]{1,0,2:T(8,128)S(1)}, f32[512,1024,8]{1,0,2:T(8,128)}, u32[]{:S(2)}) copy-start(f32[512,1024,8]{1,0,2:T(8,128)} %get-tuple-element.615) | copy-start | bytes 50331652 | tf_op jit(solution)/shard_map/while
  461.7 10.6 %copy-start.2 = (f32[512,1024,8]{1,0,2:T(8,128)S(1)}, f32[512,1024,8]{1,0,2:T(8,128)}, u32[]{:S(2)}) copy-start(f32[512,1024,8]{1,0,2:T(8,128)} %get-tuple-element.615) | copy-start | bytes 50331652 | tf_op jit(solution)/shard_map/while
  488.9 10.6 %copy-start.2 = (f32[512,1024,8]{1,0,2:T(8,128)S(1)}, f32[512,1024,8]{1,0,2:T(8,128)}, u32[]{:S(2)}) copy-start(f32[512,1024,8]{1,0,2:T(8,128)} %get-tuple-element.615) | copy-start | bytes 50331652 | tf_op jit(solution)/shard_map/while

commit v2 on v1

v2 whole, which is shorter than its diff:
```python
import functools

import jax
import jax.numpy as jnp
from jax import lax
from jax.experimental import pallas as pl
from jax.experimental.pallas import tpu as pltpu
from jax.sharding import PartitionSpec as P

DH = 128
TILE = 128
TB = 4
MESH = pl.DeviceIdType.MESH

NEG_INF = -jnp.inf


def push_kernel(axis, n, per_dest, count, *refs):
    x_refs = refs[:count]
    y_refs = refs[count : 2 * count]
    send_sem, recv_sem, local_sem = refs[2 * count :]
    me = lax.axis_index(axis)
    barrier = pltpu.get_barrier_semaphore()
    for k in range(1, n):
        peer = lax.rem(me + k, n)
        pl.semaphore_signal(barrier, inc=1, device_id={axis: peer}, device_id_type=MESH)
    pl.semaphore_wait(barrier, n - 1)
    copies = []
    for a in range(count):
        for k in range(1, n):
            peer = lax.rem(me + k, n)
            src = x_refs[a].at[peer] if per_dest else x_refs[a]
            copy = pltpu.make_async_remote_copy(
                src_ref=src,
                dst_ref=y_refs[a].at[me],
                send_sem=send_sem.at[a, k],
                recv_sem=recv_sem.at[a, k],
                device_id={axis: peer},
                device_id_type=MESH,
            )
            copy.start()
            copies.append(copy)
    locals_ = []
    for a in range(count):
        src = x_refs[a].at[me] if per_dest else x_refs[a]
        local = pltpu.make_async_copy(src, y_refs[a].at[me], local_sem.at[a])
        local.start()
        locals_.append(local)
    for local in locals_:
        local.wait()
    for copy in copies:
        copy.wait()


def push(xs, axis, n, per_dest, collective_id):
    count = len(xs)
    out_shape = []
    for x in xs:
        block = x.shape[1:] if per_dest else x.shape
        out_shape.append(jax.ShapeDtypeStruct((n,) + tuple(block), x.dtype))
    any_spec = pl.BlockSpec(memory_space=pl.ANY)
    return pl.pallas_call(
        functools.partial(push_kernel, axis, n, per_dest, count),
        out_shape=tuple(out_shape),
        in_specs=[any_spec] * count,
        out_specs=tuple([any_spec] * count),
        scratch_shapes=[
            pltpu.SemaphoreType.DMA((count, n)),
            pltpu.SemaphoreType.DMA((count, n)),
            pltpu.SemaphoreType.DMA((count,)),
        ],
        compiler_params=pltpu.CompilerParams(collective_id=collective_id, has_side_effects=True),
    )(*xs)


TPB = 4


def dot_nt(a, b):
    return lax.dot_general(a, b, (((1,), (1,)), ((), ())), preferred_element_type=jnp.float32)


def attn_kernel(tpb, group_size, kt_ref, cnt_ref, q_ref, *refs):
    k_refs = refs[:tpb]
    v_refs = refs[tpb : 2 * tpb]
    nk_ref, nv_ref, qp_ref, kp_ref = refs[2 * tpb : 2 * tpb + 4]
    acc_ref, m_out, l_out = refs[2 * tpb + 4 : 2 * tpb + 7]
    m_scr, l_scr = refs[2 * tpb + 7 :]
    g = pl.program_id(0)
    t = pl.program_id(1)
    last = pl.num_programs(1) - 1
    live = cnt_ref[g]
    scale = DH ** (-0.5)

    @pl.when(t == 0)
    def _():
        m_scr[...] = jnp.full(m_scr.shape, NEG_INF, jnp.float32)
        l_scr[...] = jnp.zeros(l_scr.shape, jnp.float32)
        acc_ref[...] = jnp.zeros(acc_ref.shape, jnp.float32)

    def fold(h, keys, values, masks):
        cols = pl.ds(pl.multiple_of(h * DH, DH), DH)
        q = q_ref[:, cols]
        scores = [dot_nt(q, k) * scale + mk for k, mk in zip(keys, masks)]
        m_prev = m_scr[h]
        m_cur = scores[0].max(axis=1, keepdims=True)
        for s in scores[1:]:
            m_cur = jnp.maximum(m_cur, s.max(axis=1, keepdims=True))
        m_new = jnp.maximum(m_prev, m_cur)
        alpha = jnp.exp(m_prev - m_new)
        m_col = m_new[:, :1]
        total = l_scr[h] * alpha
        acc = acc_ref[:, cols] * alpha[:, :1]
        for s, v in zip(scores, values):
            p = jnp.exp(s - m_col)
            total = total + p.sum(axis=1, keepdims=True)
            acc = acc + jnp.dot(p.astype(jnp.bfloat16), v, preferred_element_type=jnp.float32)
        m_scr[h] = m_new
        l_scr[h] = total
        acc_ref[:, cols] = acc

    @pl.when(t * tpb < live)
    def _():
        keys = [k[...] for k in k_refs]
        values = [v[...] for v in v_refs]
        masks = [
            jnp.where(t * tpb + j < live, 0.0, NEG_INF).astype(jnp.float32) for j in range(tpb)
        ]

        def head_body(h, carry):
            fold(h, keys, values, masks)
            return carry

        lax.fori_loop(0, group_size, head_body, 0)

    @pl.when(t == last)
    def _():
        causal = jnp.where(qp_ref[...] >= kp_ref[...], 0.0, NEG_INF).astype(jnp.float32)
        nk = nk_ref[...]
        nv = nv_ref[...]

        def head_body(h, carry):
            fold(h, [nk], [nv], [causal])
            return carry

        lax.fori_loop(0, group_size, head_body, 0)
        for h in range(group_size):
            m_out[:, h : h + 1] = m_scr[h][:, :1]
            l_out[:, h : h + 1] = l_scr[h][:, :1]


def local_attention(query_rows, cache_keys, cache_values, new_keys, new_values, keep, live, query_place, key_place):
    rows, width = query_rows.shape
    kv_local = new_keys.shape[1] // DH
    group_size = width // DH // kv_local
    slots = keep.shape[1]
    steps = slots // TPB
    q_new = new_keys.shape[0]

    def tile_map(j):
        def index_map(g, t, kt_ref, cnt_ref):
            return (kt_ref[g, jnp.minimum(t * TPB + j, cnt_ref[g] - 1)], g)

        return index_map

    tile_spec = [pl.BlockSpec((TILE, DH), tile_map(j)) for j in range(TPB)]
    grid_spec = pltpu.PrefetchScalarGridSpec(
        num_scalar_prefetch=2,
        grid=(kv_local, steps),
        in_specs=[pl.BlockSpec((rows, group_size * DH), lambda g, t, kt, cn: (0, g))]
        + tile_spec
        + tile_spec
        + [
            pl.BlockSpec((q_new, DH), lambda g, t, kt, cn: (0, g)),
            pl.BlockSpec((q_new, DH), lambda g, t, kt, cn: (0, g)),
            pl.BlockSpec((rows, 1), lambda g, t, kt, cn: (0, 0)),
            pl.BlockSpec((1, q_new), lambda g, t, kt, cn: (0, 0)),
        ],
        out_specs=[
            pl.BlockSpec((rows, group_size * DH), lambda g, t, kt, cn: (0, g)),
            pl.BlockSpec((None, rows, group_size), lambda g, t, kt, cn: (g, 0, 0)),
            pl.BlockSpec((None, rows, group_size), lambda g, t, kt, cn: (g, 0, 0)),
        ],
        scratch_shapes=[
            pltpu.VMEM((group_size, rows, DH), jnp.float32),
            pltpu.VMEM((group_size, rows, DH), jnp.float32),
        ],
    )
    keys_total = slots * TILE + q_new
    flops = 4 * rows * kv_local * group_size * keys_total * DH
    cost = pl.CostEstimate(
        flops=flops,
        transcendentals=rows * kv_local * group_size * keys_total,
        bytes_accessed=rows * width * 2 + rows * width * 4 + 2 * kv_local * slots * TILE * DH * 2,
    )
    return pl.pallas_call(
        functools.partial(attn_kernel, TPB, group_size),
        grid_spec=grid_spec,
        out_shape=[
            jax.ShapeDtypeStruct((rows, width), jnp.float32),
            jax.ShapeDtypeStruct((kv_local, rows, group_size), jnp.float32),
            jax.ShapeDtypeStruct((kv_local, rows, group_size), jnp.float32),
        ],
        compiler_params=pltpu.CompilerParams(
            dimension_semantics=("arbitrary", "arbitrary"), vmem_limit_bytes=56 * 1024 * 1024
        ),
        cost_estimate=cost,
    )(keep, live, query_rows, *([cache_keys] * TPB), *([cache_values] * TPB), new_keys, new_values, query_place, key_place)


def body(
    queries,
    new_keys,
    new_values,
    cache_keys,
    cache_values,
    keep_tiles,
    tile_count,
    owner_slot,
    out_weight,
):
    q_dev = queries.shape[0]
    kv_local = new_keys.shape[1] // DH
    q_local = queries.shape[1] // DH
    group_size = q_local // kv_local
    ctx_count = lax.axis_size("ctx")
    tp_count = lax.axis_size("tp")
    total_rows = q_dev * ctx_count
    my_index = lax.axis_index("ctx")
    key_place = owner_slot[my_index] * q_dev + jnp.arange(q_dev, dtype=jnp.int32)
    (query_blocks,) = push((queries,), "ctx", ctx_count, False, 0)
    query_rows = query_blocks.reshape(total_rows, queries.shape[1])
    row_ids = jnp.arange(total_rows, dtype=jnp.int32)
    query_place = owner_slot[row_ids // q_dev] * q_dev + row_ids % q_dev
    sums_all, maxima, totals = local_attention(
        query_rows,
        cache_keys,
        cache_values,
        new_keys,
        new_values,
        keep_tiles[0],
        tile_count[0],
        query_place.reshape(total_rows, 1),
        key_place.reshape(1, q_dev),
    )
    maxima_all = jnp.transpose(maxima, (1, 0, 2)).reshape(ctx_count, q_dev, q_local)
    totals_all = jnp.transpose(totals, (1, 0, 2)).reshape(ctx_count, q_dev, q_local)
    sums_all = sums_all.reshape(ctx_count, q_dev, q_local * DH)
    part_max, part_total, part_sum = push((maxima_all, totals_all, sums_all), "ctx", ctx_count, True, 1)
    top_max = jnp.max(part_max, axis=0)
    factor = jnp.exp(part_max - top_max[None])
    denominator = jnp.sum(part_total * factor, axis=0)
    numerator = jnp.sum(
        part_sum.reshape(ctx_count, q_dev, q_local, DH) * factor[..., None], axis=0
    )
    attn_rows = (
        (numerator / denominator[..., None]).reshape(q_dev, q_local * DH).astype(jnp.bfloat16)
    )
    (attn_blocks,) = push((attn_rows,), "ctx", ctx_count, False, 2)
    projected = jnp.dot(
        attn_blocks.reshape(total_rows, q_local * DH),
        out_weight,
        preferred_element_type=jnp.float32,
    )
    out_rows = total_rows // tp_count
    (proj_parts,) = push(
        (projected.reshape(tp_count, out_rows, projected.shape[1]),), "tp", tp_count, True, 3
    )
    return jnp.sum(proj_parts, axis=0)


def solution(mesh):
    return jax.shard_map(
        body,
        mesh=mesh,
        in_specs=(
            P("ctx", "tp"),
            P("ctx", "tp"),
            P("ctx", "tp"),
            P("ctx", "tp"),
            P("ctx", "tp"),
            P("ctx", "tp", None),
            P("ctx", "tp"),
            P(),
            P("tp", "ctx"),
        ),
        out_specs=P("tp", "ctx"),
        check_vma=False,
    )
```

time: 872 us -> 635 us (0.73)
  matrix products: 191 us -> 4.42 us
  Pallas kernels: 398 us -> 567 us
  other arithmetic: 153 us -> 38.7 us
  local copies, waits for them, and re-layouts: 127 us -> 23.7 us
    dot_general x28 -> x0, matrix products: 186 us -> none  [the longest x14 98.7 us: fold_scores(): jnp.einsum('rhk,kd->rhd', weights.astype(jnp.bfloat16), value_rows, prefe...]
    pallas_call x0 -> x1, Pallas kernels: none -> 163 us  [local_attention(): pl.pallas_call(functools.partial(attn_kernel, TPB, group_size), grid_spec...]
    reduce_sum x14 -> x0, other arithmetic: 98.9 us -> none  [fold_scores(): run_total = run_total * shrink + jnp.sum(weights, axis=-1)]
    while x36 -> x0, local copies, waits for them, and re-layouts: 30.9 us -> none
    mul x0 -> x1, other arithmetic: none -> 15.6 us  [body(): query_place = owner_slot[row_ids // q_dev] * q_dev + row_ids % q_dev]
    slice x4 -> x0, local copies, waits for them, and re-layouts: 15.1 us -> none  [the longest x1 5.92 us: body(): tiled_keys[:, :, kv_head, :]]
    add x1, other arithmetic: 15.5 us -> 0.88 us  [body(): query_place = owner_slot[row_ids // q_dev] * q_dev + row_ids % q_dev]
    dynamic_slice x12 -> x0, local copies, waits for them, and re-layouts: 11.8 us -> none  [tile_block(): lax.dynamic_slice_in_dim(kept_values[kv_head], block_id * TB, TB, 0)]
where the time goes in v2:
time: 635 us; the launch traced here: 634 us
  Pallas kernels  567 us (89%)
  other arithmetic  38.7 us (6%)
  local copies, waits for them, and re-layouts  23.7 us (4%)
    pallas_call x4, Pallas kernels, push(): pl.pallas_call(functools.partial(push_kernel, axis, n, per_dest, count),...  403 us
    pallas_call x1, Pallas kernels, local_attention(): pl.pallas_call(functools.partial(attn_kernel, TPB, group_size), grid_spec...  163 us
    mul x1, other arithmetic, body(): query_place = owner_slot[row_ids // q_dev] * q_dev + row_ids % q_dev  15.6 us
    mul x2, local copies, waits for them, and re-layouts, body(): part_sum.reshape(ctx_count, q_dev, q_local, DH) * factor[..., None]  14 us

profile of v2, /device:TPU:125, one launch (start us, length us, event | category | flops | bytes accessed | tf_op | source)
XLA Modules:
  0.0 634.0 jit_solution(4704962592909278595)
XLA Ops:
  0.0 0.0 copy-start
  0.0 90.2 %shard_map.91 = bf16[32,32,2048]{2,1,0:T(8,128)(2,1)} custom-call(bf16[32,2048]{1,0:T(8,128)(2,1)} %refs_0_.2), custom_call_target="tpu_custom_call" | custom-call | tf_op jit(solution)/shard_map/pallas_call | solution.py:62
  90.3 0.2 fusion.41
  90.4 0.2 fusion.42
  90.6 0.2 fusion.65
  90.7 0.2 fusion.64
  90.9 0.2 fusion.63
  91.1 0.2 fusion.62
  91.2 0.2 fusion.61
  91.4 0.2 fusion.60
  91.6 0.2 fusion.59
  91.8 0.2 fusion.58
  91.9 0.2 fusion.57
  92.1 0.2 fusion.56
  92.3 0.2 fusion.55
  92.5 0.2 fusion.54
  92.7 0.2 fusion.53
  92.9 0.2 fusion.52
  93.1 0.2 fusion.51
  93.3 0.2 fusion.50
  93.5 0.2 fusion.49
  93.7 0.2 fusion.48
  93.9 0.2 fusion.47
  94.1 0.2 fusion.46
  94.3 0.2 fusion.45
  94.6 0.2 fusion.44
  94.8 0.2 fusion.43
  95.0 1.9 fusion.68
  97.0 4.7 select_reduce_fusion
  101.6 2.0 fusion.67
  103.7 15.6 %select_multiply_fusion = s32[1024]{0:T(1024)S(1)} fusion(pred[1024]{0:T(1024)(128)(4,1)S(1)} %fusion.41, pred[1024]{0:T(1024)(128)(4,1)S(1)} %fusion.42, pred[1024]{0:T(1024)(128)(4,1)S(1)} %fusion.65, pred[1024]{0:T(1024)(128)(4,1)S(1)} %fusion.64, pred[1024]{0:T(1024)(128)(4,1)S(1)} %fusion.63, pred[1024]{0:T(1024)(128)(4,1)S(1)} %fusion.62, ...), kind=kLoop, calls=%fused_computation.77 | loop fusion | flops 26624 | bytes 33892 | tf_op jit(solution)/shard_map/mul | solution.py:234
  119.3 0.2 copy.12
  119.5 0.9 fusion.8.refs_10_
  121.0 0.6 iota_add_fusion.refs_11_
  121.6 163.5 %shard_map.92 = (f32[1024,2048]{1,0:T(8,128)}, f32[2,1024,8]{2,1,0:T(8,128)}, f32[2,1024,8]{2,1,0:T(8,128)}) custom-call(s32[2,24]{1,0:T(2,128)} %bitcast.63, s32[2]{0:T(128)} %bitcast.64, bf16[1024,2048]{1,0:T(8,128)(2,1)} %bitcast.57, bf16[4096,256]{1,0:T(8,128)(2,1)} %refs_3_.1, bf16[4096,256]{1,0:T(8,128)(2,1)} %refs_3_.1, bf16[4096,256]{1,0:T(8,128)(2,1)} %refs_3_.1, ...), custom_call_target="tpu_custom_call" | custom-call | flops 26038239232 | bytes 15728640 | tf_op jit(solution)/shard_map/pallas_call | solution.py:196
  285.0 1.5 copy.13
  286.6 0.1 reshape.109
  286.7 1.0 copy.15.refs_0_
  287.7 1.5 copy.14
  289.2 0.1 reshape.110
  289.4 1.1 copy.16.refs_1_
  290.4 209.2 %shard_map.93 = (f32[32,32,16]{2,1,0:T(8,128)}, f32[32,32,16]{2,1,0:T(8,128)}, f32[32,32,2048]{2,1,0:T(8,128)}) custom-call(f32[32,32,16]{2,1,0:T(8,128)} %copy.15.refs_0_, f32[32,32,16]{2,1,0:T(8,128)} %copy.16.refs_1_, f32[32,32,2048]{2,1,0:T(8,128)} %bitcast.56), custom_call_target="tpu_custom_call" | custom-call | tf_op jit(solution)/shard_map/pallas_call | solution.py:62
  499.6 1.1 reduce_max.9
  500.7 1.3 multiply_reduce_fusion.1
  502.0 4.7 mul.37
  506.7 9.3 %mul.38 = f32[32,32,2048]{2,1,0:T(8,128)} reshape(f32[32,32,16,128]{3,2,1,0:T(8,128)} %mul.37) | data formatting | bytes 16777216 | tf_op jit(solution)/shard_map/mul | solution.py:254
  516.0 7.0 %multiply_reduce_fusion = f32[32,2048]{1,0:T(8,128)S(1)} fusion(f32[32,32,2048]{2,1,0:T(8,128)} %get-tuple-element.14, f32[32,32,2048]{2,1,0:T(8,128)} %mul.38), kind=kLoop, calls=%fused_computation | loop fusion | flops 4128768 | bytes 17039360 | tf_op jit(solution)/shard_map/reduce_sum | solution.py:253
  523.0 0.1 div.21
  523.1 0.8 fusion.66.refs_0_
  523.9 85.4 %shard_map.94 = bf16[32,32,2048]{2,1,0:T(8,128)(2,1)} custom-call(bf16[32,2048]{1,0:T(8,128)(2,1)} %fusion.66.refs_0_), custom_call_target="tpu_custom_call" | custom-call | tf_op jit(solution)/shard_map/pallas_call | solution.py:62
  609.3 0.0 copy-done
  609.3 4.4 fusion.refs_0_
  613.8 18.2 %shard_map.95 = f32[4,256,256]{2,1,0:T(8,128)} custom-call(f32[4,256,256]{2,1,0:T(8,128)} %fusion.refs_0_), custom_call_target="tpu_custom_call" | custom-call | tf_op jit(solution)/shard_map/pallas_call | solution.py:62
  632.0 2.0 reduce_sum.29
Async XLA Ops:
  0.0 609.3 %copy-start = (bf16[2048,256]{1,0:T(8,128)(2,1)S(1)}, bf16[2048,256]{1,0:T(8,128)(2,1)}, u32[]{:S(2)}) copy-start(bf16[2048,256]{1,0:T(8,128)(2,1)} %param.17) | copy-start | bytes 3145732

commit v3 on v2

--- a/solution.py
+++ b/solution.py
@@ -73,7 +73,8 @@
     )(*xs)
 
 
-TPB = 4
+TPB = 8
+LOG2E = 1.4426950408889634
 
 
 def dot_nt(a, b):
@@ -84,13 +85,13 @@
     k_refs = refs[:tpb]
     v_refs = refs[tpb : 2 * tpb]
     nk_ref, nv_ref, qp_ref, kp_ref = refs[2 * tpb : 2 * tpb + 4]
-    acc_ref, m_out, l_out = refs[2 * tpb + 4 : 2 * tpb + 7]
-    m_scr, l_scr = refs[2 * tpb + 7 :]
+    sum_out, m_out, l_out = refs[2 * tpb + 4 : 2 * tpb + 7]
+    m_scr, l_scr, acc_ref = refs[2 * tpb + 7 :]
     g = pl.program_id(0)
     t = pl.program_id(1)
     last = pl.num_programs(1) - 1
     live = cnt_ref[g]
-    scale = DH ** (-0.5)
+    coef = DH ** (-0.5) * LOG2E
 
     @pl.when(t == 0)
     def _():
@@ -101,37 +102,51 @@
     def fold(h, keys, values, masks):
         cols = pl.ds(pl.multiple_of(h * DH, DH), DH)
         q = q_ref[:, cols]
-        scores = [dot_nt(q, k) * scale + mk for k, mk in zip(keys, masks)]
+        scores = []
+        for j, k in enumerate(keys):
+            s = dot_nt(q, k)
+            if masks is not None:
+                s = s + masks[j]
+            scores.append(s)
+        top = scores[0]
+        for s in scores[1:]:
+            top = jnp.maximum(top, s)
         m_prev = m_scr[h]
-        m_cur = scores[0].max(axis=1, keepdims=True)
-        for s in scores[1:]:
-            m_cur = jnp.maximum(m_cur, s.max(axis=1, keepdims=True))
-        m_new = jnp.maximum(m_prev, m_cur)
-        alpha = jnp.exp(m_prev - m_new)
-        m_col = m_new[:, :1]
-        total = l_scr[h] * alpha
+        m_new = jnp.maximum(m_prev, top.max(axis=1, keepdims=True))
+        alpha = jnp.exp2((m_prev - m_new) * coef)
+        shift = m_new[:, :1] * coef
         acc = acc_ref[:, cols] * alpha[:, :1]
+        psum = None
         for s, v in zip(scores, values):
-            p = jnp.exp(s - m_col)
-            total = total + p.sum(axis=1, keepdims=True)
+            p = jnp.exp2(s * coef - shift)
+            psum = p if psum is None else psum + p
             acc = acc + jnp.dot(p.astype(jnp.bfloat16), v, preferred_element_type=jnp.float32)
         m_scr[h] = m_new
-        l_scr[h] = total
+        l_scr[h] = l_scr[h] * alpha + psum.sum(axis=1, keepdims=True)
         acc_ref[:, cols] = acc
 
-    @pl.when(t * tpb < live)
-    def _():
+    def tiles_step(masked):
         keys = [k[...] for k in k_refs]
         values = [v[...] for v in v_refs]
-        masks = [
-            jnp.where(t * tpb + j < live, 0.0, NEG_INF).astype(jnp.float32) for j in range(tpb)
-        ]
+        masks = None
+        if masked:
+            masks = [
+                jnp.where(t * tpb + j < live, 0.0, NEG_INF).astype(jnp.float32) for j in range(tpb)
+            ]
 
         def head_body(h, carry):
             fold(h, keys, values, masks)
             return carry
 
         lax.fori_loop(0, group_size, head_body, 0)
+
+    @pl.when((t + 1) * tpb <= live)
+    def _():
+        tiles_step(False)
+
+    @pl.when(jnp.logical_and(t * tpb < live, (t + 1) * tpb > live))
+    def _():
+        tiles_step(True)
 
     @pl.when(t == last)
     def _():
@@ -144,6 +159,7 @@
             return carry
 
         lax.fori_loop(0, group_size, head_body, 0)
+        sum_out[...] = acc_ref[...].astype(sum_out.dtype)
         for h in range(group_size):
             m_out[:, h : h + 1] = m_scr[h][:, :1]
             l_out[:, h : h + 1] = l_scr[h][:, :1]
@@ -184,6 +200,7 @@
         scratch_shapes=[
             pltpu.VMEM((group_size, rows, DH), jnp.float32),
             pltpu.VMEM((group_size, rows, DH), jnp.float32),
+            pltpu.VMEM((rows, group_size * DH), jnp.float32),
         ],
     )
     keys_total = slots * TILE + q_new
@@ -197,7 +214,7 @@
         functools.partial(attn_kernel, TPB, group_size),
         grid_spec=grid_spec,
         out_shape=[
-            jax.ShapeDtypeStruct((rows, width), jnp.float32),
+            jax.ShapeDtypeStruct((rows, width), jnp.bfloat16),
             jax.ShapeDtypeStruct((kv_local, rows, group_size), jnp.float32),
             jax.ShapeDtypeStruct((kv_local, rows, group_size), jnp.float32),
         ],
@@ -248,10 +265,11 @@
     sums_all = sums_all.reshape(ctx_count, q_dev, q_local * DH)
     part_max, part_total, part_sum = push((maxima_all, totals_all, sums_all), "ctx", ctx_count, True, 1)
     top_max = jnp.max(part_max, axis=0)
-    factor = jnp.exp(part_max - top_max[None])
+    factor = jnp.exp2((part_max - top_max[None]) * (DH ** (-0.5) * LOG2E))
     denominator = jnp.sum(part_total * factor, axis=0)
     numerator = jnp.sum(
-        part_sum.reshape(ctx_count, q_dev, q_local, DH) * factor[..., None], axis=0
+        part_sum.reshape(ctx_count, q_dev, q_local, DH).astype(jnp.float32) * factor[..., None],
+        axis=0,
     )
     attn_rows = (
         (numerator / denominator[..., None]).reshape(q_dev, q_local * DH).astype(jnp.bfloat16)

time: 635 us -> 495 us (0.78)
  Pallas kernels: 567 us -> 426 us
    pallas_call x4, Pallas kernels: 403 us -> 282 us  [push(): pl.pallas_call(functools.partial(push_kernel, axis, n, per_dest, count),...]
    pallas_call x1, Pallas kernels: 163 us -> 144 us  [local_attention(): pl.pallas_call(functools.partial(attn_kernel, TPB, group_size), grid_spec...]
where the time goes in v3:
time: 495 us; the launch traced here: 492 us
  Pallas kernels  426 us (86%)
  other arithmetic  37.4 us (8%)
  local copies, waits for them, and re-layouts  23.5 us (5%)
    pallas_call x4, Pallas kernels, push(): pl.pallas_call(functools.partial(push_kernel, axis, n, per_dest, count),...  282 us
    pallas_call x1, Pallas kernels, local_attention(): pl.pallas_call(functools.partial(attn_kernel, TPB, group_size), grid_spec...  144 us
    mul x1, other arithmetic, body(): query_place = owner_slot[row_ids // q_dev] * q_dev + row_ids % q_dev  15.5 us
    mul x2, local copies, waits for them, and re-layouts, body(): part_sum.reshape(ctx_count, q_dev, q_local, DH).astype(jnp.float32)  13.9 us

profile of v3, /device:TPU:125, one launch (start us, length us, event | category | flops | bytes accessed | tf_op | source)
XLA Modules:
  0.0 491.9 jit_solution(6220126258364861749)
XLA Ops:
  0.0 0.0 copy-start
  0.0 1.9 fusion.68
  1.9 4.7 select_reduce_fusion
  6.6 2.0 fusion.67
  8.6 0.2 fusion.41
  8.8 0.2 fusion.42
  8.9 0.2 fusion.43
  9.2 0.2 fusion.44
  9.4 0.2 fusion.45
  9.7 0.2 fusion.46
  9.9 0.2 fusion.47
  10.1 0.2 fusion.48
  10.3 0.2 fusion.49
  10.5 0.2 fusion.50
  10.7 0.2 fusion.51
  10.9 0.2 fusion.52
  11.1 0.2 fusion.53
  11.3 0.2 fusion.54
  11.5 0.2 fusion.55
  11.7 0.2 fusion.56
  11.9 0.2 fusion.57
  12.1 0.2 fusion.58
  12.2 0.2 fusion.59
  12.4 0.2 fusion.60
  12.6 0.2 fusion.61
  12.7 0.2 fusion.62
  12.9 0.2 fusion.63
  13.1 0.2 fusion.64
  13.2 0.2 fusion.65
  13.4 15.5 %select_multiply_fusion = s32[1024]{0:T(1024)S(1)} fusion(pred[1024]{0:T(1024)(128)(4,1)S(1)} %fusion.41, pred[1024]{0:T(1024)(128)(4,1)S(1)} %fusion.42, pred[1024]{0:T(1024)(128)(4,1)S(1)} %fusion.65, pred[1024]{0:T(1024)(128)(4,1)S(1)} %fusion.64, pred[1024]{0:T(1024)(128)(4,1)S(1)} %fusion.63, pred[1024]{0:T(1024)(128)(4,1)S(1)} %fusion.62, ...), kind=kLoop, calls=%fused_computation.77 | loop fusion | flops 26624 | bytes 33892 | tf_op jit(solution)/shard_map/mul | solution.py:251
  28.9 0.2 copy.12
  29.2 0.9 fusion.8.refs_18_
  30.7 0.5 iota_add_fusion.refs_19_
  31.2 90.1 %shard_map.91 = bf16[32,32,2048]{2,1,0:T(8,128)(2,1)} custom-call(bf16[32,2048]{1,0:T(8,128)(2,1)} %refs_0_.2), custom_call_target="tpu_custom_call" | custom-call | tf_op jit(solution)/shard_map/pallas_call | solution.py:62
  121.3 143.6 %shard_map.92 = (bf16[1024,2048]{1,0:T(8,128)(2,1)}, f32[2,1024,8]{2,1,0:T(8,128)}, f32[2,1024,8]{2,1,0:T(8,128)}) custom-call(s32[2,24]{1,0:T(2,128)} %bitcast.63, s32[2]{0:T(128)} %bitcast.64, bf16[1024,2048]{1,0:T(8,128)(2,1)} %bitcast.57, bf16[4096,256]{1,0:T(8,128)(2,1)} %refs_7_.1, bf16[4096,256]{1,0:T(8,128)(2,1)} %refs_7_.1, ...), custom_call_target="tpu_custom_call" | custom-call | flops 26038239232 | bytes 15728640 | tf_op jit(solution)/shard_map/pallas_call | solution.py:213
  264.9 1.5 copy.13
  266.4 0.1 reshape.109
  266.6 1.0 copy.15.refs_0_
  267.6 1.5 copy.14
  269.1 0.1 reshape.110
  269.2 1.1 copy.16.refs_1_
  270.3 75.5 %shard_map.93 = (f32[32,32,16]{2,1,0:T(8,128)}, f32[32,32,16]{2,1,0:T(8,128)}, bf16[32,32,2048]{2,1,0:T(8,128)(2,1)}) custom-call(f32[32,32,16]{2,1,0:T(8,128)} %copy.15.refs_0_, f32[32,32,16]{2,1,0:T(8,128)} %copy.16.refs_1_, bf16[32,32,2048]{2,1,0:T(8,128)(2,1)} %bitcast.56), custom_call_target="tpu_custom_call" | custom-call | tf_op jit(solution)/shard_map/pallas_call | solution.py:62
  345.8 1.1 reduce_max.9
  346.9 1.3 multiply_reduce_fusion.1
  348.3 4.6 mul.39
  352.9 9.3 %mul.40 = f32[32,32,2048]{2,1,0:T(8,128)} reshape(f32[32,32,16,128]{3,2,1,0:T(8,128)} %mul.39) | data formatting | bytes 16777216 | tf_op jit(solution)/shard_map/mul | solution.py:271
  362.1 5.9 %multiply_reduce_fusion = f32[32,2048]{1,0:T(8,128)S(1)} fusion(f32[32,32,2048]{2,1,0:T(8,128)} %mul.40, bf16[32,32,2048]{2,1,0:T(8,128)(2,1)} %get-tuple-element.14), kind=kLoop, calls=%fused_computation | loop fusion | flops 6225920 | bytes 12845056 | tf_op jit(solution)/shard_map/reduce_sum | solution.py:270
  368.0 0.1 div.21
  368.1 0.8 fusion.66.refs_0_
  368.9 74.9 %shard_map.94 = bf16[32,32,2048]{2,1,0:T(8,128)(2,1)} custom-call(bf16[32,2048]{1,0:T(8,128)(2,1)} %fusion.66.refs_0_), custom_call_target="tpu_custom_call" | custom-call | tf_op jit(solution)/shard_map/pallas_call | solution.py:62
  443.8 0.0 copy-done
  443.8 4.4 fusion.refs_0_
  448.2 41.6 %shard_map.95 = f32[4,256,256]{2,1,0:T(8,128)} custom-call(f32[4,256,256]{2,1,0:T(8,128)} %fusion.refs_0_), custom_call_target="tpu_custom_call" | custom-call | tf_op jit(solution)/shard_map/pallas_call | solution.py:62
  489.9 2.0 reduce_sum.29
Async XLA Ops:
  0.0 443.8 %copy-start = (bf16[2048,256]{1,0:T(8,128)(2,1)S(1)}, bf16[2048,256]{1,0:T(8,128)(2,1)}, u32[]{:S(2)}) copy-start(bf16[2048,256]{1,0:T(8,128)(2,1)} %param.17) | copy-start | bytes 3145732

commit v4 on v3

--- a/solution.py
+++ b/solution.py
@@ -86,7 +86,7 @@
     v_refs = refs[tpb : 2 * tpb]
     nk_ref, nv_ref, qp_ref, kp_ref = refs[2 * tpb : 2 * tpb + 4]
     sum_out, m_out, l_out = refs[2 * tpb + 4 : 2 * tpb + 7]
-    m_scr, l_scr, acc_ref = refs[2 * tpb + 7 :]
+    m_scr, acc_ref = refs[2 * tpb + 7 :]
     g = pl.program_id(0)
     t = pl.program_id(1)
     last = pl.num_programs(1) - 1
@@ -96,46 +96,35 @@
     @pl.when(t == 0)
     def _():
         m_scr[...] = jnp.full(m_scr.shape, NEG_INF, jnp.float32)
-        l_scr[...] = jnp.zeros(l_scr.shape, jnp.float32)
         acc_ref[...] = jnp.zeros(acc_ref.shape, jnp.float32)
 
-    def fold(h, keys, values, masks):
+    def fold(h, keys, values_ext, mask):
         cols = pl.ds(pl.multiple_of(h * DH, DH), DH)
-        q = q_ref[:, cols]
-        scores = []
-        for j, k in enumerate(keys):
-            s = dot_nt(q, k)
-            if masks is not None:
-                s = s + masks[j]
-            scores.append(s)
-        top = scores[0]
-        for s in scores[1:]:
-            top = jnp.maximum(top, s)
+        s = dot_nt(q_ref[:, cols], keys)
+        if mask is not None:
+            s = s + mask
         m_prev = m_scr[h]
-        m_new = jnp.maximum(m_prev, top.max(axis=1, keepdims=True))
+        m_new = jnp.maximum(m_prev, s.max(axis=1, keepdims=True))
         alpha = jnp.exp2((m_prev - m_new) * coef)
-        shift = m_new[:, :1] * coef
-        acc = acc_ref[:, cols] * alpha[:, :1]
-        psum = None
-        for s, v in zip(scores, values):
-            p = jnp.exp2(s * coef - shift)
-            psum = p if psum is None else psum + p
-            acc = acc + jnp.dot(p.astype(jnp.bfloat16), v, preferred_element_type=jnp.float32)
+        p = jnp.exp2(s * coef - m_new[:, :1] * coef)
         m_scr[h] = m_new
-        l_scr[h] = l_scr[h] * alpha + psum.sum(axis=1, keepdims=True)
-        acc_ref[:, cols] = acc
+        acc_ref[h] = acc_ref[h] * alpha[:, :1] + jnp.dot(
+            p.astype(jnp.bfloat16), values_ext, preferred_element_type=jnp.float32
+        )
+
+    def with_ones(values):
+        return jnp.concatenate([values, jnp.ones(values.shape, values.dtype)], axis=1)
 
     def tiles_step(masked):
-        keys = [k[...] for k in k_refs]
-        values = [v[...] for v in v_refs]
-        masks = None
+        keys = jnp.concatenate([k[...] for k in k_refs], axis=0)
+        values_ext = with_ones(jnp.concatenate([v[...] for v in v_refs], axis=0))
+        mask = None
         if masked:
-            masks = [
-                jnp.where(t * tpb + j < live, 0.0, NEG_INF).astype(jnp.float32) for j in range(tpb)
-            ]
+            slot = t * tpb + lax.broadcasted_iota(jnp.int32, (1, tpb * TILE), 1) // TILE
+            mask = jnp.where(slot < live, 0.0, NEG_INF).astype(jnp.float32)
 
         def head_body(h, carry):
-            fold(h, keys, values, masks)
+            fold(h, keys, values_ext, mask)
             return carry
 
         lax.fori_loop(0, group_size, head_body, 0)
@@ -152,17 +141,18 @@
     def _():
         causal = jnp.where(qp_ref[...] >= kp_ref[...], 0.0, NEG_INF).astype(jnp.float32)
         nk = nk_ref[...]
-        nv = nv_ref[...]
+        nv_ext = with_ones(nv_ref[...])
 
         def head_body(h, carry):
-            fold(h, [nk], [nv], [causal])
+            fold(h, nk, nv_ext, causal)
             return carry
 
         lax.fori_loop(0, group_size, head_body, 0)
-        sum_out[...] = acc_ref[...].astype(sum_out.dtype)
         for h in range(group_size):
+            acc = acc_ref[h]
+            sum_out[:, h * DH : (h + 1) * DH] = acc[:, :DH].astype(sum_out.dtype)
             m_out[:, h : h + 1] = m_scr[h][:, :1]
-            l_out[:, h : h + 1] = l_scr[h][:, :1]
+            l_out[:, h : h + 1] = acc[:, DH : DH + 1]
 
 
 def local_attention(query_rows, cache_keys, cache_values, new_keys, new_values, keep, live, query_place, key_place):
@@ -199,8 +189,7 @@
         ],
         scratch_shapes=[
             pltpu.VMEM((group_size, rows, DH), jnp.float32),
-            pltpu.VMEM((group_size, rows, DH), jnp.float32),
-            pltpu.VMEM((rows, group_size * DH), jnp.float32),
+            pltpu.VMEM((group_size, rows, 2 * DH), jnp.float32),
         ],
     )
     keys_total = slots * TILE + q_new
@@ -247,8 +236,9 @@
     key_place = owner_slot[my_index] * q_dev + jnp.arange(q_dev, dtype=jnp.int32)
     (query_blocks,) = push((queries,), "ctx", ctx_count, False, 0)
     query_rows = query_blocks.reshape(total_rows, queries.shape[1])
-    row_ids = jnp.arange(total_rows, dtype=jnp.int32)
-    query_place = owner_slot[row_ids // q_dev] * q_dev + row_ids % q_dev
+    query_place = (
+        owner_slot[:, None] * q_dev + jnp.arange(q_dev, dtype=jnp.int32)[None, :]
+    ).reshape(total_rows)
     sums_all, maxima, totals = local_attention(
         query_rows,
         cache_keys,

time: 495 us -> 492 us (level)
  other arithmetic: 37.4 us -> 11.6 us
  Pallas kernels: 426 us -> 450 us
    pallas_call x1, Pallas kernels: 144 us -> 178 us  [local_attention(): pl.pallas_call(functools.partial(attn_kernel, TPB, group_size), grid_spec...]
    mul x1, other arithmetic: 15.5 us -> 0.01 us  [body(): owner_slot[:, None] * q_dev + jnp.arange(q_dev, dtype=jnp.int32)[None, :]]
    pallas_call x4, Pallas kernels: 282 us -> 272 us  [push(): pl.pallas_call(functools.partial(push_kernel, axis, n, per_dest, count),...]
    gather x26 -> x0, other arithmetic: 9.42 us -> none  [body(): query_place = owner_slot[row_ids // q_dev] * q_dev + row_ids % q_dev]
where the time goes in v4:
time: 492 us; the launch traced here: 489 us
  Pallas kernels  450 us (91%)
  local copies, waits for them, and re-layouts  22.1 us (4%)
  other arithmetic  11.6 us (2%)
    pallas_call x4, Pallas kernels, push(): pl.pallas_call(functools.partial(push_kernel, axis, n, per_dest, count),...  272 us
    pallas_call x1, Pallas kernels, local_attention(): pl.pallas_call(functools.partial(attn_kernel, TPB, group_size), grid_spec...  178 us
    mul x2, local copies, waits for them, and re-layouts, body(): part_sum.reshape(ctx_count, q_dev, q_local, DH).astype(jnp.float32)  13.9 us

profile of v4, /device:TPU:125, one launch (start us, length us, event | category | flops | bytes accessed | tf_op | source)
XLA Modules:
  0.0 489.1 jit_solution(17280786856224581204)
XLA Ops:
  0.0 0.0 copy-start
  0.0 0.0 copy-start.1
  0.0 1.3 dynamic_slice.3
  2.0 0.5 iota_add_fusion.1.refs_19_
  2.5 90.1 %shard_map.91 = bf16[32,32,2048]{2,1,0:T(8,128)(2,1)} custom-call(bf16[32,2048]{1,0:T(8,128)(2,1)} %refs_0_.2), custom_call_target="tpu_custom_call" | custom-call | tf_op jit(solution)/shard_map/pallas_call | solution.py:62
  92.6 0.0 copy-done.1
  92.6 0.1 iota_add_fusion
  92.7 1.4 add.46.refs_18_
  94.0 177.9 %shard_map.92 = (bf16[1024,2048]{1,0:T(8,128)(2,1)}, f32[2,1024,8]{2,1,0:T(8,128)}, f32[2,1024,8]{2,1,0:T(8,128)}) custom-call(s32[2,24]{1,0:T(2,128)} %bitcast.29, s32[2]{0:T(128)} %bitcast.30, bf16[1024,2048]{1,0:T(8,128)(2,1)} %bitcast.24, bf16[4096,256]{1,0:T(8,128)(2,1)} %refs_7_.1, bf16[4096,256]{1,0:T(8,128)(2,1)} %refs_7_.1, ...), custom_call_target="tpu_custom_call" | custom-call | flops 26038239232 | bytes 15728640 | tf_op jit(solution)/shard_map/pallas_call | solution.py:202
  272.0 1.5 copy.13
  273.5 0.1 reshape.61
  273.6 1.0 copy.15.refs_0_
  274.7 1.5 copy.14
  276.2 0.1 reshape.62
  276.3 1.1 copy.16.refs_1_
  277.4 80.1 %shard_map.93 = (f32[32,32,16]{2,1,0:T(8,128)}, f32[32,32,16]{2,1,0:T(8,128)}, bf16[32,32,2048]{2,1,0:T(8,128)(2,1)}) custom-call(f32[32,32,16]{2,1,0:T(8,128)} %copy.15.refs_0_, f32[32,32,16]{2,1,0:T(8,128)} %copy.16.refs_1_, bf16[32,32,2048]{2,1,0:T(8,128)(2,1)} %bitcast.23), custom_call_target="tpu_custom_call" | custom-call | tf_op jit(solution)/shard_map/pallas_call | solution.py:62
  357.5 1.1 reduce_max.9
  358.6 1.3 multiply_reduce_fusion.1
  359.9 4.6 mul.33
  364.5 9.3 %mul.34 = f32[32,32,2048]{2,1,0:T(8,128)} reshape(f32[32,32,16,128]{3,2,1,0:T(8,128)} %mul.33) | data formatting | bytes 16777216 | tf_op jit(solution)/shard_map/mul | solution.py:261
  373.8 5.9 %multiply_reduce_fusion = f32[32,2048]{1,0:T(8,128)S(1)} fusion(f32[32,32,2048]{2,1,0:T(8,128)} %mul.34, bf16[32,32,2048]{2,1,0:T(8,128)(2,1)} %get-tuple-element.14), kind=kLoop, calls=%fused_computation | loop fusion | flops 6225920 | bytes 12845056 | tf_op jit(solution)/shard_map/reduce_sum | solution.py:260
  379.6 0.1 div.11
  379.8 0.8 fusion.2.refs_0_
  380.5 49.4 %shard_map.94 = bf16[32,32,2048]{2,1,0:T(8,128)(2,1)} custom-call(bf16[32,2048]{1,0:T(8,128)(2,1)} %fusion.2.refs_0_), custom_call_target="tpu_custom_call" | custom-call | tf_op jit(solution)/shard_map/pallas_call | solution.py:62
  429.9 0.0 copy-done
  429.9 4.4 fusion.refs_0_
  434.3 52.8 %shard_map.95 = f32[4,256,256]{2,1,0:T(8,128)} custom-call(f32[4,256,256]{2,1,0:T(8,128)} %fusion.refs_0_), custom_call_target="tpu_custom_call" | custom-call | tf_op jit(solution)/shard_map/pallas_call | solution.py:62
  487.1 2.0 reduce_sum.29
  (1 shorter events, 0.0 us)
Async XLA Ops:
  0.0 429.9 %copy-start = (bf16[2048,256]{1,0:T(8,128)(2,1)S(1)}, bf16[2048,256]{1,0:T(8,128)(2,1)}, u32[]{:S(2)}) copy-start(bf16[2048,256]{1,0:T(8,128)(2,1)} %param.17) | copy-start | bytes 3145732
  0.0 92.6 %copy-start.1 = (s32[32]{0:T(128)S(1)}, s32[32]{0:T(128)}, u32[]{:S(2)}) copy-start(s32[32]{0:T(128)} %param.16) | copy-start | bytes 388

commit v5 on v4

--- a/solution.py
+++ b/solution.py
@@ -214,6 +214,37 @@
     )(keep, live, query_rows, *([cache_keys] * TPB), *([cache_values] * TPB), new_keys, new_values, query_place, key_place)
 
 
+def combine_kernel(heads, part_ref, fac_ref, den_ref, out_ref):
+    senders = part_ref.shape[0]
+
+    def sender_body(i, acc):
+        blk = part_ref[i].astype(jnp.float32)
+        fac = fac_ref[i]
+        return tuple(
+            acc[h] + blk[:, h * DH : (h + 1) * DH] * fac[:, h : h + 1] for h in range(heads)
+        )
+
+    rows = out_ref.shape[0]
+    start = tuple(jnp.zeros((rows, DH), jnp.float32) for _ in range(heads))
+    acc = lax.fori_loop(0, senders, sender_body, start)
+    den = den_ref[...]
+    for h in range(heads):
+        out_ref[:, h * DH : (h + 1) * DH] = (acc[h] / den[:, h : h + 1]).astype(out_ref.dtype)
+
+
+def combine(part_sum, factor, denominator):
+    senders, rows, width = part_sum.shape
+    heads = width // DH
+    vmem = pl.BlockSpec(memory_space=pltpu.VMEM)
+    return pl.pallas_call(
+        functools.partial(combine_kernel, heads),
+        out_shape=jax.ShapeDtypeStruct((rows, width), jnp.bfloat16),
+        in_specs=[vmem, vmem, vmem],
+        out_specs=vmem,
+        compiler_params=pltpu.CompilerParams(vmem_limit_bytes=32 * 1024 * 1024),
+    )(part_sum, factor, denominator)
+
+
 def body(
     queries,
     new_keys,
@@ -257,13 +288,7 @@
     top_max = jnp.max(part_max, axis=0)
     factor = jnp.exp2((part_max - top_max[None]) * (DH ** (-0.5) * LOG2E))
     denominator = jnp.sum(part_total * factor, axis=0)
-    numerator = jnp.sum(
-        part_sum.reshape(ctx_count, q_dev, q_local, DH).astype(jnp.float32) * factor[..., None],
-        axis=0,
-    )
-    attn_rows = (
-        (numerator / denominator[..., None]).reshape(q_dev, q_local * DH).astype(jnp.bfloat16)
-    )
+    attn_rows = combine(part_sum, factor, denominator)
     (attn_blocks,) = push((attn_rows,), "ctx", ctx_count, False, 2)
     projected = jnp.dot(
         attn_blocks.reshape(total_rows, q_local * DH),

time: 492 us -> 439 us (0.89)
  Pallas kernels: 450 us -> 415 us
  local copies, waits for them, and re-layouts: 22.1 us -> 11 us
  other arithmetic: 11.6 us -> 5.67 us
    pallas_call x1, Pallas kernels: 178 us -> 131 us  [local_attention(): pl.pallas_call(functools.partial(attn_kernel, TPB, group_size), grid_spec...]
    mul x2 -> x0, local copies, waits for them, and re-layouts: 13.9 us -> none  [body(): part_sum.reshape(ctx_count, q_dev, q_local, DH).astype(jnp.float32)]
    pallas_call x4, Pallas kernels: 272 us -> 279 us  [push(): pl.pallas_call(functools.partial(push_kernel, axis, n, per_dest, count),...]
    reduce_sum x1 -> x0, other arithmetic: 5.86 us -> none  [body(): jnp.sum(part_sum.reshape(ctx_count, q_dev, q_local, DH).astype(jnp.float3...]
    pallas_call x0 -> x1, Pallas kernels: none -> 5.4 us  [combine(): pl.pallas_call(functools.partial(combine_kernel, heads), out_shape=jax.Sh...]
where the time goes in v5:
time: 439 us; the launch traced here: 437 us
  Pallas kernels  415 us (95%)
  local copies, waits for them, and re-layouts  11 us (3%)
  other arithmetic  5.67 us (1%)
  matrix products  4.42 us (1%)
    pallas_call x4, Pallas kernels, push(): pl.pallas_call(functools.partial(push_kernel, axis, n, per_dest, count),...  279 us
    pallas_call x1, Pallas kernels, local_attention(): pl.pallas_call(functools.partial(attn_kernel, TPB, group_size), grid_spec...  131 us

profile of v5, /device:TPU:125, one launch (start us, length us, event | category | flops | bytes accessed | tf_op | source)
XLA Modules:
  0.0 436.7 jit_solution(3652977972813129548)
XLA Ops:
  0.0 0.0 copy-start
  0.0 1.3 dynamic_slice.3
  2.0 0.5 iota_add_fusion.1.refs_19_
  2.5 0.7 broadcast_multiply_fusion
  3.1 0.1 iota_add_fusion
  3.2 1.4 add.46.refs_18_
  4.6 90.1 %shard_map.91 = bf16[32,32,2048]{2,1,0:T(8,128)(2,1)} custom-call(bf16[32,2048]{1,0:T(8,128)(2,1)} %refs_0_.2), custom_call_target="tpu_custom_call" | custom-call | tf_op jit(solution)/shard_map/pallas_call | solution.py:62
  94.7 130.5 %shard_map.92 = (bf16[1024,2048]{1,0:T(8,128)(2,1)}, f32[2,1024,8]{2,1,0:T(8,128)}, f32[2,1024,8]{2,1,0:T(8,128)}) custom-call(s32[2,24]{1,0:T(2,128)} %bitcast.21, s32[2]{0:T(128)} %bitcast.22, bf16[1024,2048]{1,0:T(8,128)(2,1)} %bitcast.17, bf16[4096,256]{1,0:T(8,128)(2,1)} %refs_7_.1, bf16[4096,256]{1,0:T(8,128)(2,1)} %refs_7_.1, ...), custom_call_target="tpu_custom_call" | custom-call | flops 26038239232 | bytes 15728640 | tf_op jit(solution)/shard_map/pallas_call | solution.py:202
  225.2 1.5 copy.13
  226.7 1.5 copy.14
  228.2 0.1 reshape.53
  228.4 0.1 reshape.52
  228.5 1.1 copy.15.refs_0_
  229.6 1.1 copy.16.refs_1_
  230.7 76.0 %shard_map.93 = (f32[32,32,16]{2,1,0:T(8,128)}, f32[32,32,16]{2,1,0:T(8,128)}, bf16[32,32,2048]{2,1,0:T(8,128)(2,1)}) custom-call(f32[32,32,16]{2,1,0:T(8,128)} %copy.15.refs_0_, f32[32,32,16]{2,1,0:T(8,128)} %copy.16.refs_1_, bf16[32,32,2048]{2,1,0:T(8,128)(2,1)} %bitcast.16), custom_call_target="tpu_custom_call" | custom-call | tf_op jit(solution)/shard_map/pallas_call | solution.py:62
  306.7 1.1 reduce_max.9
  307.8 1.3 multiply_reduce_fusion
  309.2 0.0 copy-start.1
  309.2 2.2 copy-done.1
  311.4 5.4 %shard_map.94.refs_0_ = bf16[32,2048]{1,0:T(8,128)(2,1)S(1)} custom-call(bf16[32,32,2048]{2,1,0:T(8,128)(2,1)S(1)} %copy-done.1, f32[32,32,16]{2,1,0:T(8,128)S(1)} %get-tuple-element.18.fac_ref, f32[32,16]{1,0:T(8,128)S(1)} %get-tuple-element.17.den_ref), custom_call_target="tpu_custom_call" | custom-call | tf_op jit(solution)/shard_map/pallas_call | solution.py:239
  316.8 0.0 copy-start.2
  316.8 0.6 copy-done.2
  317.4 76.4 %shard_map.95 = bf16[32,32,2048]{2,1,0:T(8,128)(2,1)} custom-call(bf16[32,2048]{1,0:T(8,128)(2,1)} %copy-done.2), custom_call_target="tpu_custom_call" | custom-call | tf_op jit(solution)/shard_map/pallas_call | solution.py:62
  393.9 0.0 copy-done
  393.9 4.4 %fusion.refs_0_ = f32[4,256,256]{2,1,0:T(8,128)} fusion(bf16[4,256,2048]{2,1,0:T(8,128)(2,1)} %bitcast.18, bf16[2048,256]{1,0:T(8,128)(2,1)S(1)} %copy-done), kind=kOutput, calls=%fused_computation | convolution fusion | flops 1073741824 | bytes 6291456 | tf_op jit(solution)/shard_map/dot_general | solution.py:293
  398.3 36.4 %shard_map.96 = f32[4,256,256]{2,1,0:T(8,128)} custom-call(f32[4,256,256]{2,1,0:T(8,128)} %fusion.refs_0_), custom_call_target="tpu_custom_call" | custom-call | tf_op jit(solution)/shard_map/pallas_call | solution.py:62
  434.7 2.0 reduce_sum.19
Async XLA Ops:
  0.0 393.9 %copy-start = (bf16[2048,256]{1,0:T(8,128)(2,1)S(1)}, bf16[2048,256]{1,0:T(8,128)(2,1)}, u32[]{:S(2)}) copy-start(bf16[2048,256]{1,0:T(8,128)(2,1)} %param.17) | copy-start | bytes 3145732
  309.2 2.2 copy-start.1
  316.8 0.7 copy-start.2

commit v6 on v5

--- a/solution.py
+++ b/solution.py
@@ -75,6 +75,7 @@
 
 TPB = 8
 LOG2E = 1.4426950408889634
+RC = 32
 
 
 def dot_nt(a, b):
@@ -86,7 +87,7 @@
     v_refs = refs[tpb : 2 * tpb]
     nk_ref, nv_ref, qp_ref, kp_ref = refs[2 * tpb : 2 * tpb + 4]
     sum_out, m_out, l_out = refs[2 * tpb + 4 : 2 * tpb + 7]
-    m_scr, acc_ref = refs[2 * tpb + 7 :]
+    m_scr, acc_ref, s_scr, p_scr, alpha_scr = refs[2 * tpb + 7 :]
     g = pl.program_id(0)
     t = pl.program_id(1)
     last = pl.num_programs(1) - 1
@@ -112,6 +113,28 @@
             p.astype(jnp.bfloat16), values_ext, preferred_element_type=jnp.float32
         )
 
+    def fold_chunked(h, keys, values_ext, mask):
+        cols = pl.ds(pl.multiple_of(h * DH, DH), DH)
+        s_scr[...] = dot_nt(q_ref[:, cols], keys)
+        rows = s_scr.shape[0]
+
+        def chunk(r, carry):
+            rs = pl.ds(pl.multiple_of(r * RC, RC), RC)
+            s = s_scr[rs, :]
+            if mask is not None:
+                s = s + mask
+            m_prev = m_scr[h, rs, :]
+            m_new = jnp.maximum(m_prev, s.max(axis=1, keepdims=True))
+            alpha_scr[rs, :] = jnp.exp2((m_prev - m_new) * coef)
+            p_scr[rs, :] = jnp.exp2(s * coef - m_new[:, :1] * coef).astype(jnp.bfloat16)
+            m_scr[h, rs, :] = m_new
+            return carry
+
+        lax.fori_loop(0, rows // RC, chunk, 0)
+        acc_ref[h] = acc_ref[h] * alpha_scr[:, :1] + jnp.dot(
+            p_scr[...], values_ext, preferred_element_type=jnp.float32
+        )
+
     def with_ones(values):
         return jnp.concatenate([values, jnp.ones(values.shape, values.dtype)], axis=1)
 
@@ -124,7 +147,7 @@
             mask = jnp.where(slot < live, 0.0, NEG_INF).astype(jnp.float32)
 
         def head_body(h, carry):
-            fold(h, keys, values_ext, mask)
+            fold_chunked(h, keys, values_ext, mask)
             return carry
 
         lax.fori_loop(0, group_size, head_body, 0)
@@ -190,6 +213,9 @@
         scratch_shapes=[
             pltpu.VMEM((group_size, rows, DH), jnp.float32),
             pltpu.VMEM((group_size, rows, 2 * DH), jnp.float32),
+            pltpu.VMEM((rows, TPB * TILE), jnp.float32),
+            pltpu.VMEM((rows, TPB * TILE), jnp.bfloat16),
+            pltpu.VMEM((rows, DH), jnp.float32),
         ],
     )
     keys_total = slots * TILE + q_new

time: 439 us -> 702 us (1.60)
  Pallas kernels: 415 us -> 680 us
    pallas_call x1, Pallas kernels: 131 us -> 376 us  [local_attention(): pl.pallas_call(functools.partial(attn_kernel, TPB, group_size), grid_spec...]
    pallas_call x4, Pallas kernels: 279 us -> 298 us  [push(): pl.pallas_call(functools.partial(push_kernel, axis, n, per_dest, count),...]
where the time goes in v6:
time: 702 us
  Pallas kernels  680 us (97%)
  local copies, waits for them, and re-layouts  11 us (2%)
    pallas_call x1, Pallas kernels, local_attention(): pl.pallas_call(functools.partial(attn_kernel, TPB, group_size), grid_spec...  376 us
    pallas_call x4, Pallas kernels, push(): pl.pallas_call(functools.partial(push_kernel, axis, n, per_dest, count),...  298 us

profile of v6, /device:TPU:125, one launch (start us, length us, event | category | flops | bytes accessed | tf_op | source)
XLA Modules:
  0.0 701.8 jit_solution(6452718064525740497)
XLA Ops:
  0.0 0.0 copy-start
  0.0 1.3 dynamic_slice.3
  2.0 0.5 iota_add_fusion.1.refs_19_
  2.5 0.7 broadcast_multiply_fusion
  3.1 0.1 iota_add_fusion
  3.2 1.4 add.46.refs_18_
  4.6 90.1 %shard_map.91 = bf16[32,32,2048]{2,1,0:T(8,128)(2,1)} custom-call(bf16[32,2048]{1,0:T(8,128)(2,1)} %refs_0_.2), custom_call_target="tpu_custom_call" | custom-call | tf_op jit(solution)/shard_map/pallas_call | solution.py:62
  94.7 376.3 %shard_map.92 = (bf16[1024,2048]{1,0:T(8,128)(2,1)}, f32[2,1024,8]{2,1,0:T(8,128)}, f32[2,1024,8]{2,1,0:T(8,128)}) custom-call(s32[2,24]{1,0:T(2,128)} %bitcast.21, s32[2]{0:T(128)} %bitcast.22, bf16[1024,2048]{1,0:T(8,128)(2,1)} %bitcast.17, bf16[4096,256]{1,0:T(8,128)(2,1)} %refs_7_.1, bf16[4096,256]{1,0:T(8,128)(2,1)} %refs_7_.1, ...), custom_call_target="tpu_custom_call" | custom-call | flops 26038239232 | bytes 15728640 | tf_op jit(solution)/shard_map/pallas_call | solution.py:228
  471.0 1.5 copy.13
  472.5 1.5 copy.14
  474.0 0.1 reshape.53
  474.1 0.1 reshape.52
  474.3 1.1 copy.15.refs_0_
  475.4 1.1 copy.16.refs_1_
  476.5 143.2 %shard_map.93 = (f32[32,32,16]{2,1,0:T(8,128)}, f32[32,32,16]{2,1,0:T(8,128)}, bf16[32,32,2048]{2,1,0:T(8,128)(2,1)}) custom-call(f32[32,32,16]{2,1,0:T(8,128)} %copy.15.refs_0_, f32[32,32,16]{2,1,0:T(8,128)} %copy.16.refs_1_, bf16[32,32,2048]{2,1,0:T(8,128)(2,1)} %bitcast.16), custom_call_target="tpu_custom_call" | custom-call | tf_op jit(solution)/shard_map/pallas_call | solution.py:62
  619.7 1.1 reduce_max.9
  620.8 1.3 multiply_reduce_fusion
  622.1 0.0 copy-start.1
  622.1 2.2 copy-done.1
  624.3 5.4 shard_map.94.refs_0_
  629.7 0.0 copy-start.2
  629.7 0.6 copy-done.2
  630.4 49.4 %shard_map.95 = bf16[32,32,2048]{2,1,0:T(8,128)(2,1)} custom-call(bf16[32,2048]{1,0:T(8,128)(2,1)} %copy-done.2), custom_call_target="tpu_custom_call" | custom-call | tf_op jit(solution)/shard_map/pallas_call | solution.py:62
  679.7 0.0 copy-done
  679.8 4.4 fusion.refs_0_
  684.2 15.6 %shard_map.96 = f32[4,256,256]{2,1,0:T(8,128)} custom-call(f32[4,256,256]{2,1,0:T(8,128)} %fusion.refs_0_), custom_call_target="tpu_custom_call" | custom-call | tf_op jit(solution)/shard_map/pallas_call | solution.py:62
  699.8 2.0 reduce_sum.19
Async XLA Ops:
  0.0 679.7 %copy-start = (bf16[2048,256]{1,0:T(8,128)(2,1)S(1)}, bf16[2048,256]{1,0:T(8,128)(2,1)}, u32[]{:S(2)}) copy-start(bf16[2048,256]{1,0:T(8,128)(2,1)} %param.17) | copy-start | bytes 3145732
  622.1 2.2 copy-start.1
  629.7 0.7 copy-start.2

commit v7 on v5

--- a/solution.py
+++ b/solution.py
@@ -78,7 +78,7 @@
 
 
 def dot_nt(a, b):
-    return lax.dot_general(a, b, (((1,), (1,)), ((), ())), preferred_element_type=jnp.float32)
+    return jnp.dot(a, b, preferred_element_type=jnp.float32)
 
 
 def attn_kernel(tpb, group_size, kt_ref, cnt_ref, q_ref, *refs):
@@ -116,7 +116,7 @@
         return jnp.concatenate([values, jnp.ones(values.shape, values.dtype)], axis=1)
 
     def tiles_step(masked):
-        keys = jnp.concatenate([k[...] for k in k_refs], axis=0)
+        keys = jnp.concatenate([k[...] for k in k_refs], axis=1)
         values_ext = with_ones(jnp.concatenate([v[...] for v in v_refs], axis=0))
         mask = None
         if masked:
@@ -170,14 +170,22 @@
         return index_map
 
     tile_spec = [pl.BlockSpec((TILE, DH), tile_map(j)) for j in range(TPB)]
+
+    def tile_map_t(j):
+        def index_map(g, t, kt_ref, cnt_ref):
+            return (g, kt_ref[g, jnp.minimum(t * TPB + j, cnt_ref[g] - 1)])
+
+        return index_map
+
+    tile_spec_t = [pl.BlockSpec((DH, TILE), tile_map_t(j)) for j in range(TPB)]
     grid_spec = pltpu.PrefetchScalarGridSpec(
         num_scalar_prefetch=2,
         grid=(kv_local, steps),
         in_specs=[pl.BlockSpec((rows, group_size * DH), lambda g, t, kt, cn: (0, g))]
-        + tile_spec
+        + tile_spec_t
         + tile_spec
         + [
-            pl.BlockSpec((q_new, DH), lambda g, t, kt, cn: (0, g)),
+            pl.BlockSpec((DH, q_new), lambda g, t, kt, cn: (g, 0)),
             pl.BlockSpec((q_new, DH), lambda g, t, kt, cn: (0, g)),
             pl.BlockSpec((rows, 1), lambda g, t, kt, cn: (0, 0)),
             pl.BlockSpec((1, q_new), lambda g, t, kt, cn: (0, 0)),
@@ -211,7 +219,7 @@
             dimension_semantics=("arbitrary", "arbitrary"), vmem_limit_bytes=56 * 1024 * 1024
         ),
         cost_estimate=cost,
-    )(keep, live, query_rows, *([cache_keys] * TPB), *([cache_values] * TPB), new_keys, new_values, query_place, key_place)
+    )(keep, live, query_rows, *([cache_keys.T] * TPB), *([cache_values] * TPB), new_keys.T, new_values, query_place, key_place)
 
 
 def combine_kernel(heads, part_ref, fac_ref, den_ref, out_ref):

time: 439 us -> 463 us (1.055)
  Pallas kernels: 415 us -> 435 us
  local copies, waits for them, and re-layouts: 11 us -> 16.6 us
    pallas_call x1, Pallas kernels: 131 us -> 142 us  [local_attention(): pl.pallas_call(functools.partial(attn_kernel, TPB, group_size), grid_spec...]
    pallas_call x4, Pallas kernels: 279 us -> 288 us  [push(): pl.pallas_call(functools.partial(push_kernel, axis, n, per_dest, count),...]
    unnamed x6 -> x8, local copies, waits for them, and re-layouts: 2.83 us -> 8.38 us
where the time goes in v7:
time: 463 us
  Pallas kernels  435 us (94%)
  local copies, waits for them, and re-layouts  16.6 us (4%)
  other arithmetic  5.73 us (1%)
    pallas_call x4, Pallas kernels, push(): pl.pallas_call(functools.partial(push_kernel, axis, n, per_dest, count),...  288 us
    pallas_call x1, Pallas kernels, local_attention(): pl.pallas_call(functools.partial(attn_kernel, TPB, group_size), grid_spec...  142 us

profile of v7, /device:TPU:125, one launch (start us, length us, event | category | flops | bytes accessed | tf_op | source)
XLA Modules:
  0.0 462.8 jit_solution(3941852165054816316)
XLA Ops:
  0.0 0.0 copy-start
  0.0 1.3 dynamic_slice.3
  2.0 0.5 iota_add_fusion.1.refs_19_
  2.5 0.7 broadcast_multiply_fusion
  3.2 0.1 iota_add_fusion
  3.3 1.5 copy.15
  4.7 1.4 add.46.refs_18_
  6.1 4.1 copy.14
  10.2 90.2 %shard_map.91 = bf16[32,32,2048]{2,1,0:T(8,128)(2,1)} custom-call(bf16[32,2048]{1,0:T(8,128)(2,1)} %refs_0_.1), custom_call_target="tpu_custom_call" | custom-call | tf_op jit(solution)/shard_map/pallas_call | solution.py:62
  100.4 141.6 %shard_map.92 = (bf16[1024,2048]{1,0:T(8,128)(2,1)}, f32[2,1024,8]{2,1,0:T(8,128)}, f32[2,1024,8]{2,1,0:T(8,128)}) custom-call(s32[2,24]{1,0:T(2,128)} %bitcast.32, s32[2]{0:T(128)} %bitcast.33, bf16[1024,2048]{1,0:T(8,128)(2,1)} %bitcast.19, bf16[256,4096]{1,0:T(8,128)(2,1)} %bitcast.21, bf16[256,4096]{1,0:T(8,128)(2,1)} %bitcast.22, ...), custom_call_target="tpu_custom_call" | custom-call | flops 26038239232 | bytes 15728640 | tf_op jit(solution)/shard_map/pallas_call | solution.py:210
  242.0 1.5 copy.17
  243.5 1.5 copy.18
  245.0 0.1 reshape.53
  245.1 0.1 reshape.52
  245.2 1.1 copy.19.refs_0_
  246.3 1.1 copy.20.refs_1_
  247.5 100.9 %shard_map.93 = (f32[32,32,16]{2,1,0:T(8,128)}, f32[32,32,16]{2,1,0:T(8,128)}, bf16[32,32,2048]{2,1,0:T(8,128)(2,1)}) custom-call(f32[32,32,16]{2,1,0:T(8,128)} %copy.19.refs_0_, f32[32,32,16]{2,1,0:T(8,128)} %copy.20.refs_1_, bf16[32,32,2048]{2,1,0:T(8,128)(2,1)} %bitcast.18), custom_call_target="tpu_custom_call" | custom-call | tf_op jit(solution)/shard_map/pallas_call | solution.py:62
  348.3 1.1 reduce_max.9
  349.4 1.3 multiply_reduce_fusion
  350.8 0.0 copy-start.1
  350.8 2.2 copy-done.1
  353.0 5.4 %shard_map.94.refs_0_ = bf16[32,2048]{1,0:T(8,128)(2,1)S(1)} custom-call(bf16[32,32,2048]{2,1,0:T(8,128)(2,1)S(1)} %copy-done.1, f32[32,32,16]{2,1,0:T(8,128)S(1)} %get-tuple-element.18.fac_ref, f32[32,16]{1,0:T(8,128)S(1)} %get-tuple-element.17.den_ref), custom_call_target="tpu_custom_call" | custom-call | tf_op jit(solution)/shard_map/pallas_call | solution.py:247
  358.4 0.0 copy-start.2
  358.4 0.6 copy-done.2
  359.0 81.7 %shard_map.95 = bf16[32,32,2048]{2,1,0:T(8,128)(2,1)} custom-call(bf16[32,2048]{1,0:T(8,128)(2,1)} %copy-done.2), custom_call_target="tpu_custom_call" | custom-call | tf_op jit(solution)/shard_map/pallas_call | solution.py:62
  440.8 0.0 copy-done
  440.8 4.4 fusion.refs_0_
  445.2 15.6 %shard_map.96 = f32[4,256,256]{2,1,0:T(8,128)} custom-call(f32[4,256,256]{2,1,0:T(8,128)} %fusion.refs_0_), custom_call_target="tpu_custom_call" | custom-call | tf_op jit(solution)/shard_map/pallas_call | solution.py:62
  460.8 2.0 reduce_sum.19
Async XLA Ops:
  0.0 440.8 %copy-start = (bf16[2048,256]{1,0:T(8,128)(2,1)S(1)}, bf16[2048,256]{1,0:T(8,128)(2,1)}, u32[]{:S(2)}) copy-start(bf16[2048,256]{1,0:T(8,128)(2,1)} %param.17) | copy-start | bytes 3145732
  350.8 2.2 copy-start.1
  358.4 0.7 copy-start.2

commit v8 on v7

--- a/solution.py
+++ b/solution.py
@@ -222,15 +222,171 @@
     )(keep, live, query_rows, *([cache_keys.T] * TPB), *([cache_values] * TPB), new_keys.T, new_values, query_place, key_place)
 
 
+def dense_fold(q_ref, h, keys_t, values_ext, mask, m_scr, acc_ref):
+    coef = DH ** (-0.5) * LOG2E
+    cols = pl.ds(pl.multiple_of(h * DH, DH), DH)
+    s = jnp.dot(q_ref[:, cols], keys_t, preferred_element_type=jnp.float32) + mask
+    m_prev = m_scr[h]
+    m_new = jnp.maximum(m_prev, s.max(axis=1, keepdims=True))
+    alpha = jnp.exp2((m_prev - m_new) * coef)
+    p = jnp.exp2(s * coef - m_new[:, :1] * coef)
+    m_scr[h] = m_new
+    acc_ref[h] = acc_ref[h] * alpha[:, :1] + jnp.dot(
+        p.astype(jnp.bfloat16), values_ext, preferred_element_type=jnp.float32
+    )
+
+
+def attn_push_kernel(n, group_size, *refs):
+    q_ref, kt_ref, v_ref, bias_ref, nkt_ref, nv_ref, qp_ref, kp_ref = refs[:8]
+    srcs = refs[8:11]
+    sum_out, m_out, l_out = refs[11:14]
+    dsts = refs[14:17]
+    m_scr, acc_ref, send_sem, recv_sem, local_sem = refs[17:]
+    t = pl.program_id(0)
+    last = pl.num_programs(0) - 1
+    me = lax.axis_index("ctx")
+
+    def remote_copies():
+        out = []
+        for a in range(3):
+            for k in range(1, n):
+                peer = lax.rem(me + k, n)
+                out.append(
+                    pltpu.make_async_remote_copy(
+                        src_ref=srcs[a].at[peer],
+                        dst_ref=dsts[a].at[me],
+                        send_sem=send_sem.at[a, k],
+                        recv_sem=recv_sem.at[a, k],
+                        device_id={"ctx": peer},
+                        device_id_type=MESH,
+                    )
+                )
+        return out
+
+    def local_copies():
+        return [
+            pltpu.make_async_copy(srcs[a].at[me], dsts[a].at[me], local_sem.at[a]) for a in range(3)
+        ]
+
+    def with_ones(values):
+        return jnp.concatenate([values, jnp.ones(values.shape, values.dtype)], axis=1)
+
+    @pl.when(t == 0)
+    def _():
+        barrier = pltpu.get_barrier_semaphore()
+        for k in range(1, n):
+            peer = lax.rem(me + k, n)
+            pl.semaphore_signal(barrier, inc=1, device_id={"ctx": peer}, device_id_type=MESH)
+        pl.semaphore_wait(barrier, n - 1)
+        for c in remote_copies():
+            c.start()
+        for c in local_copies():
+            c.start()
+        m_scr[...] = jnp.full(m_scr.shape, NEG_INF, jnp.float32)
+        acc_ref[...] = jnp.zeros(acc_ref.shape, jnp.float32)
+
+    keys_t = kt_ref[...]
+    values_ext = with_ones(v_ref[...])
+    mask = bias_ref[...]
+
+    def head_body(h, carry):
+        dense_fold(q_ref, h, keys_t, values_ext, mask, m_scr, acc_ref)
+        return carry
+
+    lax.fori_loop(0, group_size, head_body, 0)
+
+    @pl.when(t == last)
+    def _():
+        causal = jnp.where(qp_ref[...] >= kp_ref[...], 0.0, NEG_INF).astype(jnp.float32)
+        nkt = nkt_ref[...]
+        nv_ext = with_ones(nv_ref[...])
+
+        def new_body(h, carry):
+            dense_fold(q_ref, h, nkt, nv_ext, causal, m_scr, acc_ref)
+            return carry
+
+        lax.fori_loop(0, group_size, new_body, 0)
+        for h in range(group_size):
+            acc = acc_ref[h]
+            sum_out[:, h * DH : (h + 1) * DH] = acc[:, :DH].astype(sum_out.dtype)
+            m_out[:, h : h + 1] = m_scr[h][:, :1]
+            l_out[:, h : h + 1] = acc[:, DH : DH + 1]
+        for c in local_copies():
+            c.wait()
+        for c in remote_copies():
+            c.wait()
+
+
+def attention_with_push(query_rows, keys_t, values, bias, new_keys_t, new_values, query_place, key_place, sends, n):
+    rows, width = query_rows.shape
+    group_size = width // DH
+    total_keys = keys_t.shape[1]
+    step_keys = TPB * TILE
+    steps = total_keys // step_keys
+    q_new = new_values.shape[0]
+    any_spec = pl.BlockSpec(memory_space=pl.ANY)
+    recv_shapes = [
+        jax.ShapeDtypeStruct((n,) + tuple(x.shape[1:]), x.dtype) for x in sends
+    ]
+    flops = 4 * rows * group_size * (total_keys + q_new) * DH
+    cost = pl.CostEstimate(
+        flops=flops,
+        transcendentals=rows * group_size * (total_keys + q_new),
+        bytes_accessed=rows * width * 4 + 2 * total_keys * DH * 2,
+    )
+    return pl.pallas_call(
+        functools.partial(attn_push_kernel, n, group_size),
+        grid=(steps,),
+        in_specs=[
+            pl.BlockSpec((rows, width), lambda t: (0, 0)),
+            pl.BlockSpec((DH, step_keys), lambda t: (0, t)),
+            pl.BlockSpec((step_keys, DH), lambda t: (t, 0)),
+            pl.BlockSpec((1, step_keys), lambda t: (0, t)),
+            pl.BlockSpec((DH, q_new), lambda t: (0, 0)),
+            pl.BlockSpec((q_new, DH), lambda t: (0, 0)),
+            pl.BlockSpec((rows, 1), lambda t: (0, 0)),
+            pl.BlockSpec((1, q_new), lambda t: (0, 0)),
+        ]
+        + [any_spec] * 3,
+        out_specs=[
+            pl.BlockSpec((rows, width), lambda t: (0, 0)),
+            pl.BlockSpec((rows, group_size), lambda t: (0, 0)),
+            pl.BlockSpec((rows, group_size), lambda t: (0, 0)),
+        ]
+        + [any_spec] * 3,
+        out_shape=[
+            jax.ShapeDtypeStruct((rows, width), jnp.bfloat16),
+            jax.ShapeDtypeStruct((rows, group_size), jnp.float32),
+            jax.ShapeDtypeStruct((rows, group_size), jnp.float32),
+        ]
+        + recv_shapes,
+        scratch_shapes=[
+            pltpu.VMEM((group_size, rows, DH), jnp.float32),
+            pltpu.VMEM((group_size, rows, 2 * DH), jnp.float32),
+            pltpu.SemaphoreType.DMA((3, n)),
+            pltpu.SemaphoreType.DMA((3, n)),
+            pltpu.SemaphoreType.DMA((3,)),
+        ],
+        compiler_params=pltpu.CompilerParams(
+            collective_id=4, has_side_effects=True, vmem_limit_bytes=56 * 1024 * 1024
+        ),
+        cost_estimate=cost,
+    )(query_rows, keys_t, values, bias, new_keys_t, new_values, query_place, key_place, *sends)
+
+
 def combine_kernel(heads, part_ref, fac_ref, den_ref, out_ref):
     senders = part_ref.shape[0]
+    width = part_ref.shape[3]
+    half = width // DH
 
     def sender_body(i, acc):
-        blk = part_ref[i].astype(jnp.float32)
         fac = fac_ref[i]
-        return tuple(
-            acc[h] + blk[:, h * DH : (h + 1) * DH] * fac[:, h : h + 1] for h in range(heads)
-        )
+        out = []
+        for h in range(heads):
+            j, c = divmod(h, half)
+            blk = part_ref[i, j][:, c * DH : (c + 1) * DH].astype(jnp.float32)
+            out.append(acc[h] + blk * fac[:, h : h + 1])
+        return tuple(out)
 
     rows = out_ref.shape[0]
     start = tuple(jnp.zeros((rows, DH), jnp.float32) for _ in range(heads))
@@ -241,12 +397,12 @@
 
 
 def combine(part_sum, factor, denominator):
-    senders, rows, width = part_sum.shape
-    heads = width // DH
+    senders, groups, rows, width = part_sum.shape
+    heads = groups * width // DH
     vmem = pl.BlockSpec(memory_space=pltpu.VMEM)
     return pl.pallas_call(
         functools.partial(combine_kernel, heads),
-        out_shape=jax.ShapeDtypeStruct((rows, width), jnp.bfloat16),
+        out_shape=jax.ShapeDtypeStruct((rows, heads * DH), jnp.bfloat16),
         in_specs=[vmem, vmem, vmem],
         out_specs=vmem,
         compiler_params=pltpu.CompilerParams(vmem_limit_bytes=32 * 1024 * 1024),
@@ -278,21 +434,56 @@
     query_place = (
         owner_slot[:, None] * q_dev + jnp.arange(q_dev, dtype=jnp.int32)[None, :]
     ).reshape(total_rows)
-    sums_all, maxima, totals = local_attention(
-        query_rows,
-        cache_keys,
-        cache_values,
-        new_keys,
-        new_values,
-        keep_tiles[0],
-        tile_count[0],
+    width = group_size * DH
+    sums0, maxima0, totals0 = local_attention(
+        query_rows[:, :width],
+        cache_keys[:, :DH],
+        cache_values[:, :DH],
+        new_keys[:, :DH],
+        new_values[:, :DH],
+        keep_tiles[0, :1],
+        tile_count[0, :1],
         query_place.reshape(total_rows, 1),
         key_place.reshape(1, q_dev),
     )
-    maxima_all = jnp.transpose(maxima, (1, 0, 2)).reshape(ctx_count, q_dev, q_local)
-    totals_all = jnp.transpose(totals, (1, 0, 2)).reshape(ctx_count, q_dev, q_local)
-    sums_all = sums_all.reshape(ctx_count, q_dev, q_local * DH)
-    part_max, part_total, part_sum = push((maxima_all, totals_all, sums_all), "ctx", ctx_count, True, 1)
+    slots = keep_tiles.shape[2]
+    tiles_k = cache_keys[:, DH : 2 * DH].reshape(-1, TILE, DH)
+    tiles_v = cache_values[:, DH : 2 * DH].reshape(-1, TILE, DH)
+    kept_k = jnp.take(tiles_k, keep_tiles[0, 1], axis=0).reshape(slots * TILE, DH)
+    kept_v = jnp.take(tiles_v, keep_tiles[0, 1], axis=0).reshape(slots * TILE, DH)
+    slot_ids = jnp.arange(slots * TILE, dtype=jnp.int32) // TILE
+    bias = jnp.where(slot_ids < tile_count[0, 1], 0.0, NEG_INF).astype(jnp.float32)
+    sends0 = (
+        sums0.reshape(ctx_count, q_dev, width),
+        maxima0.reshape(ctx_count, q_dev, group_size),
+        totals0.reshape(ctx_count, q_dev, group_size),
+    )
+    sums1, maxima1, totals1, recv_s0, recv_m0, recv_l0 = attention_with_push(
+        query_rows[:, width:],
+        kept_k.T,
+        kept_v,
+        bias.reshape(1, slots * TILE),
+        new_keys[:, DH:].T,
+        new_values[:, DH:],
+        query_place.reshape(total_rows, 1),
+        key_place.reshape(1, q_dev),
+        sends0,
+        ctx_count,
+    )
+    recv_s1, recv_m1, recv_l1 = push(
+        (
+            sums1.reshape(ctx_count, q_dev, width),
+            maxima1.reshape(ctx_count, q_dev, group_size),
+            totals1.reshape(ctx_count, q_dev, group_size),
+        ),
+        "ctx",
+        ctx_count,
+        True,
+        1,
+    )
+    part_max = jnp.concatenate([recv_m0, recv_m1], axis=2)
+    part_total = jnp.concatenate([recv_l0, recv_l1], axis=2)
+    part_sum = jnp.stack([recv_s0, recv_s1], axis=1)
     top_max = jnp.max(part_max, axis=0)
     factor = jnp.exp2((part_max - top_max[None]) * (DH ** (-0.5) * LOG2E))
     denominator = jnp.sum(part_total * factor, axis=0)

time: 463 us -> 451 us (0.974)
  Pallas kernels: 435 us -> 409 us
  local copies, waits for them, and re-layouts: 16.6 us -> 24.1 us
    pallas_call x0 -> x1, Pallas kernels: none -> 102 us  [attention_with_push(): pl.pallas_call(functools.partial(attn_push_kernel, n, group_size), grid=(...]
    pallas_call x1, Pallas kernels: 142 us -> 62.8 us  [local_attention(): pl.pallas_call(functools.partial(attn_kernel, TPB, group_size), grid_spec...]
    pallas_call x4, Pallas kernels: 288 us -> 238 us  [push(): pl.pallas_call(functools.partial(push_kernel, axis, n, per_dest, count),...]
    slice x0 -> x6, local copies, waits for them, and re-layouts: none -> 12.4 us  [the longest x1 4.66 us: body(): query_rows[:, :width]]
    unnamed x8 -> x19, local copies, waits for them, and re-layouts: 8.38 us -> 3.46 us
where the time goes in v8:
time: 451 us; the launch traced here: 448 us
  Pallas kernels  409 us (91%)
  local copies, waits for them, and re-layouts  24.1 us (5%)
  other arithmetic  10.1 us (2%)
    pallas_call x4, Pallas kernels, push(): pl.pallas_call(functools.partial(push_kernel, axis, n, per_dest, count),...  238 us
    pallas_call x1, Pallas kernels, attention_with_push(): pl.pallas_call(functools.partial(attn_push_kernel, n, group_size), grid=(...  102 us
    pallas_call x1, Pallas kernels, local_attention(): pl.pallas_call(functools.partial(attn_kernel, TPB, group_size), grid_spec...  62.8 us

profile of v8, /device:TPU:125, one launch (start us, length us, event | category | flops | bytes accessed | tf_op | source)
XLA Modules:
  0.0 448.4 jit_solution(868595143272020502)
XLA Ops:
  0.0 0.0 copy-start
  0.0 1.3 dynamic_slice.3
  2.0 0.5 iota_add_fusion.1.refs_19_.refs_7_
  2.5 1.3 slice_bitcast_fusion.kt_ref
  3.7 0.7 broadcast_multiply_fusion
  4.4 1.3 fusion.9
  5.7 0.7 compare_and_fusion
  6.4 1.3 compare_select_fusion.refs_3_
  7.7 0.1 iota_add_fusion
  7.7 0.7 fusion.8
  8.4 1.3 fusion.7
  9.8 0.7 copy.22
  10.5 0.7 copy.20
  11.2 1.3 add.60.refs_18_.refs_6_
  12.5 1.7 fusion.6
  14.2 1.4 copy.21
  15.6 1.6 gather_fusion
  17.1 0.0 copy-start.2
  17.1 2.7 fusion.5
  19.8 1.6 gather_fusion.1
  21.4 0.0 copy-done.2
  21.4 2.2 broadcast_select_fusion
  23.6 1.2 copy.19
  24.8 90.1 %shard_map.91 = bf16[32,32,2048]{2,1,0:T(8,128)(2,1)} custom-call(bf16[32,2048]{1,0:T(8,128)(2,1)} %refs_0_.1), custom_call_target="tpu_custom_call" | custom-call | tf_op jit(solution)/shard_map/pallas_call | solution.py:62
  114.9 4.7 %fusion.4 = (bf16[1024,1024]{1,0:T(8,128)(2,1)}, bf16[1024,1024]{1,0:T(8,128)(2,1)}) fusion(bf16[1024,2048]{1,0:T(8,128)(2,1)} %bitcast.30), kind=kLoop, calls=%fused_computation.24 | loop fusion | bytes 8388608 | tf_op jit(solution)/shard_map/slice | solution.py:439
  119.6 62.8 %shard_map.92 = (bf16[1024,1024]{1,0:T(8,128)(2,1)}, f32[1,1024,8]{2,1,0:T(8,128)}, f32[1,1024,8]{2,1,0:T(8,128)}) custom-call(s32[1,24]{1,0:T(1,128)} %slice_bitcast_fusion.kt_ref, s32[1]{0:T(128)} %bitcast.11.cnt_ref, bf16[1024,1024]{1,0:T(8,128)(2,1)} %get-tuple-element.34.q_ref, bf16[128,4096]{1,0:T(8,128)(2,1)} %bitcast.38, bf16[128,4096]{1,0:T(8,128)(2,1)} %bitcast.39, ...), custom_call_target="tpu_custom_call" | custom-call | flops 13019119616 | bytes 7864320 | tf_op jit(solution)/shard_map/pallas_call | solution.py:210
  182.3 102.3 %shard_map.93 = (bf16[1024,1024]{1,0:T(8,128)(2,1)}, f32[1024,8]{1,0:T(8,128)}, f32[1024,8]{1,0:T(8,128)}, bf16[32,32,1024]{2,1,0:T(8,128)(2,1)}, f32[32,32,8]{2,1,0:T(8,128)}, /*index=5*/f32[32,32,8]{2,1,0:T(8,128)}) custom-call(bf16[1024,1024]{1,0:T(8,128)(2,1)} %get-tuple-element.35.refs_0_, bf16[128,3072]{1,0:T(8,128)(2,1)} %bitcast.46, ...), custom_call_target="tpu_custom_call" | custom-call | flops 13019119616 | bytes 5767168 | tf_op jit(solution)/shard_map/pallas_call | solution.py:337
  284.6 0.0 copy-start.5
  284.6 36.9 %shard_map.94 = (bf16[32,32,1024]{2,1,0:T(8,128)(2,1)}, f32[32,32,8]{2,1,0:T(8,128)}, f32[32,32,8]{2,1,0:T(8,128)}) custom-call(bf16[32,32,1024]{2,1,0:T(8,128)(2,1)} %bitcast.35, f32[32,32,8]{2,1,0:T(8,128)} %bitcast.48, f32[32,32,8]{2,1,0:T(8,128)} %bitcast.49), custom_call_target="tpu_custom_call" | custom-call | tf_op jit(solution)/shard_map/pallas_call | solution.py:62
  321.6 0.0 copy-done.5
  321.6 0.0 copy-start.3
  321.6 0.0 copy-start.4
  321.6 0.0 copy-start.6
  321.6 0.0 copy-start.7
  321.6 2.1 pad_maximum_fusion.part_ref
  323.8 0.0 copy-done.3
  323.8 0.0 copy-done.4
  323.8 0.2 fusion.3
  324.0 0.0 copy-done.6
  324.0 0.0 copy-done.7
  324.0 0.3 fusion.2
  324.4 5.4 %shard_map.95.refs_0_ = bf16[32,2048]{1,0:T(8,128)(2,1)S(1)} custom-call(bf16[32,2,32,1024]{3,2,1,0:T(8,128)(2,1)S(1)} %pad_maximum_fusion.part_ref, f32[32,32,16]{2,1,0:T(8,128)S(1)} %get-tuple-element.31.fac_ref, f32[32,16]{1,0:T(8,128)S(1)} %get-tuple-element.30.den_ref), custom_call_target="tpu_custom_call" | custom-call | tf_op jit(solution)/shard_map/pallas_call | solution.py:403
  329.8 0.0 copy-start.1
  329.8 0.6 copy-done.1
  330.4 90.2 %shard_map.96 = bf16[32,32,2048]{2,1,0:T(8,128)(2,1)} custom-call(bf16[32,2048]{1,0:T(8,128)(2,1)} %copy-done.1), custom_call_target="tpu_custom_call" | custom-call | tf_op jit(solution)/shard_map/pallas_call | solution.py:62
  420.6 0.0 copy-done
  420.6 4.4 fusion.refs_0_
  425.0 21.3 %shard_map.97 = f32[4,256,256]{2,1,0:T(8,128)} custom-call(f32[4,256,256]{2,1,0:T(8,128)} %fusion.refs_0_), custom_call_target="tpu_custom_call" | custom-call | tf_op jit(solution)/shard_map/pallas_call | solution.py:62
  446.3 2.0 reduce_sum.19
  (1 shorter events, 0.0 us)
Async XLA Ops:
  0.0 420.6 %copy-start = (bf16[2048,256]{1,0:T(8,128)(2,1)S(1)}, bf16[2048,256]{1,0:T(8,128)(2,1)}, u32[]{:S(2)}) copy-start(bf16[2048,256]{1,0:T(8,128)(2,1)} %param.19) | copy-start | bytes 3145732
  17.1 4.3 copy-start.2
  284.6 37.0 %copy-start.5 = (bf16[32,32,1024]{2,1,0:T(8,128)(2,1)S(1)}, bf16[32,32,1024]{2,1,0:T(8,128)(2,1)}, u32[]{:S(2)}) copy-start(bf16[32,32,1024]{2,1,0:T(8,128)(2,1)} %get-tuple-element.21) | copy-start | bytes 6291460
  321.6 2.2 copy-start.3
  321.6 2.2 copy-start.4
  321.6 2.4 copy-start.6
  321.6 2.4 copy-start.7
  329.8 0.7 copy-start.1

commit v9 on v8

--- a/solution.py
+++ b/solution.py
@@ -236,24 +236,24 @@
     )
 
 
-def attn_push_kernel(n, group_size, *refs):
+def attn_push_kernel(n, group_size, per_dest, count, *refs):
     q_ref, kt_ref, v_ref, bias_ref, nkt_ref, nv_ref, qp_ref, kp_ref = refs[:8]
-    srcs = refs[8:11]
-    sum_out, m_out, l_out = refs[11:14]
-    dsts = refs[14:17]
-    m_scr, acc_ref, send_sem, recv_sem, local_sem = refs[17:]
+    srcs = refs[8 : 8 + count]
+    sum_out, m_out, l_out = refs[8 + count : 11 + count]
+    dsts = refs[11 + count : 11 + 2 * count]
+    m_scr, acc_ref, send_sem, recv_sem, local_sem = refs[11 + 2 * count :]
     t = pl.program_id(0)
     last = pl.num_programs(0) - 1
     me = lax.axis_index("ctx")
 
     def remote_copies():
         out = []
-        for a in range(3):
+        for a in range(count):
             for k in range(1, n):
                 peer = lax.rem(me + k, n)
                 out.append(
                     pltpu.make_async_remote_copy(
-                        src_ref=srcs[a].at[peer],
+                        src_ref=srcs[a].at[peer] if per_dest else srcs[a],
                         dst_ref=dsts[a].at[me],
                         send_sem=send_sem.at[a, k],
                         recv_sem=recv_sem.at[a, k],
@@ -265,7 +265,10 @@
 
     def local_copies():
         return [
-            pltpu.make_async_copy(srcs[a].at[me], dsts[a].at[me], local_sem.at[a]) for a in range(3)
+            pltpu.make_async_copy(
+                srcs[a].at[me] if per_dest else srcs[a], dsts[a].at[me], local_sem.at[a]
+            )
+            for a in range(count)
         ]
 
     def with_ones(values):
@@ -317,7 +320,7 @@
             c.wait()
 
 
-def attention_with_push(query_rows, keys_t, values, bias, new_keys_t, new_values, query_place, key_place, sends, n):
+def attention_with_push(query_rows, keys_t, values, bias, new_keys_t, new_values, query_place, key_place, sends, n, per_dest, collective_id):
     rows, width = query_rows.shape
     group_size = width // DH
     total_keys = keys_t.shape[1]
@@ -325,8 +328,10 @@
     steps = total_keys // step_keys
     q_new = new_values.shape[0]
     any_spec = pl.BlockSpec(memory_space=pl.ANY)
+    count = len(sends)
     recv_shapes = [
-        jax.ShapeDtypeStruct((n,) + tuple(x.shape[1:]), x.dtype) for x in sends
+        jax.ShapeDtypeStruct((n,) + tuple(x.shape[1:] if per_dest else x.shape), x.dtype)
+        for x in sends
     ]
     flops = 4 * rows * group_size * (total_keys + q_new) * DH
     cost = pl.CostEstimate(
@@ -335,7 +340,7 @@
         bytes_accessed=rows * width * 4 + 2 * total_keys * DH * 2,
     )
     return pl.pallas_call(
-        functools.partial(attn_push_kernel, n, group_size),
+        functools.partial(attn_push_kernel, n, group_size, per_dest, count),
         grid=(steps,),
         in_specs=[
             pl.BlockSpec((rows, width), lambda t: (0, 0)),
@@ -347,13 +352,13 @@
             pl.BlockSpec((rows, 1), lambda t: (0, 0)),
             pl.BlockSpec((1, q_new), lambda t: (0, 0)),
         ]
-        + [any_spec] * 3,
+        + [any_spec] * count,
         out_specs=[
             pl.BlockSpec((rows, width), lambda t: (0, 0)),
             pl.BlockSpec((rows, group_size), lambda t: (0, 0)),
             pl.BlockSpec((rows, group_size), lambda t: (0, 0)),
         ]
-        + [any_spec] * 3,
+        + [any_spec] * count,
         out_shape=[
             jax.ShapeDtypeStruct((rows, width), jnp.bfloat16),
             jax.ShapeDtypeStruct((rows, group_size), jnp.float32),
@@ -363,12 +368,12 @@
         scratch_shapes=[
             pltpu.VMEM((group_size, rows, DH), jnp.float32),
             pltpu.VMEM((group_size, rows, 2 * DH), jnp.float32),
-            pltpu.SemaphoreType.DMA((3, n)),
-            pltpu.SemaphoreType.DMA((3, n)),
-            pltpu.SemaphoreType.DMA((3,)),
+            pltpu.SemaphoreType.DMA((count, n)),
+            pltpu.SemaphoreType.DMA((count, n)),
+            pltpu.SemaphoreType.DMA((count,)),
         ],
         compiler_params=pltpu.CompilerParams(
-            collective_id=4, has_side_effects=True, vmem_limit_bytes=56 * 1024 * 1024
+            collective_id=collective_id, has_side_effects=True, vmem_limit_bytes=56 * 1024 * 1024
         ),
         cost_estimate=cost,
     )(query_rows, keys_t, values, bias, new_keys_t, new_values, query_place, key_place, *sends)
@@ -429,46 +434,48 @@
     total_rows = q_dev * ctx_count
     my_index = lax.axis_index("ctx")
     key_place = owner_slot[my_index] * q_dev + jnp.arange(q_dev, dtype=jnp.int32)
-    (query_blocks,) = push((queries,), "ctx", ctx_count, False, 0)
-    query_rows = query_blocks.reshape(total_rows, queries.shape[1])
+    width = group_size * DH
+    (q0_blocks,) = push((queries[:, :width],), "ctx", ctx_count, False, 0)
     query_place = (
         owner_slot[:, None] * q_dev + jnp.arange(q_dev, dtype=jnp.int32)[None, :]
-    ).reshape(total_rows)
-    width = group_size * DH
-    sums0, maxima0, totals0 = local_attention(
-        query_rows[:, :width],
-        cache_keys[:, :DH],
-        cache_values[:, :DH],
-        new_keys[:, :DH],
-        new_values[:, :DH],
-        keep_tiles[0, :1],
-        tile_count[0, :1],
-        query_place.reshape(total_rows, 1),
-        key_place.reshape(1, q_dev),
-    )
+    ).reshape(total_rows, 1)
+    key_place = key_place.reshape(1, q_dev)
     slots = keep_tiles.shape[2]
-    tiles_k = cache_keys[:, DH : 2 * DH].reshape(-1, TILE, DH)
-    tiles_v = cache_values[:, DH : 2 * DH].reshape(-1, TILE, DH)
-    kept_k = jnp.take(tiles_k, keep_tiles[0, 1], axis=0).reshape(slots * TILE, DH)
-    kept_v = jnp.take(tiles_v, keep_tiles[0, 1], axis=0).reshape(slots * TILE, DH)
     slot_ids = jnp.arange(slots * TILE, dtype=jnp.int32) // TILE
-    bias = jnp.where(slot_ids < tile_count[0, 1], 0.0, NEG_INF).astype(jnp.float32)
+
+    def dense_head(g):
+        cols = slice(g * DH, (g + 1) * DH)
+        tiles_k = cache_keys[:, cols].reshape(-1, TILE, DH)
+        tiles_v = cache_values[:, cols].reshape(-1, TILE, DH)
+        kept_k = jnp.take(tiles_k, keep_tiles[0, g], axis=0).reshape(slots * TILE, DH)
+        kept_v = jnp.take(tiles_v, keep_tiles[0, g], axis=0).reshape(slots * TILE, DH)
+        bias = jnp.where(slot_ids < tile_count[0, g], 0.0, NEG_INF).astype(jnp.float32)
+        return kept_k.T, kept_v, bias.reshape(1, slots * TILE), new_keys[:, cols].T, new_values[:, cols]
+
+    sums0, maxima0, totals0, q1_blocks = attention_with_push(
+        q0_blocks.reshape(total_rows, width),
+        *dense_head(0),
+        query_place,
+        key_place,
+        (queries[:, width:],),
+        ctx_count,
+        False,
+        5,
+    )
     sends0 = (
         sums0.reshape(ctx_count, q_dev, width),
         maxima0.reshape(ctx_count, q_dev, group_size),
         totals0.reshape(ctx_count, q_dev, group_size),
     )
     sums1, maxima1, totals1, recv_s0, recv_m0, recv_l0 = attention_with_push(
-        query_rows[:, width:],
-        kept_k.T,
-        kept_v,
-        bias.reshape(1, slots * TILE),
-        new_keys[:, DH:].T,
-        new_values[:, DH:],
-        query_place.reshape(total_rows, 1),
-        key_place.reshape(1, q_dev),
+        q1_blocks.reshape(total_rows, width),
+        *dense_head(1),
+        query_place,
+        key_place,
         sends0,
         ctx_count,
+        True,
+        4,
     )
     recv_s1, recv_m1, recv_l1 = push(
         (

time: 451 us -> 423 us (0.938)
  Pallas kernels: 409 us -> 380 us
    pallas_call x4, Pallas kernels: 238 us -> 200 us  [push(): pl.pallas_call(functools.partial(push_kernel, axis, n, per_dest, count),...]
    pallas_call x2, Pallas kernels: 165 us -> 174 us  [attention_with_push(): pl.pallas_call(functools.partial(attn_push_kernel, n, group_size, per_des...]
where the time goes in v9:
time: 423 us; the launch traced here: 421 us
  Pallas kernels  380 us (90%)
  local copies, waits for them, and re-layouts  22.8 us (5%)
  other arithmetic  12.6 us (3%)
  matrix products  4.41 us (1%)
    pallas_call x4, Pallas kernels, push(): pl.pallas_call(functools.partial(push_kernel, axis, n, per_dest, count),...  200 us
    pallas_call x2, Pallas kernels, attention_with_push(): pl.pallas_call(functools.partial(attn_push_kernel, n, group_size, per_des...  174 us

profile of v9, /device:TPU:125, one launch (start us, length us, event | category | flops | bytes accessed | tf_op | source)
XLA Modules:
  0.0 420.5 jit_solution(3468535503679151438)
XLA Ops:
  0.0 0.0 copy-start
  0.0 1.3 dynamic_slice.3
  2.0 0.5 iota_add_fusion.1.refs_7_
  2.5 0.7 broadcast_multiply_fusion
  3.2 1.3 fusion.9
  4.5 0.8 compare_and_fusion
  5.3 1.3 compare_select_fusion.refs_3_
  6.5 1.3 compare_select_fusion.1.refs_3_
  7.8 0.1 iota_add_fusion
  7.9 0.7 fusion.8
  8.6 1.3 fusion.7
  9.9 0.7 copy.21
  10.6 0.7 copy.20
  11.3 1.5 fusion.6
  12.9 1.3 add.68.refs_6_
  14.2 42.2 %shard_map.91 = bf16[32,32,1024]{2,1,0:T(8,128)(2,1)} custom-call(bf16[32,1024]{1,0:T(8,128)(2,1)} %get-tuple-element.43.refs_0_), custom_call_target="tpu_custom_call" | custom-call | tf_op jit(solution)/shard_map/pallas_call | solution.py:62
  56.4 1.7 fusion.5
  58.1 1.7 gather_fusion.2
  59.7 1.5 gather_fusion
  61.3 1.7 fusion.4
  63.0 1.6 gather_fusion.3
  64.5 0.0 copy-start.2
  64.5 1.6 gather_fusion.1
  66.1 0.0 copy-done.2
  66.1 3.3 broadcast_select_fusion
  69.4 2.4 copy.19
  71.8 1.2 copy.18
  73.0 83.1 %shard_map.92 = (bf16[1024,1024]{1,0:T(8,128)(2,1)}, f32[1024,8]{1,0:T(8,128)}, f32[1024,8]{1,0:T(8,128)}, bf16[32,32,1024]{2,1,0:T(8,128)(2,1)}) custom-call(bf16[1024,1024]{1,0:T(8,128)(2,1)} %bitcast.44, bf16[128,3072]{1,0:T(8,128)(2,1)} %bitcast.48, bf16[3072,128]{1,0:T(8,128)(2,1)} %bitcast.50, f32[1,3072]{1,0:T(1,128)} %compare_select_fusion.1.refs_3_, ...), custom_call_target="tpu_custom_call" | custom-call | flops 13019119616 | bytes 5767168 | tf_op jit(solution)/shard_map/pallas_call | solution.py:342
  156.1 90.9 %shard_map.93 = (bf16[1024,1024]{1,0:T(8,128)(2,1)}, f32[1024,8]{1,0:T(8,128)}, f32[1024,8]{1,0:T(8,128)}, bf16[32,32,1024]{2,1,0:T(8,128)(2,1)}, f32[32,32,8]{2,1,0:T(8,128)}, /*index=5*/f32[32,32,8]{2,1,0:T(8,128)}) custom-call(bf16[1024,1024]{1,0:T(8,128)(2,1)} %bitcast.56, bf16[128,3072]{1,0:T(8,128)(2,1)} %bitcast.47, bf16[3072,128]{1,0:T(8,128)(2,1)} %bitcast.49, ...), custom_call_target="tpu_custom_call" | custom-call | flops 13019119616 | bytes 5767168 | tf_op jit(solution)/shard_map/pallas_call | solution.py:342
  247.0 0.0 copy-start.5
  247.0 51.8 %shard_map.94 = (bf16[32,32,1024]{2,1,0:T(8,128)(2,1)}, f32[32,32,8]{2,1,0:T(8,128)}, f32[32,32,8]{2,1,0:T(8,128)}) custom-call(bf16[32,32,1024]{2,1,0:T(8,128)(2,1)} %bitcast.43, f32[32,32,8]{2,1,0:T(8,128)} %bitcast.51, f32[32,32,8]{2,1,0:T(8,128)} %bitcast.52), custom_call_target="tpu_custom_call" | custom-call | tf_op jit(solution)/shard_map/pallas_call | solution.py:62
  298.8 0.0 copy-done.5
  298.8 0.0 copy-start.3
  298.9 0.0 copy-start.4
  298.9 0.0 copy-start.6
  298.9 0.0 copy-start.7
  298.9 2.1 pad_maximum_fusion.part_ref
  301.0 0.0 copy-done.3
  301.0 0.0 copy-done.4
  301.0 0.2 fusion.3
  301.2 0.0 copy-done.6
  301.3 0.0 copy-done.7
  301.3 0.3 fusion.2
  301.6 5.4 %shard_map.95.refs_0_ = bf16[32,2048]{1,0:T(8,128)(2,1)S(1)} custom-call(bf16[32,2,32,1024]{3,2,1,0:T(8,128)(2,1)S(1)} %pad_maximum_fusion.part_ref, f32[32,32,16]{2,1,0:T(8,128)S(1)} %get-tuple-element.33.fac_ref, f32[32,16]{1,0:T(8,128)S(1)} %get-tuple-element.32.den_ref), custom_call_target="tpu_custom_call" | custom-call | tf_op jit(solution)/shard_map/pallas_call | solution.py:408
  307.0 0.0 copy-start.1
  307.0 0.6 copy-done.1
  307.7 87.4 %shard_map.96 = bf16[32,32,2048]{2,1,0:T(8,128)(2,1)} custom-call(bf16[32,2048]{1,0:T(8,128)(2,1)} %copy-done.1), custom_call_target="tpu_custom_call" | custom-call | tf_op jit(solution)/shard_map/pallas_call | solution.py:62
  395.1 0.0 copy-done
  395.1 4.4 %fusion.refs_0_ = f32[4,256,256]{2,1,0:T(8,128)} fusion(bf16[4,256,2048]{2,1,0:T(8,128)(2,1)} %bitcast.36, bf16[2048,256]{1,0:T(8,128)(2,1)S(1)} %copy-done), kind=kOutput, calls=%fused_computation.5 | convolution fusion | flops 1073741824 | bytes 6291456 | tf_op jit(solution)/shard_map/dot_general | solution.py:499
  399.5 19.0 %shard_map.97 = f32[4,256,256]{2,1,0:T(8,128)} custom-call(f32[4,256,256]{2,1,0:T(8,128)} %fusion.refs_0_), custom_call_target="tpu_custom_call" | custom-call | tf_op jit(solution)/shard_map/pallas_call | solution.py:62
  418.5 2.0 reduce_sum.19
  (2 shorter events, 0.0 us)
Async XLA Ops:
  0.0 395.1 %copy-start = (bf16[2048,256]{1,0:T(8,128)(2,1)S(1)}, bf16[2048,256]{1,0:T(8,128)(2,1)}, u32[]{:S(2)}) copy-start(bf16[2048,256]{1,0:T(8,128)(2,1)} %param.19) | copy-start | bytes 3145732
  64.5 1.6 copy-start.2
  247.0 51.8 %copy-start.5 = (bf16[32,32,1024]{2,1,0:T(8,128)(2,1)S(1)}, bf16[32,32,1024]{2,1,0:T(8,128)(2,1)}, u32[]{:S(2)}) copy-start(bf16[32,32,1024]{2,1,0:T(8,128)(2,1)} %get-tuple-element.23) | copy-start | bytes 6291460
  298.8 2.2 copy-start.3
  298.9 2.2 copy-start.4
  298.9 2.4 copy-start.6
  298.9 2.4 copy-start.7
  307.0 0.7 copy-start.1

commit v10 on v9

--- a/solution.py
+++ b/solution.py
@@ -253,7 +253,7 @@
                 peer = lax.rem(me + k, n)
                 out.append(
                     pltpu.make_async_remote_copy(
-                        src_ref=srcs[a].at[peer] if per_dest else srcs[a],
+                        src_ref=srcs[a].at[peer] if per_dest[a] else srcs[a],
                         dst_ref=dsts[a].at[me],
                         send_sem=send_sem.at[a, k],
                         recv_sem=recv_sem.at[a, k],
@@ -266,7 +266,7 @@
     def local_copies():
         return [
             pltpu.make_async_copy(
-                srcs[a].at[me] if per_dest else srcs[a], dsts[a].at[me], local_sem.at[a]
+                srcs[a].at[me] if per_dest[a] else srcs[a], dsts[a].at[me], local_sem.at[a]
             )
             for a in range(count)
         ]
@@ -330,8 +330,8 @@
     any_spec = pl.BlockSpec(memory_space=pl.ANY)
     count = len(sends)
     recv_shapes = [
-        jax.ShapeDtypeStruct((n,) + tuple(x.shape[1:] if per_dest else x.shape), x.dtype)
-        for x in sends
+        jax.ShapeDtypeStruct((n,) + tuple(x.shape[1:] if d else x.shape), x.dtype)
+        for x, d in zip(sends, per_dest)
     ]
     flops = 4 * rows * group_size * (total_keys + q_new) * DH
     cost = pl.CostEstimate(
@@ -434,8 +434,10 @@
     total_rows = q_dev * ctx_count
     my_index = lax.axis_index("ctx")
     key_place = owner_slot[my_index] * q_dev + jnp.arange(q_dev, dtype=jnp.int32)
-    width = group_size * DH
-    (q0_blocks,) = push((queries[:, :width],), "ctx", ctx_count, False, 0)
+    pieces = 4
+    piece_heads = q_local // pieces
+    width = piece_heads * DH
+    (q_blocks,) = push((queries[:, :width],), "ctx", ctx_count, False, 0)
     query_place = (
         owner_slot[:, None] * q_dev + jnp.arange(q_dev, dtype=jnp.int32)[None, :]
     ).reshape(total_rows, 1)
@@ -452,45 +454,43 @@
         bias = jnp.where(slot_ids < tile_count[0, g], 0.0, NEG_INF).astype(jnp.float32)
         return kept_k.T, kept_v, bias.reshape(1, slots * TILE), new_keys[:, cols].T, new_values[:, cols]
 
-    sums0, maxima0, totals0, q1_blocks = attention_with_push(
-        q0_blocks.reshape(total_rows, width),
-        *dense_head(0),
-        query_place,
-        key_place,
-        (queries[:, width:],),
-        ctx_count,
-        False,
-        5,
-    )
-    sends0 = (
-        sums0.reshape(ctx_count, q_dev, width),
-        maxima0.reshape(ctx_count, q_dev, group_size),
-        totals0.reshape(ctx_count, q_dev, group_size),
-    )
-    sums1, maxima1, totals1, recv_s0, recv_m0, recv_l0 = attention_with_push(
-        q1_blocks.reshape(total_rows, width),
-        *dense_head(1),
-        query_place,
-        key_place,
-        sends0,
-        ctx_count,
-        True,
-        4,
-    )
-    recv_s1, recv_m1, recv_l1 = push(
-        (
-            sums1.reshape(ctx_count, q_dev, width),
-            maxima1.reshape(ctx_count, q_dev, group_size),
-            totals1.reshape(ctx_count, q_dev, group_size),
-        ),
-        "ctx",
-        ctx_count,
-        True,
-        1,
-    )
-    part_max = jnp.concatenate([recv_m0, recv_m1], axis=2)
-    part_total = jnp.concatenate([recv_l0, recv_l1], axis=2)
-    part_sum = jnp.stack([recv_s0, recv_s1], axis=1)
+    head_data = [dense_head(g) for g in range(kv_local)]
+    received = []
+    previous = None
+    for i in range(pieces):
+        sends = []
+        flags = []
+        if i + 1 < pieces:
+            sends.append(queries[:, (i + 1) * width : (i + 2) * width])
+            flags.append(False)
+        if previous is not None:
+            sends.extend(previous)
+            flags.extend([True, True, True])
+        outs = attention_with_push(
+            q_blocks.reshape(total_rows, width),
+            *head_data[i * kv_local // pieces],
+            query_place,
+            key_place,
+            tuple(sends),
+            ctx_count,
+            tuple(flags),
+            4 + i,
+        )
+        sums_i, maxima_i, totals_i = outs[:3]
+        rest = list(outs[3:])
+        if i + 1 < pieces:
+            q_blocks = rest.pop(0)
+        if previous is not None:
+            received.append(tuple(rest))
+        previous = (
+            sums_i.reshape(ctx_count, q_dev, width),
+            maxima_i.reshape(ctx_count, q_dev, piece_heads),
+            totals_i.reshape(ctx_count, q_dev, piece_heads),
+        )
+    received.append(push(previous, "ctx", ctx_count, True, 1))
+    part_max = jnp.concatenate([r[1] for r in received], axis=2)
+    part_total = jnp.concatenate([r[2] for r in received], axis=2)
+    part_sum = jnp.stack([r[0] for r in received], axis=1)
     top_max = jnp.max(part_max, axis=0)
     factor = jnp.exp2((part_max - top_max[None]) * (DH ** (-0.5) * LOG2E))
     denominator = jnp.sum(part_total * factor, axis=0)

time: 423 us -> 406 us (0.960)
  Pallas kernels: 380 us -> 364 us
    pallas_call x4, Pallas kernels: 200 us -> 166 us  [push(): pl.pallas_call(functools.partial(push_kernel, axis, n, per_dest, count),...]
    pallas_call x2 -> x4, Pallas kernels: 174 us -> 193 us  [attention_with_push(): pl.pallas_call(functools.partial(attn_push_kernel, n, group_size, per_des...]
where the time goes in v10:
time: 406 us
  Pallas kernels  364 us (90%)
  local copies, waits for them, and re-layouts  21.9 us (5%)
  other arithmetic  14.4 us (4%)
  matrix products  4.43 us (1%)
    pallas_call x4, Pallas kernels, attention_with_push(): pl.pallas_call(functools.partial(attn_push_kernel, n, group_size, per_des...  193 us
    pallas_call x4, Pallas kernels, push(): pl.pallas_call(functools.partial(push_kernel, axis, n, per_dest, count),...  166 us

profile of v10, /device:TPU:125, one launch (start us, length us, event | category | flops | bytes accessed | tf_op | source)
XLA Modules:
  0.0 405.8 jit_solution(17887256625898602436)
XLA Ops:
  0.0 0.0 copy-start
  0.0 1.3 dynamic_slice.3
  2.0 0.5 iota_add_fusion.1.refs_7_
  2.5 0.7 broadcast_multiply_fusion
  3.2 1.3 fusion.9
  4.5 0.8 compare_and_fusion
  5.3 1.3 compare_select_fusion.refs_3_
  6.5 1.2 compare_select_fusion.1.refs_3_
  7.8 0.1 iota_add_fusion
  7.9 0.7 fusion.8
  8.6 1.3 fusion.7
  9.9 0.7 copy.23
  10.6 0.7 copy.22
  11.3 1.4 fusion.6
  12.8 1.3 add.68.refs_6_
  14.1 20.5 %shard_map.91 = bf16[32,32,512]{2,1,0:T(8,128)(2,1)} custom-call(bf16[32,512]{1,0:T(8,128)(2,1)} %get-tuple-element.74.refs_0_), custom_call_target="tpu_custom_call" | custom-call | tf_op jit(solution)/shard_map/pallas_call | solution.py:62
  34.6 1.7 fusion.5
  36.2 1.6 gather_fusion.2
  37.8 1.6 gather_fusion
  39.4 1.7 fusion.4
  41.0 1.6 gather_fusion.3
  42.6 0.7 gather_fusion.1
  43.3 3.4 broadcast_select_fusion
  46.7 2.3 copy.21
  49.0 1.1 copy.20
  50.1 44.5 %shard_map.92 = (bf16[1024,512]{1,0:T(8,128)(2,1)}, f32[1024,4]{1,0:T(8,128)}, f32[1024,4]{1,0:T(8,128)}, bf16[32,32,512]{2,1,0:T(8,128)(2,1)}) custom-call(bf16[1024,512]{1,0:T(8,128)(2,1)} %bitcast.53, bf16[128,3072]{1,0:T(8,128)(2,1)} %bitcast.61, bf16[3072,128]{1,0:T(8,128)(2,1)} %bitcast.65, f32[1,3072]{1,0:T(1,128)} %compare_select_fusion.1.refs_3_, ...), custom_call_target="tpu_custom_call" | custom-call | flops 6509559808 | bytes 3670016 | tf_op jit(solution)/shard_map/pallas_call | solution.py:342
  94.6 50.6 %shard_map.93 = (bf16[1024,512]{1,0:T(8,128)(2,1)}, f32[1024,4]{1,0:T(8,128)}, f32[1024,4]{1,0:T(8,128)}, bf16[32,32,512]{2,1,0:T(8,128)(2,1)}, bf16[32,32,512]{...) custom-call(bf16[1024,512]{1,0:T(8,128)(2,1)} %bitcast.78, bf16[128,3072]{1,0:T(8,128)(2,1)} %bitcast.62, ...), custom_call_target="tpu_custom_call" | custom-call | flops 6509559808 | bytes 3670016 | tf_op jit(solution)/shard_map/pallas_call | solution.py:342
  145.2 48.9 %shard_map.94 = (bf16[1024,512]{1,0:T(8,128)(2,1)}, f32[1024,4]{1,0:T(8,128)}, f32[1024,4]{1,0:T(8,128)}, bf16[32,32,512]{2,1,0:T(8,128)(2,1)}, bf16[32,32,512]{...) custom-call(bf16[1024,512]{1,0:T(8,128)(2,1)} %bitcast.74, bf16[128,3072]{1,0:T(8,128)(2,1)} %bitcast.59, ...), custom_call_target="tpu_custom_call" | custom-call | flops 6509559808 | bytes 3670016 | tf_op jit(solution)/shard_map/pallas_call | solution.py:342
  194.2 49.3 %shard_map.95 = (bf16[1024,512]{1,0:T(8,128)(2,1)}, f32[1024,4]{1,0:T(8,128)}, f32[1024,4]{1,0:T(8,128)}, bf16[32,32,512]{2,1,0:T(8,128)(2,1)}, f32[32,32,4]{2,1,0:T(8,128)}, /*index=5*/f32[32,32,4]{2,1,0:T(8,128)}) custom-call(bf16[1024,512]{1,0:T(8,128)(2,1)} %bitcast.76, bf16[128,3072]{1,0:T(8,128)(2,1)} %bitcast.60, bf16[3072,128]{1,0:T(8,128)(2,1)} %bitcast.64, ...), custom_call_target="tpu_custom_call" | custom-call | flops 6509559808 | bytes 3670016 | tf_op jit(solution)/shard_map/pallas_call | solution.py:342
  243.5 0.0 copy-start.2
  243.5 0.0 copy-start.3
  243.5 31.7 %shard_map.96 = (bf16[32,32,512]{2,1,0:T(8,128)(2,1)}, f32[32,32,4]{2,1,0:T(8,128)}, f32[32,32,4]{2,1,0:T(8,128)}) custom-call(bf16[32,32,512]{2,1,0:T(8,128)(2,1)} %bitcast.54, f32[32,32,4]{2,1,0:T(8,128)} %bitcast.67, f32[32,32,4]{2,1,0:T(8,128)} %bitcast.68), custom_call_target="tpu_custom_call" | custom-call | tf_op jit(solution)/shard_map/pallas_call | solution.py:62
  275.2 2.0 fusion.3
  277.2 0.0 copy-done.2
  277.2 0.0 copy-done.3
  277.2 0.0 copy-start.4
  277.2 0.0 copy-start.5
  277.2 0.0 copy-start.6
  277.2 0.0 copy-start.7
  277.2 1.9 pad_maximum_fusion.part_ref
  279.2 0.0 copy-done.4
  279.2 0.0 copy-done.5
  279.2 0.0 copy-done.6
  279.2 0.1 copy-done.7
  279.4 0.5 fusion.2
  279.8 5.4 %shard_map.97.refs_0_ = bf16[32,2048]{1,0:T(8,128)(2,1)S(1)} custom-call(bf16[32,4,32,512]{3,2,1,0:T(8,128)(2,1)S(1)} %pad_maximum_fusion.part_ref, f32[32,32,16]{2,1,0:T(8,128)S(1)} %get-tuple-element.61.fac_ref, f32[32,16]{1,0:T(8,128)S(1)} %get-tuple-element.60.den_ref), custom_call_target="tpu_custom_call" | custom-call | tf_op jit(solution)/shard_map/pallas_call | solution.py:408
  285.2 0.0 copy-start.1
  285.3 0.6 copy-done.1
  285.9 96.2 %shard_map.98 = bf16[32,32,2048]{2,1,0:T(8,128)(2,1)} custom-call(bf16[32,2048]{1,0:T(8,128)(2,1)} %copy-done.1), custom_call_target="tpu_custom_call" | custom-call | tf_op jit(solution)/shard_map/pallas_call | solution.py:62
  382.1 0.0 copy-done
  382.1 4.4 %fusion.refs_0_ = f32[4,256,256]{2,1,0:T(8,128)} fusion(bf16[4,256,2048]{2,1,0:T(8,128)(2,1)} %bitcast.46, bf16[2048,256]{1,0:T(8,128)(2,1)S(1)} %copy-done), kind=kOutput, calls=%fused_computation.5 | convolution fusion | flops 1073741824 | bytes 6291456 | tf_op jit(solution)/shard_map/dot_general | solution.py:499
  386.6 17.2 %shard_map.99 = f32[4,256,256]{2,1,0:T(8,128)} custom-call(f32[4,256,256]{2,1,0:T(8,128)} %fusion.refs_0_), custom_call_target="tpu_custom_call" | custom-call | tf_op jit(solution)/shard_map/pallas_call | solution.py:62
  403.7 2.0 reduce_sum.19
  (2 shorter events, 0.0 us)
Async XLA Ops:
  0.0 382.1 %copy-start = (bf16[2048,256]{1,0:T(8,128)(2,1)S(1)}, bf16[2048,256]{1,0:T(8,128)(2,1)}, u32[]{:S(2)}) copy-start(bf16[2048,256]{1,0:T(8,128)(2,1)} %param.19) | copy-start | bytes 3145732
  243.5 33.7 %copy-start.2 = (bf16[32,32,512]{2,1,0:T(8,128)(2,1)S(1)}, bf16[32,32,512]{2,1,0:T(8,128)(2,1)}, u32[]{:S(2)}) copy-start(bf16[32,32,512]{2,1,0:T(8,128)(2,1)} %get-tuple-element.37) | copy-start | bytes 3145732
  243.5 33.7 %copy-start.3 = (bf16[32,32,512]{2,1,0:T(8,128)(2,1)S(1)}, bf16[32,32,512]{2,1,0:T(8,128)(2,1)}, u32[]{:S(2)}) copy-start(bf16[32,32,512]{2,1,0:T(8,128)(2,1)} %get-tuple-element.42) | copy-start | bytes 3145732
  277.2 2.0 copy-start.4
  277.2 2.0 copy-start.5
  277.2 2.0 copy-start.6
  277.2 2.1 copy-start.7
  285.2 0.7 copy-start.1

commit v11 on v10

--- a/solution.py
+++ b/solution.py
@@ -455,7 +455,17 @@
         return kept_k.T, kept_v, bias.reshape(1, slots * TILE), new_keys[:, cols].T, new_values[:, cols]
 
     head_data = [dense_head(g) for g in range(kv_local)]
-    received = []
+    coef = DH ** (-0.5) * LOG2E
+
+    def combine_piece(parts):
+        part_sum, part_max, part_total = parts
+        top_max = jnp.max(part_max, axis=0)
+        factor = jnp.exp2((part_max - top_max[None]) * coef)
+        denominator = jnp.sum(part_total * factor, axis=0)
+        return combine(part_sum[:, None], factor, denominator)
+
+    attn_pieces = []
+    attn_blocks = []
     previous = None
     for i in range(pieces):
         sends = []
@@ -466,6 +476,9 @@
         if previous is not None:
             sends.extend(previous)
             flags.extend([True, True, True])
+        if i >= 2:
+            sends.append(attn_pieces[i - 2])
+            flags.append(False)
         outs = attention_with_push(
             q_blocks.reshape(total_rows, width),
             *head_data[i * kv_local // pieces],
@@ -481,26 +494,25 @@
         if i + 1 < pieces:
             q_blocks = rest.pop(0)
         if previous is not None:
-            received.append(tuple(rest))
+            got = (rest.pop(0), rest.pop(0), rest.pop(0))
+            attn_pieces.append(combine_piece(got))
+        if i >= 2:
+            attn_blocks.append(rest.pop(0))
         previous = (
             sums_i.reshape(ctx_count, q_dev, width),
             maxima_i.reshape(ctx_count, q_dev, piece_heads),
             totals_i.reshape(ctx_count, q_dev, piece_heads),
         )
-    received.append(push(previous, "ctx", ctx_count, True, 1))
-    part_max = jnp.concatenate([r[1] for r in received], axis=2)
-    part_total = jnp.concatenate([r[2] for r in received], axis=2)
-    part_sum = jnp.stack([r[0] for r in received], axis=1)
-    top_max = jnp.max(part_max, axis=0)
-    factor = jnp.exp2((part_max - top_max[None]) * (DH ** (-0.5) * LOG2E))
-    denominator = jnp.sum(part_total * factor, axis=0)
-    attn_rows = combine(part_sum, factor, denominator)
-    (attn_blocks,) = push((attn_rows,), "ctx", ctx_count, False, 2)
-    projected = jnp.dot(
-        attn_blocks.reshape(total_rows, q_local * DH),
-        out_weight,
-        preferred_element_type=jnp.float32,
-    )
+    attn_pieces.append(combine_piece(push(previous, "ctx", ctx_count, True, 1)))
+    attn_blocks.extend(push(tuple(attn_pieces[pieces - 2 :]), "ctx", ctx_count, False, 2))
+    projected = None
+    for j, blocks in enumerate(attn_blocks):
+        term = jnp.dot(
+            blocks.reshape(total_rows, width),
+            out_weight[j * width : (j + 1) * width],
+            preferred_element_type=jnp.float32,
+        )
+        projected = term if projected is None else projected + term
     out_rows = total_rows // tp_count
     (proj_parts,) = push(
         (projected.reshape(tp_count, out_rows, projected.shape[1]),), "tp", tp_count, True, 3

time: 406 us -> 373 us (0.919); the launches traced: 406 us -> 367 us
  Pallas kernels: 364 us -> 323 us
    pallas_call x4, Pallas kernels: 166 us -> 103 us  [push(): pl.pallas_call(functools.partial(push_kernel, axis, n, per_dest, count),...]
    pallas_call x4, Pallas kernels: 193 us -> 208 us  [attention_with_push(): pl.pallas_call(functools.partial(attn_push_kernel, n, group_size, per_des...]
    pallas_call x1 -> x4, Pallas kernels: 5.4 us -> 11.9 us  [combine(): pl.pallas_call(functools.partial(combine_kernel, heads), out_shape=jax.Sh...]
where the time goes in v11:
time: 373 us; the launch traced here: 367 us
  Pallas kernels  323 us (87%)
  local copies, waits for them, and re-layouts  21.8 us (6%)
  other arithmetic  16.9 us (5%)
  matrix products  4.75 us (1%)
    pallas_call x4, Pallas kernels, attention_with_push(): pl.pallas_call(functools.partial(attn_push_kernel, n, group_size, per_des...  208 us
    pallas_call x4, Pallas kernels, push(): pl.pallas_call(functools.partial(push_kernel, axis, n, per_dest, count),...  103 us
    pallas_call x4, Pallas kernels, combine(): pl.pallas_call(functools.partial(combine_kernel, heads), out_shape=jax.Sh...  11.9 us

profile of v11, /device:TPU:125, one launch (start us, length us, event | category | flops | bytes accessed | tf_op | source)
XLA Modules:
  0.0 367.3 jit_solution(6785778715069346975)
XLA Ops:
  0.0 0.8 compare_and_fusion
  0.8 1.7 fusion.6
  2.5 1.6 gather_fusion
  4.0 1.7 fusion.5
  5.7 1.6 gather_fusion.1
  7.3 1.6 gather_fusion.2
  8.9 1.5 gather_fusion.3
  10.4 0.0 copy-done.8
  10.4 0.0 copy-done.9
  10.4 3.1 broadcast_select_fusion
  13.6 2.4 copy.20
  15.9 0.0 copy-done.21
  15.9 0.6 dynamic_slice.3
  17.2 0.5 iota_add_fusion.1.refs_7_
  17.7 0.0 copy-done.17
  17.7 0.6 fusion.7
  18.3 20.4 %shard_map.91 = bf16[32,32,512]{2,1,0:T(8,128)(2,1)} custom-call(bf16[32,512]{1,0:T(8,128)(2,1)} %get-tuple-element.86.refs_0_), custom_call_target="tpu_custom_call" | custom-call | tf_op jit(solution)/shard_map/pallas_call | solution.py:62
  38.8 0.1 iota_add_fusion
  38.9 1.4 add.80.refs_6_
  40.3 0.0 copy-done.18
  40.3 0.7 copy.22
  41.0 0.0 copy-done.19
  41.0 0.6 fusion.8
  41.6 0.7 fusion.10
  42.2 1.3 compare_select_fusion.1.refs_3_
  43.5 44.5 %shard_map.92 = (bf16[1024,512]{1,0:T(8,128)(2,1)}, f32[1024,4]{1,0:T(8,128)}, f32[1024,4]{1,0:T(8,128)}, bf16[32,32,512]{2,1,0:T(8,128)(2,1)}) custom-call(bf16[1024,512]{1,0:T(8,128)(2,1)} %bitcast.63, bf16[128,3072]{1,0:T(8,128)(2,1)} %bitcast.67, bf16[3072,128]{1,0:T(8,128)(2,1)} %bitcast.73, f32[1,3072]{1,0:T(1,128)} %compare_select_fusion.1.refs_3_, ...), custom_call_target="tpu_custom_call" | custom-call | flops 6509559808 | bytes 3670016 | tf_op jit(solution)/shard_map/pallas_call | solution.py:342
  88.1 50.6 %shard_map.93 = (bf16[1024,512]{1,0:T(8,128)(2,1)}, f32[1024,4]{1,0:T(8,128)}, f32[1024,4]{1,0:T(8,128)}, bf16[32,32,512]{2,1,0:T(8,128)(2,1)}, bf16[32,32,512]{...) custom-call(bf16[1024,512]{1,0:T(8,128)(2,1)} %bitcast.86, bf16[128,3072]{1,0:T(8,128)(2,1)} %bitcast.68, ...), custom_call_target="tpu_custom_call" | custom-call | flops 6509559808 | bytes 3670016 | tf_op jit(solution)/shard_map/pallas_call | solution.py:342
  138.7 1.2 reduce_max.36
  139.8 1.3 multiply_reduce_fusion.3
  141.2 3.0 shard_map.94.refs_12_
  144.2 0.0 copy-start.6
  144.2 0.6 copy-done.6
  144.8 1.2 copy.21
  146.0 0.7 copy.23
  146.7 1.3 compare_select_fusion.refs_3_
  148.0 57.6 %shard_map.95 = (bf16[1024,512]{1,0:T(8,128)(2,1)}, f32[1024,4]{1,0:T(8,128)}, f32[1024,4]{1,0:T(8,128)}, bf16[32,32,512]{2,1,0:T(8,128)(2,1)}, bf16[32,32,512]{...) custom-call(bf16[1024,512]{1,0:T(8,128)(2,1)} %bitcast.82, ...), custom_call_target="tpu_custom_call" | custom-call | flops 6509559808 | bytes 3670016 | tf_op jit(solution)/shard_map/pallas_call | solution.py:342
  205.5 1.2 reduce_max.37
  206.7 1.3 multiply_reduce_fusion.2
  208.1 3.0 shard_map.96.refs_11_
  211.1 0.0 copy-start.7
  211.1 0.6 copy-done.7
  211.7 55.4 %shard_map.97 = (bf16[1024,512]{1,0:T(8,128)(2,1)}, f32[1024,4]{1,0:T(8,128)}, f32[1024,4]{1,0:T(8,128)}, bf16[32,32,512]{2,1,0:T(8,128)(2,1)}, f32[32,32,4]{2,1...) custom-call(bf16[1024,512]{1,0:T(8,128)(2,1)} %bitcast.84, bf16[128,3072]{1,0:T(8,128)(2,1)} %bitcast.70, ...), custom_call_target="tpu_custom_call" | custom-call | flops 6509559808 | bytes 3670016 | tf_op jit(solution)/shard_map/pallas_call | solution.py:342
  267.1 32.9 %shard_map.99 = (bf16[32,32,512]{2,1,0:T(8,128)(2,1)}, f32[32,32,4]{2,1,0:T(8,128)}, f32[32,32,4]{2,1,0:T(8,128)}) custom-call(bf16[32,32,512]{2,1,0:T(8,128)(2,1)} %bitcast.64, f32[32,32,4]{2,1,0:T(8,128)} %bitcast.75, f32[32,32,4]{2,1,0:T(8,128)} %bitcast.76), custom_call_target="tpu_custom_call" | custom-call | tf_op jit(solution)/shard_map/pallas_call | solution.py:62
  300.1 1.2 reduce_max.39
  301.3 1.3 multiply_reduce_fusion
  302.7 3.0 shard_map.100.refs_1_
  305.7 0.6 copy-done.4
  306.3 0.1 reduce_max.38
  306.3 0.0 copy-done.16
  306.3 0.1 multiply_reduce_fusion.1
  306.5 3.0 shard_map.98.refs_0_
  309.5 0.0 copy-start.5
  309.5 0.6 copy-done.5
  310.1 30.5 %shard_map.101 = (bf16[32,32,512]{2,1,0:T(8,128)(2,1)}, bf16[32,32,512]{2,1,0:T(8,128)(2,1)}) custom-call(bf16[32,512]{1,0:T(8,128)(2,1)} %copy-done.5, bf16[32,512]{1,0:T(8,128)(2,1)} %copy-done.4), custom_call_target="tpu_custom_call" | custom-call | tf_op jit(solution)/shard_map/pallas_call | solution.py:62
  340.6 1.4 fusion.3
  342.0 0.0 copy-start.15
  342.0 1.5 convolution_add_fusion.2
  343.6 0.0 copy-done.14
  343.6 0.1 copy-done.15
  343.6 0.4 convolution_add_fusion.1
  344.1 0.8 copy-done.13
  344.9 1.4 convolution_add_fusion
  346.3 19.0 %shard_map.102 = f32[4,256,256]{2,1,0:T(8,128)} custom-call(f32[4,256,256]{2,1,0:T(8,128)} %bitcast.54), custom_call_target="tpu_custom_call" | custom-call | tf_op jit(solution)/shard_map/pallas_call | solution.py:62
  365.3 2.0 reduce_sum.49
  (30 shorter events, 0.1 us)
Async XLA Ops:
  7.3 3.1 copy-start.8
  8.9 1.6 copy-start.9
  10.4 5.5 %copy-start.21 = (s32[32]{0:T(128)S(1)}, s32[32]{0:T(128)}, u32[]{:S(2)}) copy-start(s32[32]{0:T(128)} %param.18) | copy-start | bytes 388
  10.4 7.3 %copy-start.17 = (bf16[32,2048]{1,0:T(8,128)(2,1)S(1)}, bf16[32,2048]{1,0:T(8,128)(2,1)}, u32[]{:S(2)}) copy-start(bf16[32,2048]{1,0:T(8,128)(2,1)} %param.11) | copy-start | bytes 393220
  13.5 26.7 %copy-start.18 = (bf16[32,256]{1,0:T(8,128)(2,1)S(1)}, bf16[32,256]{1,0:T(8,128)(2,1)}, u32[]{:S(2)}) copy-start(bf16[32,256]{1,0:T(8,128)(2,1)} %param.12) | copy-start | bytes 49156
  13.6 27.4 %copy-start.19 = (bf16[32,256]{1,0:T(8,128)(2,1)S(1)}, bf16[32,256]{1,0:T(8,128)(2,1)}, u32[]{:S(2)}) copy-start(bf16[32,256]{1,0:T(8,128)(2,1)} %param.13) | copy-start | bytes 49156
  13.6 28.0 %copy-start.20 = (s32[1,2]{1,0:T(1,128)S(1)}, s32[1,2]{1,0:T(1,128)}, u32[]{:S(2)}) copy-start(s32[1,2]{1,0:T(1,128)} %param.17) | copy-start | bytes 28
  138.7 2.5 copy-start.1
  144.2 0.6 copy-start.6
  205.5 2.5 copy-start.2
  211.1 0.6 copy-start.7
  300.0 2.6 copy-start.3
  300.0 6.2 %copy-start.10 = (f32[32,32,4]{2,1,0:T(8,128)S(1)}, f32[32,32,4]{2,1,0:T(8,128)}, u32[]{:S(2)}) copy-start(f32[32,32,4]{2,1,0:T(8,128)} %get-tuple-element.58) | copy-start | bytes 49156
  300.0 6.3 %copy-start.16 = (f32[32,32,4]{2,1,0:T(8,128)S(1)}, f32[32,32,4]{2,1,0:T(8,128)}, u32[]{:S(2)}) copy-start(f32[32,32,4]{2,1,0:T(8,128)} %get-tuple-element.59) | copy-start | bytes 49156
  302.6 3.8 %copy-start = (bf16[32,32,512]{2,1,0:T(8,128)(2,1)S(1)}, bf16[32,32,512]{2,1,0:T(8,128)(2,1)}, u32[]{:S(2)}) copy-start(bf16[32,32,512]{2,1,0:T(8,128)(2,1)} %get-tuple-element.57) | copy-start | bytes 3145732
  305.6 0.6 copy-start.4
  306.3 34.4 %copy-start.11 = (bf16[32,32,512]{2,1,0:T(8,128)(2,1)S(1)}, bf16[32,32,512]{2,1,0:T(8,128)(2,1)}, u32[]{:S(2)}) copy-start(bf16[32,32,512]{2,1,0:T(8,128)(2,1)} %get-tuple-element.48) | copy-start | bytes 3145732
  306.5 35.6 %copy-start.12 = (bf16[32,32,512]{2,1,0:T(8,128)(2,1)S(1)}, bf16[32,32,512]{2,1,0:T(8,128)(2,1)}, u32[]{:S(2)}) copy-start(bf16[32,32,512]{2,1,0:T(8,128)(2,1)} %get-tuple-element.56) | copy-start | bytes 3145732
  309.5 0.6 copy-start.5
  342.0 1.6 copy-start.14
  342.0 1.6 copy-start.15
  343.6 1.2 copy-start.13

commit v12 on v11

--- a/solution.py
+++ b/solution.py
@@ -75,6 +75,7 @@
 
 TPB = 8
 LOG2E = 1.4426950408889634
+SPLITS = (2, 3, 3, 3, 3, 2)
 
 
 def dot_nt(a, b):
@@ -434,10 +435,10 @@
     total_rows = q_dev * ctx_count
     my_index = lax.axis_index("ctx")
     key_place = owner_slot[my_index] * q_dev + jnp.arange(q_dev, dtype=jnp.int32)
-    pieces = 4
-    piece_heads = q_local // pieces
-    width = piece_heads * DH
-    (q_blocks,) = push((queries[:, :width],), "ctx", ctx_count, False, 0)
+    splits = SPLITS
+    pieces = len(splits)
+    offsets = [sum(splits[:i]) * DH for i in range(pieces + 1)]
+    (q_blocks,) = push((queries[:, : offsets[1]],), "ctx", ctx_count, False, 0)
     query_place = (
         owner_slot[:, None] * q_dev + jnp.arange(q_dev, dtype=jnp.int32)[None, :]
     ).reshape(total_rows, 1)
@@ -471,7 +472,7 @@
         sends = []
         flags = []
         if i + 1 < pieces:
-            sends.append(queries[:, (i + 1) * width : (i + 2) * width])
+            sends.append(queries[:, offsets[i + 1] : offsets[i + 2]])
             flags.append(False)
         if previous is not None:
             sends.extend(previous)
@@ -479,9 +480,10 @@
         if i >= 2:
             sends.append(attn_pieces[i - 2])
             flags.append(False)
+        width = offsets[i + 1] - offsets[i]
         outs = attention_with_push(
             q_blocks.reshape(total_rows, width),
-            *head_data[i * kv_local // pieces],
+            *head_data[offsets[i] // DH // group_size],
             query_place,
             key_place,
             tuple(sends),
@@ -500,16 +502,16 @@
             attn_blocks.append(rest.pop(0))
         previous = (
             sums_i.reshape(ctx_count, q_dev, width),
-            maxima_i.reshape(ctx_count, q_dev, piece_heads),
-            totals_i.reshape(ctx_count, q_dev, piece_heads),
+            maxima_i.reshape(ctx_count, q_dev, splits[i]),
+            totals_i.reshape(ctx_count, q_dev, splits[i]),
         )
     attn_pieces.append(combine_piece(push(previous, "ctx", ctx_count, True, 1)))
     attn_blocks.extend(push(tuple(attn_pieces[pieces - 2 :]), "ctx", ctx_count, False, 2))
     projected = None
     for j, blocks in enumerate(attn_blocks):
         term = jnp.dot(
-            blocks.reshape(total_rows, width),
-            out_weight[j * width : (j + 1) * width],
+            blocks.reshape(total_rows, offsets[j + 1] - offsets[j]),
+            out_weight[offsets[j] : offsets[j + 1]],
             preferred_element_type=jnp.float32,
         )
         projected = term if projected is None else projected + term

time: 373 us -> 410 us (1.099)
  Pallas kernels: 323 us -> 351 us
  other arithmetic: 16.9 us -> 21.8 us
    pallas_call x4 -> x6, Pallas kernels: 208 us -> 256 us  [attention_with_push(): pl.pallas_call(functools.partial(attn_push_kernel, n, group_size, per_des...]
    pallas_call x4, Pallas kernels: 103 us -> 79.2 us  [push(): pl.pallas_call(functools.partial(push_kernel, axis, n, per_dest, count),...]
    pallas_call x4 -> x6, Pallas kernels: 11.9 us -> 16.4 us  [combine(): pl.pallas_call(functools.partial(combine_kernel, heads), out_shape=jax.Sh...]
where the time goes in v12:
time: 410 us; the launch traced here: 404 us
  Pallas kernels  351 us (86%)
  local copies, waits for them, and re-layouts  24.6 us (6%)
  other arithmetic  21.8 us (5%)
  matrix products  4.37 us (1%)
    pallas_call x6, Pallas kernels, attention_with_push(): pl.pallas_call(functools.partial(attn_push_kernel, n, group_size, per_des...  256 us
    pallas_call x4, Pallas kernels, push(): pl.pallas_call(functools.partial(push_kernel, axis, n, per_dest, count),...  79.2 us
    pallas_call x6, Pallas kernels, combine(): pl.pallas_call(functools.partial(combine_kernel, heads), out_shape=jax.Sh...  16.4 us

profile of v12, /device:TPU:125, one launch (start us, length us, event | category | flops | bytes accessed | tf_op | source)
XLA Modules:
  0.0 403.7 jit_solution(5650330301250498591)
XLA Ops:
  0.0 0.8 compare_and_fusion
  0.8 1.7 fusion.8
  2.5 1.6 gather_fusion
  4.0 1.7 fusion.7
  5.7 1.6 gather_fusion.1
  7.3 1.6 gather_fusion.2
  8.9 1.5 gather_fusion.3
  10.4 3.1 broadcast_select_fusion
  13.6 2.4 copy.22
  15.9 0.6 dynamic_slice.3
  17.1 0.6 iota_add_fusion.1.refs_7_
  17.8 1.4 add.88.refs_6_
  19.2 0.6 fusion.10
  19.8 0.7 copy.24
  20.5 0.6 fusion.11
  21.2 0.6 fusion.13
  21.8 1.2 compare_select_fusion.1.refs_3_
  23.0 0.6 fusion.9
  23.6 13.1 %shard_map.91 = bf16[32,32,256]{2,1,0:T(8,128)(2,1)} custom-call(bf16[32,256]{1,0:T(8,128)(2,1)} %get-tuple-element.121.refs_0_), custom_call_target="tpu_custom_call" | custom-call | tf_op jit(solution)/shard_map/pallas_call | solution.py:62
  36.7 26.0 %shard_map.92 = (bf16[1024,256]{1,0:T(8,128)(2,1)}, f32[1024,2]{1,0:T(8,128)}, f32[1024,2]{1,0:T(8,128)}, bf16[32,32,384]{2,1,0:T(8,128)(2,1)}) custom-call(bf16[1024,256]{1,0:T(8,128)(2,1)} %bitcast.97, bf16[128,3072]{1,0:T(8,128)(2,1)} %bitcast.77, bf16[3072,128]{1,0:T(8,128)(2,1)} %bitcast.90, f32[1,3072]{1,0:T(1,128)} %compare_select_fusion.1.refs_3_, ...), custom_call_target="tpu_custom_call" | custom-call | flops 3254779904 | bytes 2621440 | tf_op jit(solution)/shard_map/pallas_call | solution.py:343
  62.7 40.8 %shard_map.93 = (bf16[1024,384]{1,0:T(8,128)(2,1)}, f32[1024,3]{1,0:T(8,128)}, f32[1024,3]{1,0:T(8,128)}, bf16[32,32,384]{2,1,0:T(8,128)(2,1)}, bf16[32,32,256]{...) custom-call(bf16[1024,384]{1,0:T(8,128)(2,1)} %bitcast.112, bf16[128,3072]{1,0:T(8,128)(2,1)} %bitcast.78, ...), custom_call_target="tpu_custom_call" | custom-call | flops 4882169856 | bytes 3145728 | tf_op jit(solution)/shard_map/pallas_call | solution.py:343
  103.5 1.2 reduce_max.54
  104.7 1.3 multiply_reduce_fusion.5
  106.0 2.5 shard_map.94.refs_12_
  108.6 0.6 copy-done.11
  109.1 46.7 %shard_map.95 = (bf16[1024,384]{1,0:T(8,128)(2,1)}, f32[1024,3]{1,0:T(8,128)}, f32[1024,3]{1,0:T(8,128)}, bf16[32,32,384]{2,1,0:T(8,128)(2,1)}, bf16[32,32,384]{...) custom-call(bf16[1024,384]{1,0:T(8,128)(2,1)} %bitcast.109, ...), custom_call_target="tpu_custom_call" | custom-call | flops 4882169856 | bytes 3145728 | tf_op jit(solution)/shard_map/pallas_call | solution.py:343
  155.8 1.2 reduce_max.55
  157.0 1.3 multiply_reduce_fusion.4
  158.3 2.8 shard_map.96.refs_12_
  161.2 0.6 copy-done.8
  161.8 1.1 copy.23
  162.9 0.7 copy.25
  163.7 1.2 compare_select_fusion.refs_3_
  164.9 50.7 %shard_map.97 = (bf16[1024,384]{1,0:T(8,128)(2,1)}, f32[1024,3]{1,0:T(8,128)}, f32[1024,3]{1,0:T(8,128)}, bf16[32,32,384]{2,1,0:T(8,128)(2,1)}, bf16[32,32,384]{...) custom-call(bf16[1024,384]{1,0:T(8,128)(2,1)} %bitcast.106, ...), custom_call_target="tpu_custom_call" | custom-call | flops 4882169856 | bytes 3145728 | tf_op jit(solution)/shard_map/pallas_call | solution.py:343
  215.7 1.2 reduce_max.56
  216.8 1.3 multiply_reduce_fusion.3
  218.2 2.8 shard_map.98.refs_12_
  221.0 0.6 copy-done.10
  221.6 47.8 %shard_map.99 = (bf16[1024,384]{1,0:T(8,128)(2,1)}, f32[1024,3]{1,0:T(8,128)}, f32[1024,3]{1,0:T(8,128)}, bf16[32,32,256]{2,1,0:T(8,128)(2,1)}, bf16[32,32,384]{...) custom-call(bf16[1024,384]{1,0:T(8,128)(2,1)} %bitcast.111, ...), custom_call_target="tpu_custom_call" | custom-call | flops 4882169856 | bytes 3145728 | tf_op jit(solution)/shard_map/pallas_call | solution.py:343
  269.5 1.2 reduce_max.57
  270.7 1.3 multiply_reduce_fusion.2
  272.0 2.8 shard_map.100.refs_11_
  274.9 0.6 copy-done.9
  275.4 43.8 %shard_map.101 = (bf16[1024,256]{1,0:T(8,128)(2,1)}, f32[1024,2]{1,0:T(8,128)}, f32[1024,2]{1,0:T(8,128)}, bf16[32,32,384]{2,1,0:T(8,128)(2,1)}, f32[32,32,3]{2,...) custom-call(bf16[1024,256]{1,0:T(8,128)(2,1)} %bitcast.117, bf16[128,3072]{1,0:T(8,128)(2,1)} %bitcast.82, ...), custom_call_target="tpu_custom_call" | custom-call | flops 3254779904 | bytes 2621440 | tf_op jit(solution)/shard_map/pallas_call | solution.py:343
  319.2 25.3 %shard_map.103 = (bf16[32,32,256]{2,1,0:T(8,128)(2,1)}, f32[32,32,2]{2,1,0:T(8,128)}, f32[32,32,2]{2,1,0:T(8,128)}) custom-call(bf16[32,32,256]{2,1,0:T(8,128)(2,1)} %bitcast.93, f32[32,32,2]{2,1,0:T(8,128)} %bitcast.94, f32[32,32,2]{2,1,0:T(8,128)} %bitcast.95), custom_call_target="tpu_custom_call" | custom-call | tf_op jit(solution)/shard_map/pallas_call | solution.py:62
  344.5 1.2 reduce_max.59
  345.7 1.4 multiply_reduce_fusion
  347.2 2.5 shard_map.104.refs_1_
  349.7 0.6 copy-done.7
  350.4 0.1 multiply_reduce_fusion.1
  350.5 2.8 shard_map.102.refs_0_
  353.4 0.6 copy-done.6
  354.0 23.4 %shard_map.105 = (bf16[32,32,384]{2,1,0:T(8,128)(2,1)}, bf16[32,32,256]{2,1,0:T(8,128)(2,1)}) custom-call(bf16[32,384]{1,0:T(8,128)(2,1)} %copy-done.6, bf16[32,256]{1,0:T(8,128)(2,1)} %copy-done.7), custom_call_target="tpu_custom_call" | custom-call | tf_op jit(solution)/shard_map/pallas_call | solution.py:62
  377.4 1.4 fusion.5
  378.8 0.4 convolution_add_fusion.4
  379.3 0.4 convolution_add_fusion.3
  379.7 0.7 copy-done.18
  380.4 0.4 convolution_add_fusion.2
  380.8 0.7 copy-done.19
  381.5 0.4 convolution_add_fusion.1
  382.0 0.6 copy-done.21
  382.6 1.3 convolution_add_fusion
  383.8 17.5 %shard_map.106 = f32[4,256,256]{2,1,0:T(8,128)} custom-call(f32[4,256,256]{2,1,0:T(8,128)} %bitcast.70), custom_call_target="tpu_custom_call" | custom-call | tf_op jit(solution)/shard_map/pallas_call | solution.py:62
  401.4 2.0 reduce_sum.69
  (51 shorter events, 0.2 us)
Async XLA Ops:
  7.3 3.1 copy-start.12
  8.9 1.5 copy-start.13
  10.4 5.5 %copy-start.26 = (s32[32]{0:T(128)S(1)}, s32[32]{0:T(128)}, u32[]{:S(2)}) copy-start(s32[32]{0:T(128)} %param.18) | copy-start | bytes 388
  13.5 5.6 %copy-start.22 = (bf16[32,2048]{1,0:T(8,128)(2,1)S(1)}, bf16[32,2048]{1,0:T(8,128)(2,1)}, u32[]{:S(2)}) copy-start(bf16[32,2048]{1,0:T(8,128)(2,1)} %param.11) | copy-start | bytes 393220
  13.5 6.3 %copy-start.23 = (bf16[32,256]{1,0:T(8,128)(2,1)S(1)}, bf16[32,256]{1,0:T(8,128)(2,1)}, u32[]{:S(2)}) copy-start(bf16[32,256]{1,0:T(8,128)(2,1)} %param.12) | copy-start | bytes 49156
  13.5 7.0 %copy-start.24 = (bf16[32,256]{1,0:T(8,128)(2,1)S(1)}, bf16[32,256]{1,0:T(8,128)(2,1)}, u32[]{:S(2)}) copy-start(bf16[32,256]{1,0:T(8,128)(2,1)} %param.13) | copy-start | bytes 49156
  13.5 7.6 %copy-start.25 = (s32[1,2]{1,0:T(1,128)S(1)}, s32[1,2]{1,0:T(1,128)}, u32[]{:S(2)}) copy-start(s32[1,2]{1,0:T(1,128)} %param.17) | copy-start | bytes 28
  103.5 2.5 copy-start.4
  108.5 0.6 copy-start.11
  155.8 2.5 copy-start.1
  161.2 0.6 copy-start.8
  215.7 2.5 copy-start.2
  221.0 0.6 copy-start.10
  269.5 2.5 copy-start.3
  274.8 0.6 copy-start.9
  319.2 31.1 %copy-start.14 = (f32[32,32,3]{2,1,0:T(8,128)S(1)}, f32[32,32,3]{2,1,0:T(8,128)}, u32[]{:S(2)}) copy-start(f32[32,32,3]{2,1,0:T(8,128)} %get-tuple-element.90) | copy-start | bytes 36868
  344.5 2.6 copy-start.5
  344.5 5.8 %copy-start.20 = (f32[32,32,3]{2,1,0:T(8,128)S(1)}, f32[32,32,3]{2,1,0:T(8,128)}, u32[]{:S(2)}) copy-start(f32[32,32,3]{2,1,0:T(8,128)} %get-tuple-element.91) | copy-start | bytes 36868
  345.7 4.8 %copy-start = (bf16[32,32,384]{2,1,0:T(8,128)(2,1)S(1)}, bf16[32,32,384]{2,1,0:T(8,128)(2,1)}, u32[]{:S(2)}) copy-start(bf16[32,32,384]{2,1,0:T(8,128)(2,1)} %get-tuple-element.89) | copy-start | bytes 2359300
  347.2 30.2 %copy-start.15 = (bf16[2048,256]{1,0:T(8,128)(2,1)S(1)}, bf16[2048,256]{1,0:T(8,128)(2,1)}, u32[]{:S(2)}) copy-start(bf16[2048,256]{1,0:T(8,128)(2,1)} %param.19) | copy-start | bytes 3145732
  349.7 0.6 copy-start.7
  350.5 28.3 %copy-start.16 = (bf16[32,32,384]{2,1,0:T(8,128)(2,1)S(1)}, bf16[32,32,384]{2,1,0:T(8,128)(2,1)}, u32[]{:S(2)}) copy-start(bf16[32,32,384]{2,1,0:T(8,128)(2,1)} %get-tuple-element.72) | copy-start | bytes 2359300
  353.4 0.6 copy-start.6
  377.4 1.9 copy-start.17
  379.3 1.1 copy-start.18
  380.4 1.1 copy-start.19
  381.5 1.0 copy-start.21

commit v13 on v11

--- a/solution.py
+++ b/solution.py
@@ -29,7 +29,7 @@
     for a in range(count):
         for k in range(1, n):
             peer = lax.rem(me + k, n)
-            src = x_refs[a].at[peer] if per_dest else x_refs[a]
+            src = x_refs[a].at[peer] if per_dest[a] else x_refs[a]
             copy = pltpu.make_async_remote_copy(
                 src_ref=src,
                 dst_ref=y_refs[a].at[me],
@@ -42,7 +42,7 @@
             copies.append(copy)
     locals_ = []
     for a in range(count):
-        src = x_refs[a].at[me] if per_dest else x_refs[a]
+        src = x_refs[a].at[me] if per_dest[a] else x_refs[a]
         local = pltpu.make_async_copy(src, y_refs[a].at[me], local_sem.at[a])
         local.start()
         locals_.append(local)
@@ -54,9 +54,11 @@
 
 def push(xs, axis, n, per_dest, collective_id):
     count = len(xs)
+    if isinstance(per_dest, bool):
+        per_dest = (per_dest,) * count
     out_shape = []
-    for x in xs:
-        block = x.shape[1:] if per_dest else x.shape
+    for x, d in zip(xs, per_dest):
+        block = x.shape[1:] if d else x.shape
         out_shape.append(jax.ShapeDtypeStruct((n,) + tuple(block), x.dtype))
     any_spec = pl.BlockSpec(memory_space=pl.ANY)
     return pl.pallas_call(
@@ -503,8 +505,12 @@
             maxima_i.reshape(ctx_count, q_dev, piece_heads),
             totals_i.reshape(ctx_count, q_dev, piece_heads),
         )
-    attn_pieces.append(combine_piece(push(previous, "ctx", ctx_count, True, 1)))
-    attn_blocks.extend(push(tuple(attn_pieces[pieces - 2 :]), "ctx", ctx_count, False, 2))
+    last_parts = push(
+        previous + (attn_pieces[pieces - 2],), "ctx", ctx_count, (True, True, True, False), 1
+    )
+    attn_blocks.append(last_parts[3])
+    attn_pieces.append(combine_piece(last_parts[:3]))
+    attn_blocks.extend(push((attn_pieces[pieces - 1],), "ctx", ctx_count, False, 2))
     projected = None
     for j, blocks in enumerate(attn_blocks):
         term = jnp.dot(

time: 373 us -> 375 us (level)
  no operation moved by 1% of the time
where the time goes in v13:
time: 375 us; the launch traced here: 369 us
  Pallas kernels  323 us (86%)
  local copies, waits for them, and re-layouts  22.5 us (6%)
  other arithmetic  19.3 us (5%)
    pallas_call x4, Pallas kernels, attention_with_push(): pl.pallas_call(functools.partial(attn_push_kernel, n, group_size, per_des...  208 us
    pallas_call x4, Pallas kernels, push(): pl.pallas_call(functools.partial(push_kernel, axis, n, per_dest, count),...  103 us
    pallas_call x4, Pallas kernels, combine(): pl.pallas_call(functools.partial(combine_kernel, heads), out_shape=jax.Sh...  11.9 us

profile of v13, /device:TPU:125, one launch (start us, length us, event | category | flops | bytes accessed | tf_op | source)
XLA Modules:
  0.0 368.9 jit_solution(6442270919176051217)
XLA Ops:
  0.0 0.8 compare_and_fusion
  0.8 1.7 fusion.6
  2.5 1.6 gather_fusion
  4.0 1.7 fusion.5
  5.7 1.6 gather_fusion.1
  7.3 1.6 gather_fusion.2
  8.9 1.5 gather_fusion.3
  10.4 0.0 copy-done.9
  10.4 0.0 copy-done.10
  10.4 3.1 broadcast_select_fusion
  13.6 2.4 copy.20
  15.9 0.0 copy-done.19
  15.9 0.6 dynamic_slice.3
  17.2 0.5 iota_add_fusion.1.refs_7_
  17.7 0.0 copy-done.15
  17.7 0.7 fusion.7
  18.4 20.4 %shard_map.91 = bf16[32,32,512]{2,1,0:T(8,128)(2,1)} custom-call(bf16[32,512]{1,0:T(8,128)(2,1)} %get-tuple-element.84.refs_0_), custom_call_target="tpu_custom_call" | custom-call | tf_op jit(solution)/shard_map/pallas_call | solution.py:64
  38.8 0.1 iota_add_fusion
  38.9 1.4 add.80.refs_6_
  40.3 0.0 copy-done.16
  40.3 0.7 copy.22
  41.0 0.0 copy-done.17
  41.0 0.6 fusion.8
  41.6 0.6 fusion.10
  42.3 1.3 compare_select_fusion.1.refs_3_
  43.6 44.5 %shard_map.92 = (bf16[1024,512]{1,0:T(8,128)(2,1)}, f32[1024,4]{1,0:T(8,128)}, f32[1024,4]{1,0:T(8,128)}, bf16[32,32,512]{2,1,0:T(8,128)(2,1)}) custom-call(bf16[1024,512]{1,0:T(8,128)(2,1)} %bitcast.66, bf16[128,3072]{1,0:T(8,128)(2,1)} %bitcast.67, bf16[3072,128]{1,0:T(8,128)(2,1)} %bitcast.73, f32[1,3072]{1,0:T(1,128)} %compare_select_fusion.1.refs_3_, ...), custom_call_target="tpu_custom_call" | custom-call | flops 6509559808 | bytes 3670016 | tf_op jit(solution)/shard_map/pallas_call | solution.py:344
  88.1 50.6 %shard_map.93 = (bf16[1024,512]{1,0:T(8,128)(2,1)}, f32[1024,4]{1,0:T(8,128)}, f32[1024,4]{1,0:T(8,128)}, bf16[32,32,512]{2,1,0:T(8,128)(2,1)}, bf16[32,32,512]{...) custom-call(bf16[1024,512]{1,0:T(8,128)(2,1)} %bitcast.86, bf16[128,3072]{1,0:T(8,128)(2,1)} %bitcast.68, ...), custom_call_target="tpu_custom_call" | custom-call | flops 6509559808 | bytes 3670016 | tf_op jit(solution)/shard_map/pallas_call | solution.py:344
  138.7 1.2 reduce_max.36
  139.9 1.3 multiply_reduce_fusion.3
  141.3 3.0 shard_map.94.refs_12_
  144.3 0.6 copy-done.6
  144.8 1.2 copy.21
  146.0 0.7 copy.23
  146.7 1.2 compare_select_fusion.refs_3_
  148.0 57.7 %shard_map.95 = (bf16[1024,512]{1,0:T(8,128)(2,1)}, f32[1024,4]{1,0:T(8,128)}, f32[1024,4]{1,0:T(8,128)}, bf16[32,32,512]{2,1,0:T(8,128)(2,1)}, bf16[32,32,512]{...) custom-call(bf16[1024,512]{1,0:T(8,128)(2,1)} %bitcast.82, ...), custom_call_target="tpu_custom_call" | custom-call | flops 6509559808 | bytes 3670016 | tf_op jit(solution)/shard_map/pallas_call | solution.py:344
  205.7 1.2 reduce_max.37
  206.9 1.3 multiply_reduce_fusion.2
  208.2 3.0 shard_map.96.refs_11_
  211.2 0.0 copy-start.7
  211.2 0.6 copy-done.7
  211.8 55.3 %shard_map.97 = (bf16[1024,512]{1,0:T(8,128)(2,1)}, f32[1024,4]{1,0:T(8,128)}, f32[1024,4]{1,0:T(8,128)}, bf16[32,32,512]{2,1,0:T(8,128)(2,1)}, f32[32,32,4]{2,1...) custom-call(bf16[1024,512]{1,0:T(8,128)(2,1)} %bitcast.84, bf16[128,3072]{1,0:T(8,128)(2,1)} %bitcast.70, ...), custom_call_target="tpu_custom_call" | custom-call | flops 6509559808 | bytes 3670016 | tf_op jit(solution)/shard_map/pallas_call | solution.py:344
  267.2 1.2 reduce_max.38
  268.4 1.3 multiply_reduce_fusion.1
  269.7 0.0 copy-done
  269.7 3.0 shard_map.98.refs_3_
  272.7 0.0 copy-start.4
  272.7 0.6 copy-done.4
  273.3 44.0 %shard_map.99 = (bf16[32,32,512]{2,1,0:T(8,128)(2,1)}, f32[32,32,4]{2,1,0:T(8,128)}, f32[32,32,4]{2,1,0:T(8,128)}, bf16[32,32,512]{2,1,0:T(8,128)(2,1)}) custom-call(bf16[32,32,512]{2,1,0:T(8,128)(2,1)} %bitcast.64, f32[32,32,4]{2,1,0:T(8,128)} %bitcast.75, f32[32,32,4]{2,1,0:T(8,128)} %bitcast.76, bf16[32,512]{1,0:T(8,128)(2,1)} %copy-done.4), custom_call_target="tpu_custom_call" | custom-call | tf_op jit(solution)/shard_map/pallas_call | solution.py:64
  317.3 1.2 reduce_max.39
  318.5 0.0 copy-start.14
  318.5 1.5 multiply_reduce_fusion
  320.0 0.0 copy-done.3
  320.0 3.0 shard_map.100.refs_0_
  323.0 0.0 copy-start.5
  323.0 0.6 copy-done.5
  323.6 20.3 %shard_map.101 = bf16[32,32,512]{2,1,0:T(8,128)(2,1)} custom-call(bf16[32,512]{1,0:T(8,128)(2,1)} %copy-done.5), custom_call_target="tpu_custom_call" | custom-call | tf_op jit(solution)/shard_map/pallas_call | solution.py:64
  344.0 0.4 fusion.3
  344.5 0.4 convolution_add_fusion.2
  344.9 0.8 copy-done.13
  345.7 0.4 convolution_add_fusion.1
  346.1 0.8 copy-done.8
  346.9 1.4 convolution_add_fusion
  348.3 18.6 %shard_map.102 = f32[4,256,256]{2,1,0:T(8,128)} custom-call(f32[4,256,256]{2,1,0:T(8,128)} %bitcast.55), custom_call_target="tpu_custom_call" | custom-call | tf_op jit(solution)/shard_map/pallas_call | solution.py:64
  366.9 2.0 reduce_sum.49
  (26 shorter events, 0.1 us)
Async XLA Ops:
  7.3 3.1 copy-start.9
  8.9 1.6 copy-start.10
  10.4 5.5 %copy-start.19 = (s32[32]{0:T(128)S(1)}, s32[32]{0:T(128)}, u32[]{:S(2)}) copy-start(s32[32]{0:T(128)} %param.18) | copy-start | bytes 388
  10.4 7.3 %copy-start.15 = (bf16[32,2048]{1,0:T(8,128)(2,1)S(1)}, bf16[32,2048]{1,0:T(8,128)(2,1)}, u32[]{:S(2)}) copy-start(bf16[32,2048]{1,0:T(8,128)(2,1)} %param.11) | copy-start | bytes 393220
  13.6 26.7 %copy-start.16 = (bf16[32,256]{1,0:T(8,128)(2,1)S(1)}, bf16[32,256]{1,0:T(8,128)(2,1)}, u32[]{:S(2)}) copy-start(bf16[32,256]{1,0:T(8,128)(2,1)} %param.12) | copy-start | bytes 49156
  13.6 27.5 %copy-start.17 = (bf16[32,256]{1,0:T(8,128)(2,1)S(1)}, bf16[32,256]{1,0:T(8,128)(2,1)}, u32[]{:S(2)}) copy-start(bf16[32,256]{1,0:T(8,128)(2,1)} %param.13) | copy-start | bytes 49156
  13.6 28.1 %copy-start.18 = (s32[1,2]{1,0:T(1,128)S(1)}, s32[1,2]{1,0:T(1,128)}, u32[]{:S(2)}) copy-start(s32[1,2]{1,0:T(1,128)} %param.17) | copy-start | bytes 28
  138.7 2.5 copy-start.1
  144.2 0.6 copy-start.6
  205.7 2.5 copy-start.2
  211.2 0.6 copy-start.7
  267.2 2.5 copy-start
  272.7 0.6 copy-start.4
  317.3 2.7 copy-start.3
  318.5 25.5 %copy-start.11 = (bf16[32,32,512]{2,1,0:T(8,128)(2,1)S(1)}, bf16[32,32,512]{2,1,0:T(8,128)(2,1)}, u32[]{:S(2)}) copy-start(bf16[32,32,512]{2,1,0:T(8,128)(2,1)} %get-tuple-element.47) | copy-start | bytes 3145732
  318.5 25.5 %copy-start.14 = (bf16[2048,256]{1,0:T(8,128)(2,1)S(1)}, bf16[2048,256]{1,0:T(8,128)(2,1)}, u32[]{:S(2)}) copy-start(bf16[2048,256]{1,0:T(8,128)(2,1)} %param.19) | copy-start | bytes 3145732
  323.0 0.6 copy-start.5
  323.6 20.8 %copy-start.12 = (bf16[32,32,512]{2,1,0:T(8,128)(2,1)S(1)}, bf16[32,32,512]{2,1,0:T(8,128)(2,1)}, u32[]{:S(2)}) copy-start(bf16[32,32,512]{2,1,0:T(8,128)(2,1)} %get-tuple-element.55) | copy-start | bytes 3145732
  344.5 1.2 copy-start.13
  345.7 1.2 copy-start.8

commit v14 on v11

--- a/solution.py
+++ b/solution.py
@@ -225,7 +225,9 @@
 def dense_fold(q_ref, h, keys_t, values_ext, mask, m_scr, acc_ref):
     coef = DH ** (-0.5) * LOG2E
     cols = pl.ds(pl.multiple_of(h * DH, DH), DH)
-    s = jnp.dot(q_ref[:, cols], keys_t, preferred_element_type=jnp.float32) + mask
+    s = lax.dot_general(
+        q_ref[:, cols], keys_t, (((1,), (1,)), ((), ())), preferred_element_type=jnp.float32
+    ) + mask
     m_prev = m_scr[h]
     m_new = jnp.maximum(m_prev, s.max(axis=1, keepdims=True))
     alpha = jnp.exp2((m_prev - m_new) * coef)
@@ -323,7 +325,7 @@
 def attention_with_push(query_rows, keys_t, values, bias, new_keys_t, new_values, query_place, key_place, sends, n, per_dest, collective_id):
     rows, width = query_rows.shape
     group_size = width // DH
-    total_keys = keys_t.shape[1]
+    total_keys = keys_t.shape[0]
     step_keys = TPB * TILE
     steps = total_keys // step_keys
     q_new = new_values.shape[0]
@@ -344,10 +346,10 @@
         grid=(steps,),
         in_specs=[
             pl.BlockSpec((rows, width), lambda t: (0, 0)),
-            pl.BlockSpec((DH, step_keys), lambda t: (0, t)),
+            pl.BlockSpec((step_keys, DH), lambda t: (t, 0)),
             pl.BlockSpec((step_keys, DH), lambda t: (t, 0)),
             pl.BlockSpec((1, step_keys), lambda t: (0, t)),
-            pl.BlockSpec((DH, q_new), lambda t: (0, 0)),
+            pl.BlockSpec((q_new, DH), lambda t: (0, 0)),
             pl.BlockSpec((q_new, DH), lambda t: (0, 0)),
             pl.BlockSpec((rows, 1), lambda t: (0, 0)),
             pl.BlockSpec((1, q_new), lambda t: (0, 0)),
@@ -452,7 +454,7 @@
         kept_k = jnp.take(tiles_k, keep_tiles[0, g], axis=0).reshape(slots * TILE, DH)
         kept_v = jnp.take(tiles_v, keep_tiles[0, g], axis=0).reshape(slots * TILE, DH)
         bias = jnp.where(slot_ids < tile_count[0, g], 0.0, NEG_INF).astype(jnp.float32)
-        return kept_k.T, kept_v, bias.reshape(1, slots * TILE), new_keys[:, cols].T, new_values[:, cols]
+        return kept_k, kept_v, bias.reshape(1, slots * TILE), new_keys[:, cols], new_values[:, cols]
 
     head_data = [dense_head(g) for g in range(kv_local)]
     coef = DH ** (-0.5) * LOG2E

time: 373 us -> 386 us (1.035)
  the two profiles are of different devices: /device:TPU:125 before, /device:TPU:1 now
where the time goes in v14:
time: 386 us; the launch traced here: 380 us
  Pallas kernels  339 us (88%)
  other arithmetic  17.2 us (4%)
  local copies, waits for them, and re-layouts  16.8 us (4%)
  matrix products  5.06 us (1%)
    pallas_call x4, Pallas kernels, attention_with_push(): pl.pallas_call(functools.partial(attn_push_kernel, n, group_size, per_des...  220 us
    pallas_call x4, Pallas kernels, push(): pl.pallas_call(functools.partial(push_kernel, axis, n, per_dest, count),...  107 us
    pallas_call x4, Pallas kernels, combine(): pl.pallas_call(functools.partial(combine_kernel, heads), out_shape=jax.Sh...  12.2 us

profile of v14, /device:TPU:1, one launch (start us, length us, event | category | flops | bytes accessed | tf_op | source)
XLA Modules:
  0.0 379.5 jit_solution(17184654002025866024)
XLA Ops:
  0.0 0.8 compare_and_fusion
  0.8 1.7 fusion.6
  2.5 1.6 gather_fusion
  4.0 1.7 fusion.5
  5.7 1.6 gather_fusion.1
  7.3 1.6 gather_fusion.2
  8.9 1.6 gather_fusion.3
  10.4 0.0 copy-done.8
  10.4 0.0 copy-done.9
  10.4 0.0 copy-start.18
  10.5 0.0 copy-start.16
  10.5 0.0 copy-start.19
  10.5 3.4 broadcast_select_fusion
  13.9 0.0 copy-done.20
  13.9 0.6 dynamic_slice.3
  15.1 0.5 iota_add_fusion.1.refs_7_
  15.7 0.0 copy-done.17
  15.7 0.6 fusion.8
  16.3 0.0 copy-done.16
  16.3 0.6 fusion.7
  16.9 24.3 %shard_map.91 = bf16[32,32,512]{2,1,0:T(8,128)(2,1)} custom-call(bf16[32,512]{1,0:T(8,128)(2,1)} %get-tuple-element.86.refs_0_), custom_call_target="tpu_custom_call" | custom-call | tf_op jit(solution)/shard_map/pallas_call | solution.py:62
  41.3 0.1 iota_add_fusion
  41.4 1.3 add.80.refs_6_
  42.7 0.0 copy-done.19
  42.7 0.7 fusion.10
  43.4 1.3 compare_select_fusion.1.refs_3_
  44.7 50.8 %shard_map.92 = (bf16[1024,512]{1,0:T(8,128)(2,1)}, f32[1024,4]{1,0:T(8,128)}, f32[1024,4]{1,0:T(8,128)}, bf16[32,32,512]{2,1,0:T(8,128)(2,1)}) custom-call(bf16[1024,512]{1,0:T(8,128)(2,1)} %bitcast.58, bf16[3072,128]{1,0:T(8,128)(2,1)} %bitcast.65, bf16[3072,128]{1,0:T(8,128)(2,1)} %bitcast.67, f32[1,3072]{1,0:T(1,128)} %compare_select_fusion.1.refs_3_, ...), custom_call_target="tpu_custom_call" | custom-call | flops 6509559808 | bytes 3670016 | tf_op jit(solution)/shard_map/pallas_call | solution.py:344
  95.5 52.1 %shard_map.93 = (bf16[1024,512]{1,0:T(8,128)(2,1)}, f32[1024,4]{1,0:T(8,128)}, f32[1024,4]{1,0:T(8,128)}, bf16[32,32,512]{2,1,0:T(8,128)(2,1)}, bf16[32,32,512]{...) custom-call(bf16[1024,512]{1,0:T(8,128)(2,1)} %bitcast.76, bf16[3072,128]{1,0:T(8,128)(2,1)} %bitcast.66, ...), custom_call_target="tpu_custom_call" | custom-call | flops 6509559808 | bytes 3670016 | tf_op jit(solution)/shard_map/pallas_call | solution.py:344
  147.6 1.2 reduce_max.36
  148.7 1.3 multiply_reduce_fusion.3
  150.1 0.0 copy-done.1
  150.1 3.0 shard_map.94.refs_12_
  153.1 0.6 copy-done.6
  153.7 1.3 compare_select_fusion.refs_3_
  155.0 65.4 %shard_map.95 = (bf16[1024,512]{1,0:T(8,128)(2,1)}, f32[1024,4]{1,0:T(8,128)}, f32[1024,4]{1,0:T(8,128)}, bf16[32,32,512]{2,1,0:T(8,128)(2,1)}, bf16[32,32,512]{...) custom-call(bf16[1024,512]{1,0:T(8,128)(2,1)} %bitcast.72, ...), custom_call_target="tpu_custom_call" | custom-call | flops 6509559808 | bytes 3670016 | tf_op jit(solution)/shard_map/pallas_call | solution.py:344
  220.4 1.2 reduce_max.37
  221.6 1.3 multiply_reduce_fusion.2
  222.9 3.0 shard_map.96.refs_11_
  225.9 0.0 copy-start.7
  225.9 0.6 copy-done.7
  226.5 51.4 %shard_map.97 = (bf16[1024,512]{1,0:T(8,128)(2,1)}, f32[1024,4]{1,0:T(8,128)}, f32[1024,4]{1,0:T(8,128)}, bf16[32,32,512]{2,1,0:T(8,128)(2,1)}, f32[32,32,4]{2,1...) custom-call(bf16[1024,512]{1,0:T(8,128)(2,1)} %bitcast.74, bf16[3072,128]{1,0:T(8,128)(2,1)} %bitcast.64, ...), custom_call_target="tpu_custom_call" | custom-call | flops 6509559808 | bytes 3670016 | tf_op jit(solution)/shard_map/pallas_call | solution.py:344
  277.9 33.2 %shard_map.99 = (bf16[32,32,512]{2,1,0:T(8,128)(2,1)}, f32[32,32,4]{2,1,0:T(8,128)}, f32[32,32,4]{2,1,0:T(8,128)}) custom-call(bf16[32,32,512]{2,1,0:T(8,128)(2,1)} %bitcast.57, f32[32,32,4]{2,1,0:T(8,128)} %bitcast.69, f32[32,32,4]{2,1,0:T(8,128)} %bitcast.70), custom_call_target="tpu_custom_call" | custom-call | tf_op jit(solution)/shard_map/pallas_call | solution.py:62
  311.2 1.2 reduce_max.39
  312.4 1.3 multiply_reduce_fusion
  313.8 0.0 copy-done.3
  313.8 3.0 shard_map.100.refs_1_
  316.8 0.0 copy-start.4
  316.8 0.6 copy-done.4
  317.4 0.1 reduce_max.38
  317.4 0.1 multiply_reduce_fusion.1
  317.6 3.2 shard_map.98.refs_0_
  320.8 0.0 copy-start.5
  320.8 0.6 copy-done.5
  321.4 27.8 %shard_map.101 = (bf16[32,32,512]{2,1,0:T(8,128)(2,1)}, bf16[32,32,512]{2,1,0:T(8,128)(2,1)}) custom-call(bf16[32,512]{1,0:T(8,128)(2,1)} %copy-done.5, bf16[32,512]{1,0:T(8,128)(2,1)} %copy-done.4), custom_call_target="tpu_custom_call" | custom-call | tf_op jit(solution)/shard_map/pallas_call | solution.py:62
  349.2 0.0 copy-done.11
  349.2 1.4 fusion.3
  350.6 0.0 copy-start.14
  350.6 1.8 convolution_add_fusion.2
  352.5 0.1 copy-done.14
  352.6 0.4 convolution_add_fusion.1
  353.0 0.8 copy-done.12
  353.8 1.4 convolution_add_fusion
  355.2 22.1 %shard_map.102 = f32[4,256,256]{2,1,0:T(8,128)} custom-call(f32[4,256,256]{2,1,0:T(8,128)} %bitcast.50), custom_call_target="tpu_custom_call" | custom-call | tf_op jit(solution)/shard_map/pallas_call | solution.py:62
  377.3 2.0 reduce_sum.49
  (23 shorter events, 0.1 us)
Async XLA Ops:
  7.3 3.1 copy-start.8
  8.9 1.6 copy-start.9
  10.4 3.5 copy-start.20
  10.4 5.2 %copy-start.17 = (bf16[32,256]{1,0:T(8,128)(2,1)S(1)}, bf16[32,256]{1,0:T(8,128)(2,1)}, u32[]{:S(2)}) copy-start(bf16[32,256]{1,0:T(8,128)(2,1)} %param.13) | copy-start | bytes 49156
  10.4 5.2 %copy-start.18 = (bf16[32,256]{1,0:T(8,128)(2,1)S(1)}, bf16[32,256]{1,0:T(8,128)(2,1)}, u32[]{:S(2)}) copy-start(bf16[32,256]{1,0:T(8,128)(2,1)} %param.12) | copy-start | bytes 49156
  10.5 5.9 %copy-start.16 = (bf16[32,2048]{1,0:T(8,128)(2,1)S(1)}, bf16[32,2048]{1,0:T(8,128)(2,1)}, u32[]{:S(2)}) copy-start(bf16[32,2048]{1,0:T(8,128)(2,1)} %param.11) | copy-start | bytes 393220
  10.5 32.3 %copy-start.19 = (s32[1,2]{1,0:T(1,128)S(1)}, s32[1,2]{1,0:T(1,128)}, u32[]{:S(2)}) copy-start(s32[1,2]{1,0:T(1,128)} %param.17) | copy-start | bytes 28
  147.6 2.5 copy-start.1
  153.1 0.6 copy-start.6
  220.4 2.5 copy-start.2
  225.9 0.6 copy-start.7
  311.2 2.6 copy-start.3
  311.2 6.2 %copy-start.10 = (f32[32,32,4]{2,1,0:T(8,128)S(1)}, f32[32,32,4]{2,1,0:T(8,128)}, u32[]{:S(2)}) copy-start(f32[32,32,4]{2,1,0:T(8,128)} %get-tuple-element.58) | copy-start | bytes 49156
  311.2 6.3 %copy-start.15 = (f32[32,32,4]{2,1,0:T(8,128)S(1)}, f32[32,32,4]{2,1,0:T(8,128)}, u32[]{:S(2)}) copy-start(f32[32,32,4]{2,1,0:T(8,128)} %get-tuple-element.59) | copy-start | bytes 49156
  313.8 3.8 %copy-start = (bf16[32,32,512]{2,1,0:T(8,128)(2,1)S(1)}, bf16[32,32,512]{2,1,0:T(8,128)(2,1)}, u32[]{:S(2)}) copy-start(bf16[32,32,512]{2,1,0:T(8,128)(2,1)} %get-tuple-element.57) | copy-start | bytes 3145732
  316.8 0.6 copy-start.4
  317.4 31.8 %copy-start.11 = (bf16[32,32,512]{2,1,0:T(8,128)(2,1)S(1)}, bf16[32,32,512]{2,1,0:T(8,128)(2,1)}, u32[]{:S(2)}) copy-start(bf16[32,32,512]{2,1,0:T(8,128)(2,1)} %get-tuple-element.48) | copy-start | bytes 3145732
  320.8 0.6 copy-start.5
  350.6 1.9 copy-start.13
  350.6 1.9 copy-start.14
  352.6 1.2 copy-start.12

commit v15 on v13

--- a/solution.py
+++ b/solution.py
@@ -478,8 +478,8 @@
         if previous is not None:
             sends.extend(previous)
             flags.extend([True, True, True])
-        if i >= 2:
-            sends.append(attn_pieces[i - 2])
+        if i >= 3:
+            sends.append(attn_pieces[i - 3])
             flags.append(False)
         outs = attention_with_push(
             q_blocks.reshape(total_rows, width),
@@ -498,7 +498,7 @@
         if previous is not None:
             got = (rest.pop(0), rest.pop(0), rest.pop(0))
             attn_pieces.append(combine_piece(got))
-        if i >= 2:
+        if i >= 3:
             attn_blocks.append(rest.pop(0))
         previous = (
             sums_i.reshape(ctx_count, q_dev, width),
@@ -506,9 +506,13 @@
             totals_i.reshape(ctx_count, q_dev, piece_heads),
         )
     last_parts = push(
-        previous + (attn_pieces[pieces - 2],), "ctx", ctx_count, (True, True, True, False), 1
-    )
-    attn_blocks.append(last_parts[3])
+        previous + tuple(attn_pieces[pieces - 3 :]),
+        "ctx",
+        ctx_count,
+        (True, True, True, False, False),
+        1,
+    )
+    attn_blocks.extend(last_parts[3:])
     attn_pieces.append(combine_piece(last_parts[:3]))
     attn_blocks.extend(push((attn_pieces[pieces - 1],), "ctx", ctx_count, False, 2))
     projected = None

time: 375 us -> 376 us (level)
  matrix products: 2.71 us -> 7.84 us
  other arithmetic: 19.3 us -> 14.7 us
    pallas_call x4, Pallas kernels: 103 us -> 120 us  [push(): pl.pallas_call(functools.partial(push_kernel, axis, n, per_dest, count),...]
    pallas_call x4, Pallas kernels: 208 us -> 194 us  [attention_with_push(): pl.pallas_call(functools.partial(attn_push_kernel, n, group_size, per_des...]
    dot_general x4, matrix products: 2.71 us -> 7.84 us  [body(): jnp.dot(blocks.reshape(total_rows, width), out_weight[j * width:(j + 1) *...]
where the time goes in v15:
time: 376 us; the launch traced here: 373 us
  Pallas kernels  326 us (87%)
  local copies, waits for them, and re-layouts  23.5 us (6%)
  other arithmetic  14.7 us (4%)
  matrix products  7.84 us (2%)
    pallas_call x4, Pallas kernels, attention_with_push(): pl.pallas_call(functools.partial(attn_push_kernel, n, group_size, per_des...  194 us
    pallas_call x4, Pallas kernels, push(): pl.pallas_call(functools.partial(push_kernel, axis, n, per_dest, count),...  120 us
    pallas_call x4, Pallas kernels, combine(): pl.pallas_call(functools.partial(combine_kernel, heads), out_shape=jax.Sh...  11.9 us
    dot_general x4, matrix products, body(): jnp.dot(blocks.reshape(total_rows, width), out_weight[j * width:(j + 1) *...  7.84 us

profile of v15, /device:TPU:125, one launch (start us, length us, event | category | flops | bytes accessed | tf_op | source)
XLA Modules:
  0.0 373.4 jit_solution(12356821037960600182)
XLA Ops:
  0.0 1.2 dynamic_slice.3
  1.9 0.5 iota_add_fusion.1.refs_7_
  2.4 0.7 broadcast_multiply_fusion
  3.1 1.3 fusion.10
  4.4 0.8 compare_and_fusion
  5.2 1.3 compare_select_fusion.refs_3_
  6.4 1.2 compare_select_fusion.1.refs_3_
  7.6 0.1 iota_add_fusion
  7.7 0.7 fusion.9
  8.4 1.3 fusion.8
  9.7 0.7 copy.23
  10.4 0.7 copy.22
  11.1 1.5 fusion.7
  12.6 1.3 add.80.refs_6_
  13.9 20.5 %shard_map.91 = bf16[32,32,512]{2,1,0:T(8,128)(2,1)} custom-call(bf16[32,512]{1,0:T(8,128)(2,1)} %get-tuple-element.84.refs_0_), custom_call_target="tpu_custom_call" | custom-call | tf_op jit(solution)/shard_map/pallas_call | solution.py:64
  34.4 1.7 fusion.6
  36.0 0.7 gather_fusion.2
  36.8 1.6 gather_fusion
  38.3 1.7 fusion.5
  40.0 1.6 gather_fusion.3
  41.6 1.6 gather_fusion.1
  43.1 0.0 copy-done.8
  43.1 0.0 copy-done.9
  43.1 2.9 broadcast_select_fusion
  46.1 2.3 copy.21
  48.4 1.2 copy.20
  49.6 44.5 %shard_map.92 = (bf16[1024,512]{1,0:T(8,128)(2,1)}, f32[1024,4]{1,0:T(8,128)}, f32[1024,4]{1,0:T(8,128)}, bf16[32,32,512]{2,1,0:T(8,128)(2,1)}) custom-call(bf16[1024,512]{1,0:T(8,128)(2,1)} %bitcast.63, bf16[128,3072]{1,0:T(8,128)(2,1)} %bitcast.69, bf16[3072,128]{1,0:T(8,128)(2,1)} %bitcast.73, f32[1,3072]{1,0:T(1,128)} %compare_select_fusion.1.refs_3_, ...), custom_call_target="tpu_custom_call" | custom-call | flops 6509559808 | bytes 3670016 | tf_op jit(solution)/shard_map/pallas_call | solution.py:344
  94.1 50.5 %shard_map.93 = (bf16[1024,512]{1,0:T(8,128)(2,1)}, f32[1024,4]{1,0:T(8,128)}, f32[1024,4]{1,0:T(8,128)}, bf16[32,32,512]{2,1,0:T(8,128)(2,1)}, bf16[32,32,512]{...) custom-call(bf16[1024,512]{1,0:T(8,128)(2,1)} %bitcast.86, bf16[128,3072]{1,0:T(8,128)(2,1)} %bitcast.70, ...), custom_call_target="tpu_custom_call" | custom-call | flops 6509559808 | bytes 3670016 | tf_op jit(solution)/shard_map/pallas_call | solution.py:344
  144.7 0.0 copy-start.2
  144.7 1.2 reduce_max.36
  145.9 1.3 multiply_reduce_fusion.3
  147.2 0.0 copy-done.2
  147.2 3.0 shard_map.95.refs_11_
  150.2 0.0 copy-start.7
  150.2 0.6 copy-done.7
  150.8 48.8 %shard_map.94 = (bf16[1024,512]{1,0:T(8,128)(2,1)}, f32[1024,4]{1,0:T(8,128)}, f32[1024,4]{1,0:T(8,128)}, bf16[32,32,512]{2,1,0:T(8,128)(2,1)}, bf16[32,32,512]{...) custom-call(bf16[1024,512]{1,0:T(8,128)(2,1)} %bitcast.82, bf16[128,3072]{1,0:T(8,128)(2,1)} %bitcast.67, ...), custom_call_target="tpu_custom_call" | custom-call | flops 6509559808 | bytes 3670016 | tf_op jit(solution)/shard_map/pallas_call | solution.py:344
  199.7 50.2 %shard_map.96 = (bf16[1024,512]{1,0:T(8,128)(2,1)}, f32[1024,4]{1,0:T(8,128)}, f32[1024,4]{1,0:T(8,128)}, bf16[32,32,512]{2,1,0:T(8,128)(2,1)}, f32[32,32,4]{2,1...) custom-call(bf16[1024,512]{1,0:T(8,128)(2,1)} %bitcast.84, bf16[128,3072]{1,0:T(8,128)(2,1)} %bitcast.68, ...), custom_call_target="tpu_custom_call" | custom-call | flops 6509559808 | bytes 3670016 | tf_op jit(solution)/shard_map/pallas_call | solution.py:344
  249.9 0.0 copy-start.10
  249.9 0.0 copy-start.13
  249.9 0.0 copy-start.1
  249.9 1.8 fusion.3
  251.8 0.1 reduce_max.38
  251.9 0.1 multiply_reduce_fusion.1
  252.0 3.0 shard_map.98.refs_4_
  255.0 0.0 copy-start.4
  255.0 0.6 copy-done.4
  255.6 1.1 reduce_max.37
  256.7 1.3 multiply_reduce_fusion.2
  258.1 3.0 shard_map.97.refs_3_
  261.1 0.0 copy-start.5
  261.1 0.6 copy-done.5
  261.7 55.2 %shard_map.99 = (bf16[32,32,512]{2,1,0:T(8,128)(2,1)}, f32[32,32,4]{2,1,0:T(8,128)}, f32[32,32,4]{2,1,0:T(8,128)}, bf16[32,32,512]{2,1,0:T(8,128)(2,1)}, bf16[32,32,512]{2,1,0:T(8,128)(2,1)}) custom-call(bf16[32,32,512]{2,1,0:T(8,128)(2,1)} %bitcast.62, f32[32,32,4]{2,1,0:T(8,128)} %bitcast.75, f32[32,32,4]{2,1,0:T(8,128)} %bitcast.76, ...), custom_call_target="tpu_custom_call" | custom-call | tf_op jit(solution)/shard_map/pallas_call | solution.py:64
  316.9 0.0 copy-start.12
  316.9 1.8 convolution_add_fusion.2
  318.7 1.5 convolution_add_fusion.1
  320.3 0.1 reduce_max.39
  320.4 0.1 multiply_reduce_fusion
  320.5 3.0 shard_map.100.refs_0_
  323.5 0.0 copy-start.6
  323.5 0.6 copy-done.6
  324.1 26.8 %shard_map.101 = bf16[32,32,512]{2,1,0:T(8,128)(2,1)} custom-call(bf16[32,512]{1,0:T(8,128)(2,1)} %copy-done.6), custom_call_target="tpu_custom_call" | custom-call | tf_op jit(solution)/shard_map/pallas_call | solution.py:64
  350.9 2.7 convolution_add_fusion
  353.6 17.8 %shard_map.102 = f32[4,256,256]{2,1,0:T(8,128)} custom-call(f32[4,256,256]{2,1,0:T(8,128)} %bitcast.55), custom_call_target="tpu_custom_call" | custom-call | tf_op jit(solution)/shard_map/pallas_call | solution.py:64
  371.4 2.0 reduce_sum.49
  (16 shorter events, 0.0 us)
Async XLA Ops:
  41.6 1.6 copy-start.8
  41.6 1.6 copy-start.9
  144.7 2.5 copy-start.2
  150.2 0.6 copy-start.7
  249.9 1.9 copy-start.10
  249.9 1.9 copy-start.13
  249.9 2.1 copy-start.1
  252.0 6.1 %copy-start = (bf16[32,32,512]{2,1,0:T(8,128)(2,1)S(1)}, bf16[32,32,512]{2,1,0:T(8,128)(2,1)}, u32[]{:S(2)}) copy-start(bf16[32,32,512]{2,1,0:T(8,128)(2,1)} %get-tuple-element.55) | copy-start | bytes 3145732
  255.0 0.6 copy-start.4
  261.1 0.6 copy-start.5
  316.9 1.8 copy-start.12
  318.7 1.6 copy-start.11
  318.7 1.6 copy-start.14
  318.7 1.8 copy-start.3
  323.5 0.6 copy-start.6

commit v16 on v11

--- a/solution.py
+++ b/solution.py
@@ -324,7 +324,7 @@
     rows, width = query_rows.shape
     group_size = width // DH
     total_keys = keys_t.shape[1]
-    step_keys = TPB * TILE
+    step_keys = total_keys
     steps = total_keys // step_keys
     q_new = new_values.shape[0]
     any_spec = pl.BlockSpec(memory_space=pl.ANY)

time: 373 us -> 374 us (level)
  the two profiles are of different devices: /device:TPU:125 before, /device:TPU:1 now
where the time goes in v16:
time: 374 us; the launch traced here: 370 us
  Pallas kernels  325 us (87%)
  local copies, waits for them, and re-layouts  21.8 us (6%)
  other arithmetic  16.9 us (5%)
  matrix products  4.75 us (1%)
    pallas_call x4, Pallas kernels, attention_with_push(): pl.pallas_call(functools.partial(attn_push_kernel, n, group_size, per_des...  202 us
    pallas_call x4, Pallas kernels, push(): pl.pallas_call(functools.partial(push_kernel, axis, n, per_dest, count),...  110 us
    pallas_call x4, Pallas kernels, combine(): pl.pallas_call(functools.partial(combine_kernel, heads), out_shape=jax.Sh...  12.2 us

profile of v16, /device:TPU:1, one launch (start us, length us, event | category | flops | bytes accessed | tf_op | source)
XLA Modules:
  0.0 369.7 jit_solution(14098657299835307668)
XLA Ops:
  0.0 0.8 compare_and_fusion
  0.8 1.7 fusion.6
  2.5 1.6 gather_fusion
  4.0 1.7 fusion.5
  5.7 1.6 gather_fusion.1
  7.3 1.6 gather_fusion.2
  8.9 1.5 gather_fusion.3
  10.4 0.0 copy-done.8
  10.4 0.0 copy-done.9
  10.4 3.1 broadcast_select_fusion
  13.6 2.4 copy.20
  15.9 0.0 copy-done.21
  15.9 0.6 dynamic_slice.3
  17.2 0.5 iota_add_fusion.1.refs_7_
  17.7 0.0 copy-done.17
  17.7 0.6 fusion.7
  18.3 24.3 %shard_map.91 = bf16[32,32,512]{2,1,0:T(8,128)(2,1)} custom-call(bf16[32,512]{1,0:T(8,128)(2,1)} %get-tuple-element.86.refs_0_), custom_call_target="tpu_custom_call" | custom-call | tf_op jit(solution)/shard_map/pallas_call | solution.py:62
  42.7 0.1 iota_add_fusion
  42.8 1.4 add.80.refs_6_
  44.1 0.0 copy-done.18
  44.2 0.7 copy.22
  44.9 0.0 copy-done.19
  44.9 0.6 fusion.8
  45.5 0.7 fusion.10
  46.1 1.3 compare_select_fusion.1.refs_3_
  47.4 43.6 %shard_map.92 = (bf16[1024,512]{1,0:T(8,128)(2,1)}, f32[1024,4]{1,0:T(8,128)}, f32[1024,4]{1,0:T(8,128)}, bf16[32,32,512]{2,1,0:T(8,128)(2,1)}) custom-call(bf16[1024,512]{1,0:T(8,128)(2,1)} %bitcast.63, bf16[128,3072]{1,0:T(8,128)(2,1)} %bitcast.67, bf16[3072,128]{1,0:T(8,128)(2,1)} %bitcast.73, f32[1,3072]{1,0:T(1,128)} %compare_select_fusion.1.refs_3_, ...), custom_call_target="tpu_custom_call" | custom-call | flops 6509559808 | bytes 3670016 | tf_op jit(solution)/shard_map/pallas_call | solution.py:342
  91.0 47.6 %shard_map.93 = (bf16[1024,512]{1,0:T(8,128)(2,1)}, f32[1024,4]{1,0:T(8,128)}, f32[1024,4]{1,0:T(8,128)}, bf16[32,32,512]{2,1,0:T(8,128)(2,1)}, bf16[32,32,512]{...) custom-call(bf16[1024,512]{1,0:T(8,128)(2,1)} %bitcast.86, bf16[128,3072]{1,0:T(8,128)(2,1)} %bitcast.68, ...), custom_call_target="tpu_custom_call" | custom-call | flops 6509559808 | bytes 3670016 | tf_op jit(solution)/shard_map/pallas_call | solution.py:342
  138.6 1.2 reduce_max.36
  139.8 1.3 multiply_reduce_fusion.3
  141.1 3.0 shard_map.94.refs_12_
  144.1 0.0 copy-start.6
  144.1 0.6 copy-done.6
  144.7 1.2 copy.21
  145.9 0.7 copy.23
  146.6 1.3 compare_select_fusion.refs_3_
  147.9 66.4 %shard_map.95 = (bf16[1024,512]{1,0:T(8,128)(2,1)}, f32[1024,4]{1,0:T(8,128)}, f32[1024,4]{1,0:T(8,128)}, bf16[32,32,512]{2,1,0:T(8,128)(2,1)}, bf16[32,32,512]{...) custom-call(bf16[1024,512]{1,0:T(8,128)(2,1)} %bitcast.82, ...), custom_call_target="tpu_custom_call" | custom-call | flops 6509559808 | bytes 3670016 | tf_op jit(solution)/shard_map/pallas_call | solution.py:342
  214.3 1.2 reduce_max.37
  215.5 1.3 multiply_reduce_fusion.2
  216.8 0.0 copy-done.2
  216.8 3.0 shard_map.96.refs_11_
  219.8 0.0 copy-start.7
  219.8 0.6 copy-done.7
  220.4 44.9 %shard_map.97 = (bf16[1024,512]{1,0:T(8,128)(2,1)}, f32[1024,4]{1,0:T(8,128)}, f32[1024,4]{1,0:T(8,128)}, bf16[32,32,512]{2,1,0:T(8,128)(2,1)}, f32[32,32,4]{2,1...) custom-call(bf16[1024,512]{1,0:T(8,128)(2,1)} %bitcast.84, bf16[128,3072]{1,0:T(8,128)(2,1)} %bitcast.70, ...), custom_call_target="tpu_custom_call" | custom-call | flops 6509559808 | bytes 3670016 | tf_op jit(solution)/shard_map/pallas_call | solution.py:342
  265.3 36.2 %shard_map.99 = (bf16[32,32,512]{2,1,0:T(8,128)(2,1)}, f32[32,32,4]{2,1,0:T(8,128)}, f32[32,32,4]{2,1,0:T(8,128)}) custom-call(bf16[32,32,512]{2,1,0:T(8,128)(2,1)} %bitcast.64, f32[32,32,4]{2,1,0:T(8,128)} %bitcast.75, f32[32,32,4]{2,1,0:T(8,128)} %bitcast.76), custom_call_target="tpu_custom_call" | custom-call | tf_op jit(solution)/shard_map/pallas_call | solution.py:62
  301.5 1.2 reduce_max.39
  302.8 1.3 multiply_reduce_fusion
  304.1 3.0 shard_map.100.refs_1_
  307.1 0.6 copy-done.4
  307.7 0.1 reduce_max.38
  307.8 0.0 copy-done.16
  307.8 0.1 multiply_reduce_fusion.1
  308.0 3.2 shard_map.98.refs_0_
  311.2 0.0 copy-start.5
  311.2 0.6 copy-done.5
  311.8 33.5 %shard_map.101 = (bf16[32,32,512]{2,1,0:T(8,128)(2,1)}, bf16[32,32,512]{2,1,0:T(8,128)(2,1)}) custom-call(bf16[32,512]{1,0:T(8,128)(2,1)} %copy-done.5, bf16[32,512]{1,0:T(8,128)(2,1)} %copy-done.4), custom_call_target="tpu_custom_call" | custom-call | tf_op jit(solution)/shard_map/pallas_call | solution.py:62
  345.3 1.4 fusion.3
  346.7 0.0 copy-start.15
  346.7 1.5 convolution_add_fusion.2
  348.2 0.1 copy-done.15
  348.3 0.4 convolution_add_fusion.1
  348.7 0.8 copy-done.13
  349.5 1.4 convolution_add_fusion
  350.9 16.5 %shard_map.102 = f32[4,256,256]{2,1,0:T(8,128)} custom-call(f32[4,256,256]{2,1,0:T(8,128)} %bitcast.54), custom_call_target="tpu_custom_call" | custom-call | tf_op jit(solution)/shard_map/pallas_call | solution.py:62
  367.4 2.0 reduce_sum.49
  (30 shorter events, 0.1 us)
Async XLA Ops:
  7.3 3.1 copy-start.8
  8.9 1.6 copy-start.9
  10.4 5.5 %copy-start.21 = (s32[32]{0:T(128)S(1)}, s32[32]{0:T(128)}, u32[]{:S(2)}) copy-start(s32[32]{0:T(128)} %param.18) | copy-start | bytes 388
  10.4 7.3 %copy-start.17 = (bf16[32,2048]{1,0:T(8,128)(2,1)S(1)}, bf16[32,2048]{1,0:T(8,128)(2,1)}, u32[]{:S(2)}) copy-start(bf16[32,2048]{1,0:T(8,128)(2,1)} %param.11) | copy-start | bytes 393220
  13.5 30.6 %copy-start.18 = (bf16[32,256]{1,0:T(8,128)(2,1)S(1)}, bf16[32,256]{1,0:T(8,128)(2,1)}, u32[]{:S(2)}) copy-start(bf16[32,256]{1,0:T(8,128)(2,1)} %param.12) | copy-start | bytes 49156
  13.6 31.3 %copy-start.19 = (bf16[32,256]{1,0:T(8,128)(2,1)S(1)}, bf16[32,256]{1,0:T(8,128)(2,1)}, u32[]{:S(2)}) copy-start(bf16[32,256]{1,0:T(8,128)(2,1)} %param.13) | copy-start | bytes 49156
  13.6 31.9 %copy-start.20 = (s32[1,2]{1,0:T(1,128)S(1)}, s32[1,2]{1,0:T(1,128)}, u32[]{:S(2)}) copy-start(s32[1,2]{1,0:T(1,128)} %param.17) | copy-start | bytes 28
  138.6 2.5 copy-start.1
  144.1 0.6 copy-start.6
  214.3 2.5 copy-start.2
  219.8 0.6 copy-start.7
  301.5 2.6 copy-start.3
  301.5 6.2 %copy-start.10 = (f32[32,32,4]{2,1,0:T(8,128)S(1)}, f32[32,32,4]{2,1,0:T(8,128)}, u32[]{:S(2)}) copy-start(f32[32,32,4]{2,1,0:T(8,128)} %get-tuple-element.58) | copy-start | bytes 49156
  301.5 6.3 %copy-start.16 = (f32[32,32,4]{2,1,0:T(8,128)S(1)}, f32[32,32,4]{2,1,0:T(8,128)}, u32[]{:S(2)}) copy-start(f32[32,32,4]{2,1,0:T(8,128)} %get-tuple-element.59) | copy-start | bytes 49156
  304.1 3.8 %copy-start = (bf16[32,32,512]{2,1,0:T(8,128)(2,1)S(1)}, bf16[32,32,512]{2,1,0:T(8,128)(2,1)}, u32[]{:S(2)}) copy-start(bf16[32,32,512]{2,1,0:T(8,128)(2,1)} %get-tuple-element.57) | copy-start | bytes 3145732
  307.1 0.6 copy-start.4
  307.7 37.5 %copy-start.11 = (bf16[32,32,512]{2,1,0:T(8,128)(2,1)S(1)}, bf16[32,32,512]{2,1,0:T(8,128)(2,1)}, u32[]{:S(2)}) copy-start(bf16[32,32,512]{2,1,0:T(8,128)(2,1)} %get-tuple-element.48) | copy-start | bytes 3145732
  307.9 38.7 %copy-start.12 = (bf16[32,32,512]{2,1,0:T(8,128)(2,1)S(1)}, bf16[32,32,512]{2,1,0:T(8,128)(2,1)}, u32[]{:S(2)}) copy-start(bf16[32,32,512]{2,1,0:T(8,128)(2,1)} %get-tuple-element.56) | copy-start | bytes 3145732
  311.2 0.6 copy-start.5
  346.7 1.6 copy-start.14
  346.7 1.6 copy-start.15
  348.3 1.2 copy-start.13

commit v17 on v11

--- a/solution.py
+++ b/solution.py
@@ -414,6 +414,40 @@
     )(part_sum, factor, denominator)
 
 
+def combine_fused_kernel(heads, part_ref, max_ref, tot_ref, out_ref):
+    senders = part_ref.shape[0]
+    coef = DH ** (-0.5) * LOG2E
+    top = lax.fori_loop(1, senders, lambda i, m: jnp.maximum(m, max_ref[i]), max_ref[0])
+
+    def sender_body(i, carry):
+        acc, den = carry
+        fac = jnp.exp2((max_ref[i] - top) * coef)
+        blk = part_ref[i].astype(jnp.float32)
+        acc = tuple(
+            acc[h] + blk[:, h * DH : (h + 1) * DH] * fac[:, h : h + 1] for h in range(heads)
+        )
+        return acc, den + tot_ref[i] * fac
+
+    rows = out_ref.shape[0]
+    start = tuple(jnp.zeros((rows, DH), jnp.float32) for _ in range(heads))
+    acc, den = lax.fori_loop(0, senders, sender_body, (start, jnp.zeros_like(top)))
+    for h in range(heads):
+        out_ref[:, h * DH : (h + 1) * DH] = (acc[h] / den[:, h : h + 1]).astype(out_ref.dtype)
+
+
+def combine_fused(part_sum, part_max, part_total):
+    senders, rows, width = part_sum.shape
+    heads = width // DH
+    vmem = pl.BlockSpec(memory_space=pltpu.VMEM)
+    return pl.pallas_call(
+        functools.partial(combine_fused_kernel, heads),
+        out_shape=jax.ShapeDtypeStruct((rows, width), jnp.bfloat16),
+        in_specs=[vmem, vmem, vmem],
+        out_specs=vmem,
+        compiler_params=pltpu.CompilerParams(vmem_limit_bytes=32 * 1024 * 1024),
+    )(part_sum, part_max, part_total)
+
+
 def body(
     queries,
     new_keys,
@@ -459,10 +493,7 @@
 
     def combine_piece(parts):
         part_sum, part_max, part_total = parts
-        top_max = jnp.max(part_max, axis=0)
-        factor = jnp.exp2((part_max - top_max[None]) * coef)
-        denominator = jnp.sum(part_total * factor, axis=0)
-        return combine(part_sum[:, None], factor, denominator)
+        return combine_fused(part_sum, part_max, part_total)
 
     attn_pieces = []
     attn_blocks = []

time: 373 us -> 375 us (level)
  local copies, waits for them, and re-layouts: 21.8 us -> 31.1 us
  other arithmetic: 16.9 us -> 9.06 us
    unnamed x46 -> x56, local copies, waits for them, and re-layouts: 4.73 us -> 15.4 us
    reduce_sum x4 -> x0, other arithmetic: 4.14 us -> none  [combine_piece(): denominator = jnp.sum(part_total * factor, axis=0)]
where the time goes in v17:
time: 375 us; the launch traced here: 369 us
  Pallas kernels  324 us (86%)
  local copies, waits for them, and re-layouts  31.1 us (8%)
  other arithmetic  9.06 us (2%)
    pallas_call x4, Pallas kernels, attention_with_push(): pl.pallas_call(functools.partial(attn_push_kernel, n, group_size, per_des...  208 us
    pallas_call x4, Pallas kernels, push(): pl.pallas_call(functools.partial(push_kernel, axis, n, per_dest, count),...  103 us
    unnamed x56, local copies, waits for them, and re-layouts  15.4 us
    pallas_call x4, Pallas kernels, combine_fused(): pl.pallas_call(functools.partial(combine_fused_kernel, heads), out_shape=...  13.5 us

profile of v17, /device:TPU:125, one launch (start us, length us, event | category | flops | bytes accessed | tf_op | source)
XLA Modules:
  0.0 369.0 jit_solution(14819286062784740180)
XLA Ops:
  0.0 0.8 compare_and_fusion
  0.8 1.7 fusion.6
  2.5 1.6 gather_fusion
  4.0 1.7 fusion.5
  5.7 1.6 gather_fusion.1
  7.3 1.6 gather_fusion.2
  8.8 1.6 gather_fusion.3
  10.4 0.0 copy-done.16
  10.4 3.1 broadcast_select_fusion
  13.6 1.2 copy.20
  14.7 0.0 copy-done.26
  14.7 0.6 dynamic_slice.3
  16.0 0.6 iota_add_fusion.1.refs_7_
  16.6 0.0 copy-done.22
  16.6 0.6 fusion.7
  17.2 20.4 %shard_map.91 = bf16[32,32,512]{2,1,0:T(8,128)(2,1)} custom-call(bf16[32,512]{1,0:T(8,128)(2,1)} %get-tuple-element.78.refs_0_), custom_call_target="tpu_custom_call" | custom-call | tf_op jit(solution)/shard_map/pallas_call | solution.py:62
  37.7 0.1 iota_add_fusion
  37.7 1.3 add.80.refs_6_
  39.1 0.0 copy-done.23
  39.1 0.7 copy.22
  39.8 0.0 copy-done.24
  39.8 0.6 fusion.8
  40.4 0.0 copy-done.25
  40.4 0.6 fusion.10
  41.0 1.3 compare_select_fusion.1.refs_3_
  42.3 44.5 %shard_map.92 = (bf16[1024,512]{1,0:T(8,128)(2,1)}, f32[1024,4]{1,0:T(8,128)}, f32[1024,4]{1,0:T(8,128)}, bf16[32,32,512]{2,1,0:T(8,128)(2,1)}) custom-call(bf16[1024,512]{1,0:T(8,128)(2,1)} %bitcast.55, bf16[128,3072]{1,0:T(8,128)(2,1)} %bitcast.59, bf16[3072,128]{1,0:T(8,128)(2,1)} %bitcast.65, f32[1,3072]{1,0:T(1,128)} %compare_select_fusion.1.refs_3_, ...), custom_call_target="tpu_custom_call" | custom-call | flops 6509559808 | bytes 3670016 | tf_op jit(solution)/shard_map/pallas_call | solution.py:342
  86.8 50.5 %shard_map.93 = (bf16[1024,512]{1,0:T(8,128)(2,1)}, f32[1024,4]{1,0:T(8,128)}, f32[1024,4]{1,0:T(8,128)}, bf16[32,32,512]{2,1,0:T(8,128)(2,1)}, bf16[32,32,512]{...) custom-call(bf16[1024,512]{1,0:T(8,128)(2,1)} %bitcast.78, bf16[128,3072]{1,0:T(8,128)(2,1)} %bitcast.60, ...), custom_call_target="tpu_custom_call" | custom-call | flops 6509559808 | bytes 3670016 | tf_op jit(solution)/shard_map/pallas_call | solution.py:342
  137.3 0.0 copy-start.1
  137.3 1.2 copy-done.1
  138.5 1.0 copy-done.6
  139.6 1.0 copy-done.7
  140.6 3.4 shard_map.94.refs_12_
  144.0 0.0 copy-start.14
  144.0 0.6 copy-done.14
  144.6 1.2 copy.21
  145.8 0.7 copy.23
  146.5 1.2 compare_select_fusion.refs_3_
  147.7 57.6 %shard_map.95 = (bf16[1024,512]{1,0:T(8,128)(2,1)}, f32[1024,4]{1,0:T(8,128)}, f32[1024,4]{1,0:T(8,128)}, bf16[32,32,512]{2,1,0:T(8,128)(2,1)}, bf16[32,32,512]{...) custom-call(bf16[1024,512]{1,0:T(8,128)(2,1)} %bitcast.74, ...), custom_call_target="tpu_custom_call" | custom-call | flops 6509559808 | bytes 3670016 | tf_op jit(solution)/shard_map/pallas_call | solution.py:342
  205.3 1.2 copy-done.2
  206.5 1.0 copy-done.8
  207.5 1.0 copy-done.9
  208.6 3.4 shard_map.96.refs_11_
  212.0 0.0 copy-start.15
  212.0 0.6 copy-done.15
  212.6 55.4 %shard_map.97 = (bf16[1024,512]{1,0:T(8,128)(2,1)}, f32[1024,4]{1,0:T(8,128)}, f32[1024,4]{1,0:T(8,128)}, bf16[32,32,512]{2,1,0:T(8,128)(2,1)}, f32[32,32,4]{2,1...) custom-call(bf16[1024,512]{1,0:T(8,128)(2,1)} %bitcast.76, bf16[128,3072]{1,0:T(8,128)(2,1)} %bitcast.62, ...), custom_call_target="tpu_custom_call" | custom-call | flops 6509559808 | bytes 3670016 | tf_op jit(solution)/shard_map/pallas_call | solution.py:342
  268.0 33.0 %shard_map.99 = (bf16[32,32,512]{2,1,0:T(8,128)(2,1)}, f32[32,32,4]{2,1,0:T(8,128)}, f32[32,32,4]{2,1,0:T(8,128)}) custom-call(bf16[32,32,512]{2,1,0:T(8,128)(2,1)} %bitcast.56, f32[32,32,4]{2,1,0:T(8,128)} %bitcast.67, f32[32,32,4]{2,1,0:T(8,128)} %bitcast.68), custom_call_target="tpu_custom_call" | custom-call | tf_op jit(solution)/shard_map/pallas_call | solution.py:62
  301.0 1.2 copy-done.3
  302.3 1.0 copy-done.10
  303.3 1.0 copy-done.11
  304.3 3.4 shard_map.100.refs_1_
  307.7 0.6 copy-done.12
  308.4 3.4 shard_map.98.refs_0_
  311.8 0.0 copy-start.13
  311.8 0.6 copy-done.13
  312.4 30.4 %shard_map.101 = (bf16[32,32,512]{2,1,0:T(8,128)(2,1)}, bf16[32,32,512]{2,1,0:T(8,128)(2,1)}) custom-call(bf16[32,512]{1,0:T(8,128)(2,1)} %copy-done.13, bf16[32,512]{1,0:T(8,128)(2,1)} %copy-done.12), custom_call_target="tpu_custom_call" | custom-call | tf_op jit(solution)/shard_map/pallas_call | solution.py:62
  342.8 0.0 copy-done.17
  342.8 1.4 fusion.3
  344.2 0.4 convolution_add_fusion.2
  344.7 0.8 copy-done.20
  345.5 0.4 convolution_add_fusion.1
  345.9 0.8 copy-done.19
  346.7 1.4 convolution_add_fusion
  348.1 18.9 %shard_map.102 = f32[4,256,256]{2,1,0:T(8,128)} custom-call(f32[4,256,256]{2,1,0:T(8,128)} %bitcast.46), custom_call_target="tpu_custom_call" | custom-call | tf_op jit(solution)/shard_map/pallas_call | solution.py:62
  366.9 2.0 reduce_sum.9
  (32 shorter events, 0.1 us)
Async XLA Ops:
  7.3 3.1 copy-start.16
  10.4 4.3 %copy-start.26 = (s32[32]{0:T(128)S(1)}, s32[32]{0:T(128)}, u32[]{:S(2)}) copy-start(s32[32]{0:T(128)} %param.18) | copy-start | bytes 388
  10.4 6.2 %copy-start.22 = (bf16[32,2048]{1,0:T(8,128)(2,1)S(1)}, bf16[32,2048]{1,0:T(8,128)(2,1)}, u32[]{:S(2)}) copy-start(bf16[32,2048]{1,0:T(8,128)(2,1)} %param.11) | copy-start | bytes 393220
  13.6 25.5 %copy-start.23 = (bf16[32,256]{1,0:T(8,128)(2,1)S(1)}, bf16[32,256]{1,0:T(8,128)(2,1)}, u32[]{:S(2)}) copy-start(bf16[32,256]{1,0:T(8,128)(2,1)} %param.12) | copy-start | bytes 49156
  13.6 26.2 %copy-start.24 = (bf16[32,256]{1,0:T(8,128)(2,1)S(1)}, bf16[32,256]{1,0:T(8,128)(2,1)}, u32[]{:S(2)}) copy-start(bf16[32,256]{1,0:T(8,128)(2,1)} %param.13) | copy-start | bytes 49156
  13.6 26.8 %copy-start.25 = (s32[1,2]{1,0:T(1,128)S(1)}, s32[1,2]{1,0:T(1,128)}, u32[]{:S(2)}) copy-start(s32[1,2]{1,0:T(1,128)} %param.17) | copy-start | bytes 28
  137.3 1.2 copy-start.1
  138.5 1.0 copy-start.6
  139.6 1.0 copy-start.7
  144.0 0.6 copy-start.14
  205.3 1.2 copy-start.2
  206.5 1.0 copy-start.8
  207.5 1.0 copy-start.9
  212.0 0.6 copy-start.15
  268.0 40.4 %copy-start = (bf16[32,32,512]{2,1,0:T(8,128)(2,1)S(1)}, bf16[32,32,512]{2,1,0:T(8,128)(2,1)}, u32[]{:S(2)}) copy-start(bf16[32,32,512]{2,1,0:T(8,128)(2,1)} %get-tuple-element.57.part_ref) | copy-start | bytes 3145732
  268.0 40.4 %copy-start.4 = (f32[32,32,4]{2,1,0:T(8,128)S(1)}, f32[32,32,4]{2,1,0:T(8,128)}, u32[]{:S(2)}) copy-start(f32[32,32,4]{2,1,0:T(8,128)} %get-tuple-element.58.max_ref) | copy-start | bytes 49156
  268.0 40.4 %copy-start.5 = (f32[32,32,4]{2,1,0:T(8,128)S(1)}, f32[32,32,4]{2,1,0:T(8,128)}, u32[]{:S(2)}) copy-start(f32[32,32,4]{2,1,0:T(8,128)} %get-tuple-element.59.tot_ref) | copy-start | bytes 49156
  301.0 1.2 copy-start.3
  302.3 1.0 copy-start.10
  303.3 1.0 copy-start.11
  304.3 38.5 %copy-start.17 = (bf16[32,32,512]{2,1,0:T(8,128)(2,1)S(1)}, bf16[32,32,512]{2,1,0:T(8,128)(2,1)}, u32[]{:S(2)}) copy-start(bf16[32,32,512]{2,1,0:T(8,128)(2,1)} %get-tuple-element.48) | copy-start | bytes 3145732
  307.7 0.6 copy-start.12
  311.8 0.6 copy-start.13
  312.4 31.8 %copy-start.18 = (bf16[32,32,512]{2,1,0:T(8,128)(2,1)S(1)}, bf16[32,32,512]{2,1,0:T(8,128)(2,1)}, u32[]{:S(2)}) copy-start(bf16[32,32,512]{2,1,0:T(8,128)(2,1)} %get-tuple-element.56) | copy-start | bytes 3145732
  312.4 31.8 %copy-start.21 = (bf16[2048,256]{1,0:T(8,128)(2,1)S(1)}, bf16[2048,256]{1,0:T(8,128)(2,1)}, u32[]{:S(2)}) copy-start(bf16[2048,256]{1,0:T(8,128)(2,1)} %param.19) | copy-start | bytes 3145732
  344.2 1.2 copy-start.20
  345.4 1.2 copy-start.19
